TPU v7x, 512 devices: a whole 4x4x16 slice. The times are simulated.
512 devices in a mesh: req: 128 (over z_hi, y, x, core), tp: 4 (over z_lo).
Axes of the slice: x: 4, y: 4, z: 16 (z_hi: 4, z_lo: 4; z = z_hi * 4 + z_lo), core: 2. Of those that a mesh axis runs over, the one named last changes fastest.
Arguments:
- queries: bfloat16 [8192, 2560], P('req', 'tp'), may hold values from -20 to 20
- key_values: bfloat16 [8192, 1024], P('req', 'tp'), may hold values from -6 to 6
- hidden: bfloat16 [8192, 2560], P('req'), may hold values from -6 to 6
- lengths: int32 [128, 4], P('req'), may hold values from 1 to 32, 64 in all within a row
- page_table: int32 [128, 4, 2], P('req'), may hold values from 0 to 7, as said below
- out_weight: bfloat16 [2560, 2560], P('tp', 'req'), may hold values from -0.125 to 0.125
- norm_gain: float32 [2560], replicated, may hold values from 0.4 to 1.6
- expert_choice: int32 [8192, 6], P('req'), may hold values from 0 to 63, all different within a row; in each aligned block of 64 rows (0 to 63, 64 to 127, ...) at most 8 rows name the same one
- route_weight: float32 [8192, 6], P('req'), may hold values from 0.05 to 0.5
- gate_up: bfloat16 [128, 2560, 1536], P('req', None, 'tp'), may hold values from -0.125 to 0.125
- down: bfloat16 [128, 768, 2560], P('req', 'tp'), may hold values from -0.15625 to 0.15625
Outputs:
- layer_out: bfloat16 [8192, 2560], P('req', 'tp')
- kv_cache: bfloat16 [1024, 16, 1024], P('req', None, 'tp')
Inputs may be any that keep to these rules, and one draw needn't show every extreme that they name: `expert_choice`: among the 64 rows of one index of req no expert is named by more than 8 rows; the 6 experts of a row differ. `page_table`: the 4 x 2 entries of one index of req are its 8 pool pages, each once.
All inputs are finite; a program needn't handle non-finite values.
Results may differ from a plain program's by a relative error of at most 0.0065.
Values may be sent and summed in bfloat16 or wider, within the bound.
No kernel may reach another device: no remote copies, remote signals or barrier semaphores. Data moves between devices by JAX's collectives and lax.ppermute only.
A program may use at most 64 MiB of HBM per device.

v0:
```python
import jax
import jax.numpy as jnp
from jax import lax
from jax.sharding import PartitionSpec as P

HEAD_DIM = 128
PAGE = 16


epsilon = 1e-05


def prompt_layout(lengths, count):
    ends = jnp.cumsum(lengths)
    starts = ends - lengths
    places = jnp.arange(count, dtype=jnp.int32)
    segment = jnp.sum((ends[None, :] <= places[:, None]).astype(jnp.int32), axis=1)
    picked = segment[:, None] == jnp.arange(lengths.shape[0], dtype=jnp.int32)[None, :]
    offset = places - jnp.sum(jnp.where(picked, starts[None, :], 0), axis=1)
    return (segment, offset)


def attend(queries, key_values, segment):
    count = queries.shape[0]
    local_kv = key_values.shape[1] // (2 * HEAD_DIM)
    local_heads = queries.shape[1] // HEAD_DIM
    group = local_heads // local_kv
    query_rows = queries.reshape(count, local_kv, group, HEAD_DIM)
    key_rows = key_values.reshape(count, local_kv, 2, HEAD_DIM)
    scores = jnp.einsum(
        "qhgd,khd->hgqk", query_rows, key_rows[:, :, 0], preferred_element_type=jnp.float32
    ) * HEAD_DIM ** (-0.5)
    places = jnp.arange(count, dtype=jnp.int32)
    allowed = (segment[:, None] == segment[None, :]) & (places[None, :] <= places[:, None])
    scores = jnp.where(allowed[None, None], scores, -1e30)
    highest = jnp.max(scores, axis=-1, keepdims=True)
    weights = jnp.exp(scores - highest)
    probs = (weights / jnp.sum(weights, axis=-1, keepdims=True)).astype(jnp.bfloat16)
    context = jnp.einsum(
        "hgqk,khd->qhgd", probs, key_rows[:, :, 1], preferred_element_type=jnp.float32
    )
    return context.astype(jnp.bfloat16).reshape(count, local_heads * HEAD_DIM)


def on_device(
    queries,
    key_values,
    hidden,
    lengths,
    page_table,
    out_weight,
    norm_gain,
    expert_choice,
    route_weight,
    gate_up,
    down,
):
    count = queries.shape[0]
    width = hidden.shape[1]
    share = width // lax.axis_size("tp")
    own_start = lax.axis_index("tp") * share
    segment, offset = prompt_layout(lengths[0], count)
    context = attend(queries, key_values, segment)
    attn_part = jnp.dot(
        context,
        lax.all_gather(out_weight, "req", axis=1, tiled=True),
        preferred_element_type=jnp.float32,
    )
    attn = lax.psum(attn_part, "tp")
    mid_full = (hidden.astype(jnp.float32) + attn).astype(jnp.bfloat16)
    mid_wide = lax.optimization_barrier(mid_full).astype(jnp.float32)
    square = jnp.mean(mid_wide * mid_wide, axis=1, keepdims=True)
    normed = (mid_wide * lax.rsqrt(square + epsilon) * norm_gain).astype(jnp.bfloat16)
    mid_own = lax.dynamic_slice_in_dim(mid_wide, own_start, share, 1)
    chosen_count = expert_choice.shape[1]
    experts = lax.axis_size("req") // 2
    capacity = 2 * ((count * chosen_count * 2 + 3 * experts - 1) // (3 * experts))
    flat_choice = expert_choice.reshape(-1)
    hits = (flat_choice[:, None] == jnp.arange(experts, dtype=jnp.int32)[None, :]).astype(jnp.int32)
    ranks = jnp.sum((jnp.cumsum(hits, axis=0) - hits) * hits, axis=1)
    target = flat_choice * capacity + ranks
    onehot = (target[:, None] == jnp.arange(experts * capacity, dtype=jnp.int32)[None, :]).astype(
        jnp.bfloat16
    )
    selector = jnp.sum(onehot.reshape(count, chosen_count, experts * capacity), axis=1)
    outgoing = jnp.dot(selector.T, normed, preferred_element_type=jnp.float32).astype(jnp.bfloat16)
    outgoing = outgoing.reshape(experts, capacity, normed.shape[1])
    gate_up_local = gate_up[0]
    down_local = down[0]
    units = down_local.shape[0]
    doubled = jnp.broadcast_to(outgoing[:, None], (experts, 2, capacity, outgoing.shape[2]))
    doubled = doubled.reshape(2 * experts, capacity, outgoing.shape[2])
    full_rows = lax.all_to_all(doubled, "req", split_axis=0, concat_axis=0, tiled=True)
    senders = full_rows.shape[0]
    items = full_rows.shape[1]
    projected = jnp.dot(
        full_rows.reshape(senders * items, width), gate_up_local, preferred_element_type=jnp.float32
    )
    activated = (jax.nn.silu(projected[:, :units]) * projected[:, units:]).astype(jnp.bfloat16)
    partial_value = jnp.dot(activated, down_local, preferred_element_type=jnp.float32).astype(
        jnp.bfloat16
    )
    incoming = lax.all_to_all(
        partial_value.reshape(senders, items, width), "req", split_axis=0, concat_axis=0, tiled=True
    )
    slot_out = jnp.sum(incoming.reshape(experts, 2, capacity, width).astype(jnp.float32), axis=1)
    slot_out = slot_out.reshape(experts * capacity, width)
    picked = jnp.take(slot_out, target, axis=0).reshape(count, chosen_count, width)
    moe_part = jnp.sum(picked * route_weight[:, :, None], axis=1)
    moe = lax.psum_scatter(
        moe_part.astype(jnp.bfloat16), "tp", scatter_dimension=1, tiled=True
    ).astype(jnp.float32)
    layer_out = (mid_own + moe).astype(jnp.bfloat16)
    pages = page_table[0]
    flat_pages = pages.reshape(-1)
    pool_pages = flat_pages.shape[0]
    page_of = segment * pages.shape[1] + offset // PAGE
    slot_page = jnp.sum(
        jnp.where(
            page_of[:, None] == jnp.arange(pool_pages, dtype=jnp.int32)[None, :],
            flat_pages[None, :],
            0,
        ),
        axis=1,
    )
    cache_rows = slot_page * PAGE + offset % PAGE
    cache = (
        jnp.zeros((pool_pages * PAGE, key_values.shape[1]), jnp.bfloat16)
        .at[cache_rows]
        .set(key_values)
    )
    return (layer_out, cache.reshape(pool_pages, PAGE, key_values.shape[1]))


def solution(mesh):
    placed = (
        P("req", "tp"),
        P("req", "tp"),
        P("req", None),
        P("req", None),
        P("req", None, None),
        P("tp", "req"),
        P(),
        P("req", None),
        P("req", None),
        P("req", None, "tp"),
        P("req", "tp", None),
    )
    return jax.shard_map(
        on_device,
        mesh=mesh,
        in_specs=placed,
        out_specs=(P("req", "tp"), P("req", None, "tp")),
        check_vma=False,
    )
```

profile of v0, /device:TPU:6, one launch (start us, length us, event | category | flops | bytes accessed | tf_op | source)
XLA Modules:
  0.0 765.0 jit_solution(7705690440970895287)
XLA Ops:
  7.2 0.7 all-gather.3.cloned.1.call-update
  8.0 0.8 reshape.288
  8.7 0.8 reduce-window.10
  9.6 0.1 convert_reduce_fusion.1
  9.7 0.1 fusion.30
  9.8 1.1 fusion.41
  10.9 0.2 fusion.7
  11.2 0.1 copy.57
  11.2 0.8 copy.58
  12.0 0.1 eq.88
  12.2 117.9 %all-gather.3.cloned.1.call-done = bf16[128,20,640]{2,1,0:T(8,128)(2,1)} async-done(((bf16[1,20,640]{2,1,0:T(8,128)(2,1)}), bf16[128,20,640]{2,1,0:T(8,128)(2,1)}) %all-gather.3.cloned.1.call-update) | async-done | bytes 3276816 | tf_op jit(solution)/shard_map/all_gather | solution.py:66
  130.1 6.1 reshape.320
  136.2 3.9 fusion.22
  140.1 0.1 reshape.294
  140.3 0.9 reduce-window.11
  141.2 0.2 slice_reduce_fusion
  141.5 0.1 fusion.20
  141.6 0.1 reduce_sum.93
  141.7 0.1 copy.61
  141.8 0.1 fusion.11
  142.0 56.9 %all-reduce.2.cloned.1.call-done = f32[64,2560]{1,0:T(8,128)} async-done(((f32[64,2560]{1,0:T(8,128)}), f32[64,2560]{1,0:T(8,128)}) %all-reduce.2.cloned.1.call-update) | async-done | bytes 655376 | tf_op jit(solution)/shard_map/psum | solution.py:69
  198.9 1.1 add_convert_fusion
  200.0 0.2 multiply_reduce_fusion.1
  200.2 0.9 fusion.3
  201.1 0.4 broadcast_in_dim.85
  201.6 253.6 %all_to_all.10 = bf16[128,8,2560]{2,1,0:T(8,128)(2,1)S(1)} all-to-all(bf16[128,8,2560]{2,1,0:T(8,128)(2,1)S(1)} %bitcast.109), channel_id=1, replica_groups=mesh['req'=128,'tp'=4] {'req'}, dimensions={0} | all-to-all | bytes 10485760 | tf_op jit(solution)/shard_map/all_to_all | solution.py:93
  455.2 2.2 fusion
  457.4 4.0 fusion.2
  461.4 9.2 %all-to-all-start.1 = ((bf16[128,8,2560]{2,1,0:T(8,128)(2,1)}), bf16[128,8,2560]{2,1,0:T(8,128)(2,1)}, u32[]{:S(2)}, u32[]{:S(2)}) async-start(bf16[128,8,2560]{2,1,0:T(8,128)(2,1)} %fusion.2), calls=%async_computation.1 | async-start | bytes 10485760 | tf_op jit(solution)/shard_map/all_to_all | solution.py:103
  470.6 0.2 reduce-scatter.4.cloned.1.call-start
  470.8 0.1 copy.63
  470.9 0.1 mul.113
  471.1 0.1 copy.62
  471.2 0.1 copy.64
  471.3 0.1 copy.65
  471.4 0.1 broadcast_in_dim.91
  471.5 195.2 %all-to-all-done.1 = bf16[128,8,2560]{2,1,0:T(8,128)(2,1)} async-done(((bf16[128,8,2560]{2,1,0:T(8,128)(2,1)}), bf16[128,8,2560]{2,1,0:T(8,128)(2,1)}, u32[]{:S(2)}, u32[]{:S(2)}) %all-to-all-start.1) | async-done | bytes 5242912 | tf_op jit(solution)/shard_map/all_to_all | solution.py:103
  666.7 6.2 convert_reduce_fusion
  673.0 8.4 %gather_fusion = f32[384,2560]{1,0:T(8,128)} fusion(f32[512,2560]{1,0:T(8,128)} %bitcast.108, s32[1024]{0:T(1024)S(1)} %pad_clamp_fusion), kind=kCustom, calls=%fused_computation | custom fusion | bytes 7865856 | tf_op jit(solution)/shard_map/jit(_take)/gather | solution.py:108
  681.3 5.1 gather.7
  686.5 4.7 multiply_reduce_fusion
  691.2 1.1 copy.67
  692.3 0.1 select_reduce_fusion.1
  692.4 0.1 select_reduce_fusion
  692.5 1.6 scatter_custom_fusion
  694.2 62.5 %reduce-scatter.4.cloned.1.call-done = bf16[640,64]{1,0:T(8,128)(2,1)} async-done(((bf16[2560,64]{1,0:T(8,128)(2,1)}), bf16[640,64]{1,0:T(8,128)(2,1)}) %reduce-scatter.4.cloned.1.call-update) | async-done | bytes 81936
  756.7 1.0 copy.68
  757.8 0.7 add_convert_fusion.1
  (33 shorter events, 0.4 us)
Async XLA Ops:
  7.2 448.0 %copy-start = (bf16[1,2560,384]{2,1,0:T(8,128)(2,1)S(1)}, bf16[1,2560,384]{2,1,0:T(8,128)(2,1)}, u32[]{:S(2)}) copy-start(bf16[1,2560,384]{2,1,0:T(8,128)(2,1)} %param.20) | copy-start | bytes 5898244
  7.2 122.9 %all-gather.3.cloned.1.call-start = ((), (), s32[]{:S(2)}) async-start(), calls=%async_computation.4 | async-start | bytes 3962880 | tf_op jit(solution)/shard_map/all_gather | solution.py:66
  7.9 191.0 %all-reduce.2.cloned.1.call-start = ((), (), s32[]{:S(2)}) async-start(), calls=%async_computation.3 | async-start | bytes 1310720 | tf_op jit(solution)/shard_map/psum | solution.py:69
  12.1 129.6 %copy-start.2 = (s32[64,6]{0,1:T(8,128)S(1)}, s32[64,6]{0,1:T(8,128)}, u32[]{:S(2)}) copy-start(s32[64,6]{0,1:T(8,128)} %param.18) | copy-start | bytes 4612
  12.2 186.7 %copy-start.1 = (bf16[64,2560]{1,0:T(8,128)(2,1)S(1)}, bf16[64,2560]{1,0:T(8,128)(2,1)}, u32[]{:S(2)}) copy-start(bf16[64,2560]{1,0:T(8,128)(2,1)} %param.13) | copy-start | bytes 983044
  136.2 64.0 %copy-start.3 = (f32[2560]{0:T(1024)S(1)}, f32[2560]{0:T(1024)}, u32[]{:S(2)}) copy-start(f32[2560]{0:T(1024)} %param.17) | copy-start | bytes 30724
  455.2 2.2 copy-start.6
  461.4 9.8 %copy-start.4 = (f32[64,6]{0,1:T(8,128)S(1)}, f32[64,6]{0,1:T(8,128)}, u32[]{:S(2)}) copy-start(f32[64,6]{0,1:T(8,128)} %param.19) | copy-start | bytes 4612
  461.4 9.9 %copy-start.5 = (s32[1,4,2]{1,2,0:T(2,128)S(1)}, s32[1,4,2]{1,2,0:T(2,128)}, u32[]{:S(2)}) copy-start(s32[1,4,2]{1,2,0:T(2,128)} %param.15) | copy-start | bytes 100
  461.4 10.1 %copy-start.7 = (s32[1,4]{1,0:T(1,128)S(1)}, s32[1,4]{1,0:T(1,128)}, u32[]{:S(2)}) copy-start(s32[1,4]{1,0:T(1,128)} %param.14) | copy-start | bytes 52
  461.4 205.3 %all-to-all-start.1 = ((bf16[128,8,2560]{2,1,0:T(8,128)(2,1)}), bf16[128,8,2560]{2,1,0:T(8,128)(2,1)}, u32[]{:S(2)}, u32[]{:S(2)}) async-start(bf16[128,8,2560]{2,1,0:T(8,128)(2,1)} %fusion.2), calls=%async_computation.1 | async-start | bytes 10485760 | tf_op jit(solution)/shard_map/all_to_all | solution.py:103
  470.6 286.2 %reduce-scatter.4.cloned.1.call-start = ((), (), s32[]{:S(2)}) async-start(), calls=%async_computation.5 | async-start | bytes 819200
Sparse Core Ops, SparseCore 0:
  12.3 117.7 all-gather.2
  140.2 58.6 all-reduce.1
  692.4 64.2 reduce-scatter.3
where the time goes:
time: 766 us; the launch traced here: 765 us
  waiting for transfers between devices  433 us (57%)
  blocking collectives  254 us (33%)
  local copies, waits for them, and re-layouts  26.8 us (3%)
  other arithmetic  15.5 us (2%)
  between operations  13.9 us (2%)
  matrix products  12.3 us (2%)
  starting transfers between devices  9.47 us (1%)
    all_to_all x1, blocking collectives, on_device(): lax.all_to_all(doubled, 'req', split_axis=0, concat_axis=0, tiled=True)  254 us
    all_to_all x1, waiting for transfers between devices, on_device(): lax.all_to_all(partial_value.reshape(senders, items, width), 'req', split...  195 us
    all_gather x1, waiting for transfers between devices, on_device(): lax.all_gather(out_weight, 'req', axis=1, tiled=True)  118 us
    unnamed x4, waiting for transfers between devices  63.2 us
    psum x1, waiting for transfers between devices, on_device(): attn = lax.psum(attn_part, 'tp')  56.9 us
  transfers between devices with their start and end apart: 4, of which 4 were waited for; matrix products, arithmetic and copies ran while one was open for 1% of the time, Pallas kernels for 0%

commit v1 on v0

v1 whole, which is shorter than its diff:
```python
import jax
import jax.numpy as jnp
from jax import lax
from jax.sharding import Mesh, PartitionSpec as P

HEAD_DIM = 128
PAGE = 16
SLOTS = 8
epsilon = 1e-05

AXES = ("zh", "y", "x", "c", "tp")
REQ = ("zh", "y", "x", "c")
PLANE = ("y", "x")
LINE = ("zh", "tp")
F32 = jnp.float32
BF16 = jnp.bfloat16
I32 = jnp.int32


def dot(a, b, dims):
    return lax.dot_general(a, b, (dims, ((), ())), preferred_element_type=F32)


def iota(shape, dim):
    return lax.broadcasted_iota(I32, shape, dim)


def from_ahead(value, axis, step, size):
    return lax.ppermute(value, axis, [((i + step) % size, i) for i in range(size)])


def swap_cores(value):
    return lax.ppermute(value, "c", [(0, 1), (1, 0)])


def prompt_layout(lengths, count):
    ends = [lengths[0]]
    for i in range(1, lengths.shape[0]):
        ends.append(ends[-1] + lengths[i])
    return ends


def attend(queries, key_values, segment_row, segment_col):
    count = queries.shape[0]
    heads = queries.shape[1] // HEAD_DIM
    keys, values = key_values[:, :HEAD_DIM], key_values[:, HEAD_DIM:]
    stacked = jnp.concatenate(
        [queries[:, h * HEAD_DIM : (h + 1) * HEAD_DIM] for h in range(heads)], axis=0
    )
    scores = dot(stacked, keys, ((1,), (1,))) * HEAD_DIM ** (-0.5)
    scores = scores.reshape(heads, count, count)
    allowed = (segment_col == segment_row) & (iota((count, count), 1) <= iota((count, count), 0))
    scores = jnp.where(allowed[None], scores, -1e30)
    highest = jnp.max(scores, axis=-1, keepdims=True)
    weights = jnp.exp(scores - highest)
    probs = (weights / jnp.sum(weights, axis=-1, keepdims=True)).astype(BF16)
    context = dot(probs.reshape(heads * count, count), values, ((1,), (0,))).astype(BF16)
    return jnp.concatenate(
        [context[h * count : (h + 1) * count] for h in range(heads)], axis=1
    )


def routing(choice_t, weight_t, first, own_experts, blocks):
    top, tokens = choice_t.shape
    count = tokens // blocks
    local = (choice_t - first).T
    weight = weight_t.T
    named = jnp.zeros((tokens, own_experts), F32)
    routed = jnp.zeros((tokens, own_experts), F32)
    places = iota((tokens, own_experts), 1)
    for k in range(top):
        hit = local[:, k : k + 1] == places
        named = named + hit.astype(F32)
        routed = routed + jnp.where(hit, weight[:, k : k + 1], 0.0)
    here, before = iota((tokens, tokens), 0), iota((tokens, tokens), 1)
    earlier = ((before < here) & (before // count == here // count)).astype(BF16)
    named = named.astype(BF16)
    ranks = dot(earlier, named, ((1,), (0,))).astype(BF16)
    high = lax.reduce_precision(routed, 8, 7)
    low = (routed - high).astype(BF16)
    high = high.astype(BF16)
    rows = own_experts * blocks * SLOTS
    spread = (
        iota((own_experts, rows), 1) // (blocks * SLOTS) == iota((own_experts, rows), 0)
    ).astype(BF16)
    column = iota((tokens, rows), 1)
    mine = (column // SLOTS) % blocks == iota((tokens, rows), 0) // count
    taken = (
        mine
        & (dot(named, spread, ((1,), (0,))) > 0.5)
        & (dot(ranks, spread, ((1,), (0,))).astype(I32) == column % SLOTS)
    )
    selector = taken.astype(BF16)
    parts = [
        jnp.where(taken, dot(part, spread, ((1,), (0,))), 0.0).astype(BF16)
        for part in (high, low)
    ]
    return selector, parts


def normalize(mid, gain):
    wide = mid.astype(F32)
    square = jnp.mean(wide * wide, axis=1, keepdims=True)
    return (wide * lax.rsqrt(square + epsilon) * gain).astype(BF16)


def features_joined(pieces):
    return jnp.concatenate(pieces, axis=1)


def experts_of(rows, weights):
    total = None
    for gate_up, down in weights:
        units = down.shape[0]
        projected = dot(rows, gate_up, ((1,), (0,)))
        activated = (jax.nn.silu(projected[:, :units]) * projected[:, units:]).astype(BF16)
        part = dot(activated, down, ((1,), (0,)))
        total = part if total is None else total + part
    return total.astype(BF16)


def combined(returned, parts):
    high, low = parts
    return dot(high, returned, ((1,), (0,))) + dot(low, returned, ((1,), (0,)))


def on_device(
    queries,
    key_values,
    hidden,
    lengths,
    page_table,
    out_weight,
    norm_gain,
    expert_choice,
    route_weight,
    gate_up,
    down,
):
    count = queries.shape[0]
    width = hidden.shape[1]
    n_zh, n_tp = lax.axis_size("zh"), lax.axis_size("tp")
    planes = lax.axis_size("y") * lax.axis_size("x")
    zh, tp = lax.axis_index("zh"), lax.axis_index("tp")
    share = width // n_tp
    own_start = tp * share
    columns = out_weight.shape[1]

    weight_t = out_weight.T
    shards = [
        lax.ppermute(
            weight_t,
            LINE,
            [(a * n_tp + b, ((b - k) % n_zh) * n_tp + a) for a in range(n_zh) for b in range(n_tp)],
        )
        for k in range(n_zh)
    ]
    choice_t = expert_choice.T
    rw_t = route_weight.T
    choices = [choice_t] + [from_ahead(choice_t, "zh", j, n_zh) for j in range(1, n_zh)]
    route = [rw_t] + [from_ahead(rw_t, "zh", j, n_zh) for j in range(1, n_zh)]

    row = lengths[0]
    places = jnp.arange(count, dtype=I32)
    ends = jnp.cumsum(row)
    starts = ends - row
    segment = jnp.sum((ends[None, :] <= places[:, None]).astype(I32), axis=1)
    picked = segment[:, None] == jnp.arange(row.shape[0], dtype=I32)[None, :]
    offset = places - jnp.sum(jnp.where(picked, starts[None, :], 0), axis=1)

    context = attend(queries, key_values, segment[None, :], segment[:, None])
    contexts = jnp.stack([context] + [from_ahead(context, "tp", j, n_tp) for j in range(1, n_tp)])

    sent = jnp.concatenate(shards, axis=0)
    sent = jnp.broadcast_to(sent[None], (planes,) + sent.shape)
    half = lax.all_to_all(sent, PLANE, 0, 0, tiled=True)
    other = swap_cores(half)

    gate_up_own, down_own = gate_up[0], down[0]
    weights = ((gate_up_own, down_own), (swap_cores(gate_up_own), swap_cores(down_own)))

    blocks = [
        lax.dynamic_index_in_dim(contexts, (zh + k - tp) % n_tp, 0, keepdims=False)
        for k in range(n_zh)
    ]
    stacked = jnp.concatenate(blocks, axis=0)
    halves = []
    for piece in (half, other):
        full = dot(stacked, piece.reshape(-1, piece.shape[2]), ((1,), (1,)))
        full = full.reshape(n_zh, count, planes, n_zh, columns)
        halves.append(sum(full[k, :, :, k, :] for k in range(n_zh)))
    core = lax.axis_index("c")
    first = jnp.where(core == 0, halves[0], halves[1])
    second = jnp.where(core == 0, halves[1], halves[0])
    attn = jnp.stack([first, second], axis=2).reshape(count, share)
    hidden_own = lax.dynamic_slice_in_dim(hidden, own_start, share, 1)
    mid_own = (hidden_own.astype(F32) + attn).astype(BF16)
    mid_own = lax.optimization_barrier(mid_own)

    distant = jnp.concatenate([from_ahead(mid_own, "zh", j, n_zh) for j in range(1, n_zh)], axis=0)
    near = lax.all_gather(mid_own, "tp")
    near = features_joined([near[i] for i in range(n_tp)])
    far = [distant] + [from_ahead(distant, "tp", j, n_tp) for j in range(1, n_tp)]
    far = jnp.stack(far)
    own_experts = planes
    first_expert = zh * own_experts
    near_sel, near_parts = routing(choices[0], route[0], first_expert, own_experts, 1)
    far_sel, far_parts = routing(
        jnp.concatenate(choices[1:], axis=1),
        jnp.concatenate(route[1:], axis=1),
        first_expert,
        own_experts,
        n_zh - 1,
    )
    near_rows = dot(near_sel, normalize(near, norm_gain), ((0,), (0,))).astype(BF16)
    near_rows = near_rows.reshape(planes, SLOTS, width)
    near_in = lax.all_to_all(near_rows, PLANE, 0, 0, tiled=True)
    far_mid = features_joined(
        [
            lax.dynamic_index_in_dim(far, (i - tp) % n_tp, 0, keepdims=False)
            for i in range(n_tp)
        ]
    )
    far_rows = dot(far_sel, normalize(far_mid, norm_gain), ((0,), (0,))).astype(BF16)
    far_rows = far_rows.reshape(planes, (n_zh - 1) * SLOTS, width)
    far_in = lax.all_to_all(far_rows, PLANE, 0, 0, tiled=True)

    far_out = experts_of(far_in.reshape(-1, width), weights).reshape(far_in.shape)
    far_back = lax.all_to_all(far_out, PLANE, 0, 0, tiled=True)
    near_out = experts_of(near_in.reshape(-1, width), weights).reshape(near_in.shape)
    near_back = lax.all_to_all(near_out, PLANE, 0, 0, tiled=True)

    far_moe = combined(far_back.reshape(-1, width), far_parts).astype(BF16)
    far_quarters = jnp.stack([far_moe[:, i * share : (i + 1) * share] for i in range(n_tp)])
    far_sum = lax.dynamic_index_in_dim(far_quarters, tp, 0, keepdims=False).astype(F32)
    for j in range(1, n_tp):
        piece = lax.dynamic_index_in_dim(far_quarters, (tp - j) % n_tp, 0, keepdims=False)
        far_sum = far_sum + from_ahead(piece, "tp", j, n_tp).astype(F32)
    far_sum = far_sum.astype(BF16)
    near_moe = combined(near_back.reshape(-1, width), near_parts).astype(BF16)
    near_quarters = jnp.stack([near_moe[:, i * share : (i + 1) * share] for i in range(n_tp)])
    near_got = lax.all_to_all(near_quarters, "tp", 0, 0, tiled=True)
    moe = jnp.sum(near_got.astype(F32), axis=0)
    for j in range(1, n_zh):
        moe = moe + from_ahead(far_sum[(j - 1) * count : j * count], "zh", -j, n_zh).astype(F32)
    layer_out = (mid_own.astype(F32) + moe).astype(BF16)

    pages = page_table[0]
    flat_pages = pages.reshape(-1)
    pool = flat_pages.shape[0]
    page_of = segment * pages.shape[1] + offset // PAGE
    slot_page = jnp.sum(
        jnp.where(
            page_of[:, None] == jnp.arange(pool, dtype=I32)[None, :], flat_pages[None, :], 0
        ),
        axis=1,
    )
    cache_rows = slot_page * PAGE + offset % PAGE
    put = (iota((pool * PAGE, count), 0) == cache_rows[None, :]).astype(BF16)
    cache = dot(put, key_values, ((1,), (0,))).astype(BF16)
    return (layer_out, cache.reshape(pool, PAGE, key_values.shape[1]))


def solution(mesh):
    grid = Mesh(mesh.devices.reshape(4, 4, 4, 2, 4), AXES)
    placed = (
        P(REQ, "tp"),
        P(REQ, "tp"),
        P(REQ, None),
        P(REQ, None),
        P(REQ, None, None),
        P("tp", REQ),
        P(),
        P(REQ, None),
        P(REQ, None),
        P(REQ, None, "tp"),
        P(REQ, "tp", None),
    )
    return jax.shard_map(
        on_device,
        mesh=grid,
        in_specs=placed,
        out_specs=(P(REQ, "tp"), P(REQ, None, "tp")),
        check_vma=False,
    )
```

time: 766 us -> 316 us (0.41)
  the two profiles are of different devices: /device:TPU:6 before, /device:TPU:109 now
where the time goes in v1:
time: 316 us; the launch traced here: 314 us
  starting transfers between devices  159 us (50%)
  waiting for transfers between devices  79.7 us (25%)
  matrix products  36.2 us (11%)
  blocking collectives  22.4 us (7%)
  local copies, waits for them, and re-layouts  7.98 us (3%)
  other arithmetic  6.63 us (2%)
    ppermute x21, starting transfers between devices, from_ahead(): lax.ppermute(value, axis, [((i + step) % size, i) for i in range(size)])  84.3 us
    ppermute x21, waiting for transfers between devices, from_ahead(): lax.ppermute(value, axis, [((i + step) % size, i) for i in range(size)])  37.4 us
    dot_general x23, matrix products, dot(): return lax.dot_general(a, b, (dims, ((), ())), preferred_element_type=F32)  36.2 us
    ppermute x4, starting transfers between devices, on_device(): lax.ppermute(weight_t, LINE, [(a * n_tp + b, (b - k) % n_zh * n_tp + a) f...  22.6 us
    all_gather x1, blocking collectives, on_device(): near = lax.all_gather(mid_own, 'tp')  22.4 us
    all_to_all x1, waiting for transfers between devices, on_device(): far_back = lax.all_to_all(far_out, PLANE, 0, 0, tiled=True)  20.6 us
    all_to_all x1, waiting for transfers between devices, on_device(): half = lax.all_to_all(sent, PLANE, 0, 0, tiled=True)  19.7 us
    ppermute x3, starting transfers between devices, swap_cores(): return lax.ppermute(value, 'c', [(0, 1), (1, 0)])  9.99 us
  transfers between devices with their start and end apart: 34, of which 8 were waited for; matrix products, arithmetic and copies ran while one was open for 16% of the time, Pallas kernels for 0%

profile of v1, /device:TPU:109, one launch (start us, length us, event | category | flops | bytes accessed | tf_op | source)
XLA Modules:
  0.0 314.0 jit_solution(2989834896367182189)
XLA Ops:
  2.6 6.4 %collective-permute-start.5 = (bf16[20,640]{1,0:T(8,128)(2,1)}, bf16[20,640]{1,0:T(8,128)(2,1)S(1)}, u32[]{:S(2)}, u32[]{:S(2)}) collective-permute-start(bf16[20,640]{1,0:T(8,128)(2,1)} %bitcast.236), channel_id=1, source_target_pairs={{0,256},{1,384},{2,0},{3,128},{128,257},{129,385},{130,1},{131,129... | collective-permute-start | bytes 76808 | tf_op jit(solution)/shard_map/ppermute | solution.py:151
  8.9 10.2 %collective-permute-start.4 = (bf16[20,640]{1,0:T(8,128)(2,1)}, bf16[20,640]{1,0:T(8,128)(2,1)S(1)}, u32[]{:S(2)}, u32[]{:S(2)}) collective-permute-start(bf16[20,640]{1,0:T(8,128)(2,1)} %bitcast.237), channel_id=1, source_target_pairs={{0,384},{1,0},{2,128},{3,256},{128,385},{129,1},{130,129},{131,257... | collective-permute-start | bytes 76808 | tf_op jit(solution)/shard_map/ppermute | solution.py:151
  19.1 4.1 %collective-permute-start.3 = (bf16[20,640]{1,0:T(8,128)(2,1)}, bf16[20,640]{1,0:T(8,128)(2,1)S(1)}, u32[]{:S(2)}, u32[]{:S(2)}) collective-permute-start(bf16[20,640]{1,0:T(8,128)(2,1)} %bitcast.238), channel_id=1, source_target_pairs={{0,0},{1,128},{2,256},{3,384},{128,1},{129,129},{130,257},{131,385... | collective-permute-start | bytes 76808 | tf_op jit(solution)/shard_map/ppermute | solution.py:151
  23.3 1.9 collective-permute-start.12
  33.6 9.8 %collective-permute-start.11 = (s32[6,64]{1,0:T(8,128)}, s32[6,64]{1,0:T(8,128)S(1)}, u32[]{:S(2)}, u32[]{:S(2)}) collective-permute-start(s32[6,64]{1,0:T(8,128)} %bitcast.230), channel_id=1, source_target_pairs={{256,0},{384,128},{0,256},{128,384},{257,1},{385,129},{1,257},{129... | collective-permute-start | bytes 4616 | tf_op jit(solution)/shard_map/ppermute | solution.py:29
  43.4 6.0 %collective-permute-start.10 = (s32[6,64]{1,0:T(8,128)}, s32[6,64]{1,0:T(8,128)S(1)}, u32[]{:S(2)}, u32[]{:S(2)}) collective-permute-start(s32[6,64]{1,0:T(8,128)} %bitcast.231), channel_id=1, source_target_pairs={{128,0},{256,128},{384,256},{0,384},{129,1},{257,129},{385,257},{1... | collective-permute-start | bytes 4616 | tf_op jit(solution)/shard_map/ppermute | solution.py:29
  49.4 2.6 collective-permute-start.2
  53.4 6.9 %all-to-all-start = ((bf16[16,80,640]{2,1,0:T(8,128)(2,1)}), bf16[16,80,640]{2,1,0:T(8,128)(2,1)S(1)}, u32[]{:S(2)}, u32[]{:S(2)}) async-start(bf16[16,80,640]{2,1,0:T(8,128)(2,1)} %broadcast_in_dim.186), calls=%async_computation | async-start | bytes 3276800 | tf_op jit(solution)/shard_map/all_to_all | solution.py:176
  61.3 19.7 %all-to-all-done = bf16[16,80,640]{2,1,0:T(8,128)(2,1)S(1)} async-done(((bf16[16,80,640]{2,1,0:T(8,128)(2,1)}), bf16[16,80,640]{2,1,0:T(8,128)(2,1)S(1)}, u32[]{:S(2)}, u32[]{:S(2)}) %all-to-all-start) | async-done | bytes 1638432 | tf_op jit(solution)/shard_map/all_to_all | solution.py:176
  81.4 3.0 collective-permute-start.7
  84.7 2.0 collective-permute-start.1
  86.7 2.8 collective-permute-start
  89.5 2.5 collective-permute-start.8
  96.6 2.9 fusion.9
  100.7 3.7 %collective-permute-start.16 = (bf16[64,640]{1,0:T(8,128)(2,1)S(1)}, bf16[64,640]{1,0:T(8,128)(2,1)S(1)}, u32[]{:S(2)}, u32[]{:S(2)}) collective-permute-start(bf16[64,640]{1,0:T(8,128)(2,1)S(1)} %add_convert_fusion.1), channel_id=1, source_target_pairs={{128,0},{256,128},{384,256},{0,384},{129,1},{257,129},{385,257},{1... | collective-permute-start | bytes 245768 | tf_op jit(solution)/shard_map/ppermute | solution.py:29
  104.4 8.4 %collective-permute-start.17 = (bf16[64,640]{1,0:T(8,128)(2,1)S(1)}, bf16[64,640]{1,0:T(8,128)(2,1)S(1)}, u32[]{:S(2)}, u32[]{:S(2)}) collective-permute-start(bf16[64,640]{1,0:T(8,128)(2,1)S(1)} %add_convert_fusion.1), channel_id=1, source_target_pairs={{256,0},{384,128},{0,256},{128,384},{257,1},{385,129},{1,257},{129... | collective-permute-start | bytes 245768 | tf_op jit(solution)/shard_map/ppermute | solution.py:29
  112.8 1.9 collective-permute-start.18
  114.8 22.4 %all-gather = bf16[256,640]{1,0:T(8,128)(2,1)S(1)} all-gather(bf16[64,640]{1,0:T(8,128)(2,1)S(1)} %add_convert_fusion.1), channel_id=2, replica_groups=mesh['zh'=4,'y'=4,'x'=4,'c'=2,'tp'=4] {'tp'}, dimensions={0}, use_global_device_ids=true | all-gather | bytes 409600 | tf_op jit(solution)/shard_map/all_gather | solution.py:201
  137.4 2.9 collective-permute-start.21
  142.3 2.8 collective-permute-start.19
  146.4 7.3 %all-to-all-start.1 = ((bf16[16,8,2560]{2,1,0:T(8,128)(2,1)}), bf16[16,8,2560]{2,1,0:T(8,128)(2,1)S(1)}, u32[]{:S(2)}, u32[]{:S(2)}) async-start(bf16[16,8,2560]{2,1,0:T(8,128)(2,1)} %fusion.3), calls=%async_computation.1 | async-start | bytes 1310720 | tf_op jit(solution)/shard_map/all_to_all | solution.py:217
  153.7 7.9 %collective-permute-done.20 = bf16[192,640]{1,0:T(8,128)(2,1)S(1)} collective-permute-done((bf16[192,640]{1,0:T(8,128)(2,1)S(1)}, bf16[192,640]{1,0:T(8,128)(2,1)S(1)}, u32[]{:S(2)}, u32[]{:S(2)}) %collective-permute-start.20) | collective-permute-done | bytes 245792 | tf_op jit(solution)/shard_map/ppermute | solution.py:29
  162.2 2.1 convolution_convert_fusion
  164.4 8.2 %all-to-all-start.4 = ((bf16[16,24,2560]{2,1,0:T(8,128)(2,1)}), bf16[16,24,2560]{2,1,0:T(8,128)(2,1)}, u32[]{:S(2)}, u32[]{:S(2)}) async-start(bf16[16,24,2560]{2,1,0:T(8,128)(2,1)} %bitcast.179), calls=%async_computation.4 | async-start | bytes 3932160 | tf_op jit(solution)/shard_map/all_to_all | solution.py:226
  172.6 4.5 %collective-permute-start.15 = (f32[6,64]{1,0:T(8,128)S(1)}, f32[6,64]{1,0:T(8,128)S(1)}, u32[]{:S(2)}, u32[]{:S(2)}) collective-permute-start(f32[6,64]{1,0:T(8,128)S(1)} %bitcast.232), channel_id=1, source_target_pairs={{384,0},{0,128},{128,256},{256,384},{385,1},{1,129},{129,257},{257... | collective-permute-start | bytes 4616 | tf_op jit(solution)/shard_map/ppermute | solution.py:29
  177.1 6.7 %collective-permute-start.14 = (f32[6,64]{1,0:T(8,128)S(1)}, f32[6,64]{1,0:T(8,128)S(1)}, u32[]{:S(2)}, u32[]{:S(2)}) collective-permute-start(f32[6,64]{1,0:T(8,128)S(1)} %bitcast.233), channel_id=1, source_target_pairs={{256,0},{384,128},{0,256},{128,384},{257,1},{385,129},{1,257},{129... | collective-permute-start | bytes 4616 | tf_op jit(solution)/shard_map/ppermute | solution.py:29
  183.8 3.3 %collective-permute-start.13 = (f32[6,64]{1,0:T(8,128)S(1)}, f32[6,64]{1,0:T(8,128)S(1)}, u32[]{:S(2)}, u32[]{:S(2)}) collective-permute-start(f32[6,64]{1,0:T(8,128)S(1)} %bitcast.234), channel_id=1, source_target_pairs={{128,0},{256,128},{384,256},{0,384},{129,1},{257,129},{385,257},{1... | collective-permute-start | bytes 4616 | tf_op jit(solution)/shard_map/ppermute | solution.py:29
  187.1 4.5 %collective-permute-start.9 = (bf16[192,2560]{1,0:T(8,128)(2,1)S(1)}, bf16[192,2560]{1,0:T(8,128)(2,1)S(1)}, u32[]{:S(2)}, u32[]{:S(2)}) collective-permute-start(bf16[192,2560]{1,0:T(8,128)(2,1)S(1)} %bitcast.177), channel_id=1, source_target_pairs={{0,4},{4,0},{1,5},{5,1},{2,6},{6,2},{3,7},{7,3},{8,12},{12,8},{9,1... | collective-permute-start | bytes 2949128 | tf_op jit(solution)/shard_map/ppermute | solution.py:33
  191.8 2.1 fusion.37
  194.3 2.1 fusion.35
  197.7 2.0 all-to-all-done.4
  199.6 5.9 %all-to-all-start.2 = ((bf16[16,8,2560]{2,1,0:T(8,128)(2,1)}), bf16[16,8,2560]{2,1,0:T(8,128)(2,1)S(1)}, u32[]{:S(2)}, u32[]{:S(2)}) async-start(bf16[16,8,2560]{2,1,0:T(8,128)(2,1)} %fusion.4), calls=%async_computation.2 | async-start | bytes 1310720 | tf_op jit(solution)/shard_map/all_to_all | solution.py:231
  205.5 3.4 %fusion.163 = f32[384,384]{0,1:T(8,128)S(1)} fusion(bf16[384,2560]{1,0:T(8,128)(2,1)} %bitcast.73, bf16[1,2560,384]{2,1,0:T(8,128)(2,1)} %param.20), kind=kOutput, calls=%fused_computation.293 | convolution fusion | flops 754974720 | bytes 4521984 | tf_op jit(solution)/shard_map/dot_general | solution.py:21
  209.6 3.4 %fusion.183 = f32[384,384]{0,1:T(8,128)S(1)} fusion(bf16[384,2560]{1,0:T(8,128)(2,1)} %bitcast.73, bf16[2560,384]{1,0:T(8,128)(2,1)} %collective-permute-done.8), kind=kOutput, calls=%fused_computation.309 | convolution fusion | flops 754974720 | bytes 4521984 | tf_op jit(solution)/shard_map/dot_general | solution.py:21
  213.0 2.0 fusion
  215.1 6.7 %all-to-all-start.5 = ((bf16[16,24,2560]{2,1,0:T(8,128)(2,1)}), bf16[16,24,2560]{2,1,0:T(8,128)(2,1)S(1)}, u32[]{:S(2)}, u32[]{:S(2)}) async-start(bf16[16,24,2560]{2,1,0:T(8,128)(2,1)} %bitcast.176), calls=%async_computation.5 | async-start | bytes 3932160 | tf_op jit(solution)/shard_map/all_to_all | solution.py:229
  227.6 20.6 %all-to-all-done.5 = bf16[16,24,2560]{2,1,0:T(8,128)(2,1)S(1)} async-done(((bf16[16,24,2560]{2,1,0:T(8,128)(2,1)}), bf16[16,24,2560]{2,1,0:T(8,128)(2,1)S(1)}, u32[]{:S(2)}, u32[]{:S(2)}) %all-to-all-start.5) | async-done | bytes 1966112 | tf_op jit(solution)/shard_map/all_to_all | solution.py:229
  248.2 7.2 %all-to-all-start.3 = ((bf16[4,64,640]{2,1,0:T(8,128)(2,1)}), bf16[4,64,640]{2,1,0:T(8,128)(2,1)S(1)}, u32[]{:S(2)}, u32[]{:S(2)}) async-start(bf16[4,64,640]{2,1,0:T(8,128)(2,1)} %pad_maximum_fusion.7), calls=%async_computation.3 | async-start | bytes 655360 | tf_op jit(solution)/shard_map/all_to_all | solution.py:242
  255.4 2.4 fusion.17
  257.8 2.6 fusion.1
  262.8 3.4 %collective-permute-start.23 = (bf16[192,640]{1,0:T(8,128)(2,1)S(1)}, bf16[192,640]{1,0:T(8,128)(2,1)S(1)}, u32[]{:S(2)}, u32[]{:S(2)}) collective-permute-start(bf16[192,640]{1,0:T(8,128)(2,1)S(1)} %get-tuple-element.7), channel_id=1, source_target_pairs={{2,0},{3,1},{0,2},{1,3},{6,4},{7,5},{4,6},{5,7},{10,8},{11,9},{8,1... | collective-permute-start | bytes 737288 | tf_op jit(solution)/shard_map/ppermute | solution.py:29
  266.1 2.9 collective-permute-start.22
  269.9 15.1 %collective-permute-done.23 = bf16[192,640]{1,0:T(8,128)(2,1)S(1)} collective-permute-done((bf16[192,640]{1,0:T(8,128)(2,1)S(1)}, bf16[192,640]{1,0:T(8,128)(2,1)S(1)}, u32[]{:S(2)}, u32[]{:S(2)}) %collective-permute-start.23) | collective-permute-done | bytes 245792 | tf_op jit(solution)/shard_map/ppermute | solution.py:29
  285.1 4.2 %collective-permute-start.27 = (bf16[64,640]{1,0:T(8,128)(2,1)S(1)}, bf16[64,640]{1,0:T(8,128)(2,1)S(1)}, u32[]{:S(2)}, u32[]{:S(2)}) collective-permute-start(bf16[64,640]{1,0:T(8,128)(2,1)S(1)} %get-tuple-element.29), channel_id=1, source_target_pairs={{128,0},{256,128},{384,256},{0,384},{129,1},{257,129},{385,257},{1... | collective-permute-start | bytes 245768 | tf_op jit(solution)/shard_map/ppermute | solution.py:29
  289.4 7.3 %collective-permute-start.26 = (bf16[64,640]{1,0:T(8,128)(2,1)S(1)}, bf16[64,640]{1,0:T(8,128)(2,1)S(1)}, u32[]{:S(2)}, u32[]{:S(2)}) collective-permute-start(bf16[64,640]{1,0:T(8,128)(2,1)S(1)} %get-tuple-element.30), channel_id=1, source_target_pairs={{256,0},{384,128},{0,256},{128,384},{257,1},{385,129},{1,257},{129... | collective-permute-start | bytes 245768 | tf_op jit(solution)/shard_map/ppermute | solution.py:29
  296.7 3.2 %collective-permute-start.25 = (bf16[64,640]{1,0:T(8,128)(2,1)S(1)}, bf16[64,640]{1,0:T(8,128)(2,1)S(1)}, u32[]{:S(2)}, u32[]{:S(2)}) collective-permute-start(bf16[64,640]{1,0:T(8,128)(2,1)S(1)} %get-tuple-element.28), channel_id=1, source_target_pairs={{384,0},{0,128},{128,256},{256,384},{385,1},{1,129},{129,257},{257... | collective-permute-start | bytes 245768 | tf_op jit(solution)/shard_map/ppermute | solution.py:29
  300.0 3.5 %collective-permute-done.26 = bf16[64,640]{1,0:T(8,128)(2,1)S(1)} collective-permute-done((bf16[64,640]{1,0:T(8,128)(2,1)S(1)}, bf16[64,640]{1,0:T(8,128)(2,1)S(1)}, u32[]{:S(2)}, u32[]{:S(2)}) %collective-permute-start.26) | collective-permute-done | bytes 81952 | tf_op jit(solution)/shard_map/ppermute | solution.py:29
  303.6 9.8 %collective-permute-done.25 = bf16[64,640]{1,0:T(8,128)(2,1)S(1)} collective-permute-done((bf16[64,640]{1,0:T(8,128)(2,1)S(1)}, bf16[64,640]{1,0:T(8,128)(2,1)S(1)}, u32[]{:S(2)}, u32[]{:S(2)}) %collective-permute-start.25) | collective-permute-done | bytes 81952 | tf_op jit(solution)/shard_map/ppermute | solution.py:29
  (194 shorter events, 34.7 us)
Async XLA Ops:
  0.6 32.9 %collective-permute-start.6 = (bf16[20,640]{1,0:T(8,128)(2,1)}, bf16[20,640]{1,0:T(8,128)(2,1)S(1)}, u32[]{:S(2)}, u32[]{:S(2)}) collective-permute-start(bf16[20,640]{1,0:T(8,128)(2,1)} %bitcast.235), channel_id=1, source_target_pairs={{0,128},{1,256},{2,384},{3,0},{128,129},{129,257},{130,385},{131,1... | collective-permute-start | bytes 76808 | tf_op jit(solution)/shard_map/ppermute | solution.py:151
  2.6 40.8 %collective-permute-start.5 = (bf16[20,640]{1,0:T(8,128)(2,1)}, bf16[20,640]{1,0:T(8,128)(2,1)S(1)}, u32[]{:S(2)}, u32[]{:S(2)}) collective-permute-start(bf16[20,640]{1,0:T(8,128)(2,1)} %bitcast.236), channel_id=1, source_target_pairs={{0,256},{1,384},{2,0},{3,128},{128,257},{129,385},{130,1},{131,129... | collective-permute-start | bytes 76808 | tf_op jit(solution)/shard_map/ppermute | solution.py:151
  8.9 40.4 %collective-permute-start.4 = (bf16[20,640]{1,0:T(8,128)(2,1)}, bf16[20,640]{1,0:T(8,128)(2,1)S(1)}, u32[]{:S(2)}, u32[]{:S(2)}) collective-permute-start(bf16[20,640]{1,0:T(8,128)(2,1)} %bitcast.237), channel_id=1, source_target_pairs={{0,384},{1,0},{2,128},{3,256},{128,385},{129,1},{130,129},{131,257... | collective-permute-start | bytes 76808 | tf_op jit(solution)/shard_map/ppermute | solution.py:151
  19.1 32.9 %collective-permute-start.3 = (bf16[20,640]{1,0:T(8,128)(2,1)}, bf16[20,640]{1,0:T(8,128)(2,1)S(1)}, u32[]{:S(2)}, u32[]{:S(2)}) collective-permute-start(bf16[20,640]{1,0:T(8,128)(2,1)} %bitcast.238), channel_id=1, source_target_pairs={{0,0},{1,128},{2,256},{3,384},{128,1},{129,129},{130,257},{131,385... | collective-permute-start | bytes 76808 | tf_op jit(solution)/shard_map/ppermute | solution.py:151
  23.3 61.4 %collective-permute-start.12 = (s32[6,64]{1,0:T(8,128)}, s32[6,64]{1,0:T(8,128)S(1)}, u32[]{:S(2)}, u32[]{:S(2)}) collective-permute-start(s32[6,64]{1,0:T(8,128)} %bitcast.229), channel_id=1, source_target_pairs={{384,0},{0,128},{128,256},{256,384},{385,1},{1,129},{129,257},{257... | collective-permute-start | bytes 4616 | tf_op jit(solution)/shard_map/ppermute | solution.py:29
  26.3 34.7 %copy-start.20 = (s32[128]{0:T(128)}, s32[128]{0:T(128)S(1)}, u32[]{:S(2)}) copy-start(s32[128]{0:T(128)S(1)} %iota_shift-right-logical_fusion.2) | copy-start | bytes 1540
  33.6 27.5 %copy-start.21 = (s32[128]{0:T(128)}, s32[128]{0:T(128)S(1)}, u32[]{:S(2)}) copy-start(s32[128]{0:T(128)S(1)} %broadcast_add_fusion.4) | copy-start | bytes 1540
  33.6 53.1 %collective-permute-start.11 = (s32[6,64]{1,0:T(8,128)}, s32[6,64]{1,0:T(8,128)S(1)}, u32[]{:S(2)}, u32[]{:S(2)}) collective-permute-start(s32[6,64]{1,0:T(8,128)} %bitcast.230), channel_id=1, source_target_pairs={{256,0},{384,128},{0,256},{128,384},{257,1},{385,129},{1,257},{129... | collective-permute-start | bytes 4616 | tf_op jit(solution)/shard_map/ppermute | solution.py:29
  43.4 46.1 %collective-permute-start.10 = (s32[6,64]{1,0:T(8,128)}, s32[6,64]{1,0:T(8,128)S(1)}, u32[]{:S(2)}, u32[]{:S(2)}) collective-permute-start(s32[6,64]{1,0:T(8,128)} %bitcast.231), channel_id=1, source_target_pairs={{128,0},{256,128},{384,256},{0,384},{129,1},{257,129},{385,257},{1... | collective-permute-start | bytes 4616 | tf_op jit(solution)/shard_map/ppermute | solution.py:29
  49.4 44.5 %collective-permute-start.2 = (bf16[64,640]{1,0:T(8,128)(2,1)S(1)}, bf16[64,640]{1,0:T(8,128)(2,1)S(1)}, u32[]{:S(2)}, u32[]{:S(2)}) collective-permute-start(bf16[64,640]{1,0:T(8,128)(2,1)S(1)} %constant_dynamic-update-slice_fusion.5), channel_id=1, source_target_pairs={{3,0},{0,1},{1,2},{2,3},{7,4},{4,5},{5,6},{6,7},{11,8},{8,9},{9,10... | collective-permute-start | bytes 245768 | tf_op jit(solution)/shard_map/ppermute | solution.py:29
  53.4 27.6 %all-to-all-start = ((bf16[16,80,640]{2,1,0:T(8,128)(2,1)}), bf16[16,80,640]{2,1,0:T(8,128)(2,1)S(1)}, u32[]{:S(2)}, u32[]{:S(2)}) async-start(bf16[16,80,640]{2,1,0:T(8,128)(2,1)} %broadcast_in_dim.186), calls=%async_computation | async-start | bytes 3276800 | tf_op jit(solution)/shard_map/all_to_all | solution.py:176
  60.4 21.0 %copy-start.22 = (pred[128]{0:T(512)(128)(4,1)}, pred[128]{0:T(512)(128)(4,1)S(1)}, u32[]{:S(2)}) copy-start(pred[128]{0:T(512)(128)(4,1)S(1)} %compare_and_fusion.2) | copy-start | bytes 388
  60.4 31.7 %copy-start.26 = (s32[192]{0:T(256)}, s32[192]{0:T(256)S(1)}, u32[]{:S(2)}) copy-start(s32[192]{0:T(256)S(1)} %get-tuple-element.63) | copy-start | bytes 2308
  60.4 31.7 %copy-start.27 = (s32[192]{0:T(256)}, s32[192]{0:T(256)S(1)}, u32[]{:S(2)}) copy-start(s32[192]{0:T(256)S(1)} %get-tuple-element.64) | copy-start | bytes 2308
  61.0 31.1 %copy-start.18 = (pred[384]{0:T(512)(128)(4,1)S(1)}, pred[384]{0:T(512)(128)(4,1)}, u32[]{:S(2)}) copy-start(pred[384]{0:T(512)(128)(4,1)} %get-tuple-element.57) | copy-start | bytes 1156
  61.0 31.1 %copy-start.35 = (pred[384]{0:T(512)(128)(4,1)S(1)}, pred[384]{0:T(512)(128)(4,1)}, u32[]{:S(2)}) copy-start(pred[384]{0:T(512)(128)(4,1)} %get-tuple-element.58) | copy-start | bytes 1156
  61.1 31.1 %copy-start.36 = (pred[192]{0:T(512)(128)(4,1)S(1)}, pred[192]{0:T(512)(128)(4,1)}, u32[]{:S(2)}) copy-start(pred[192]{0:T(512)(128)(4,1)} %compare_and_fusion) | copy-start | bytes 580
  81.4 15.1 %collective-permute-start.7 = (bf16[16,80,640]{2,0,1:T(8,128)(2,1)S(1)}, bf16[16,80,640]{2,0,1:T(8,128)(2,1)}, u32[]{:S(2)}, u32[]{:S(2)}) collective-permute-start(bf16[16,80,640]{2,0,1:T(8,128)(2,1)S(1)} %copy.50), channel_id=1, source_target_pairs={{0,4},{4,0},{1,5},{5,1},{2,6},{6,2},{3,7},{7,3},{8,12},{12,8},{9,1... | collective-permute-start | bytes 4915208 | tf_op jit(solution)/shard_map/ppermute | solution.py:33
  84.7 10.3 %collective-permute-start.1 = (bf16[64,640]{1,0:T(8,128)(2,1)S(1)}, bf16[64,640]{1,0:T(8,128)(2,1)S(1)}, u32[]{:S(2)}, u32[]{:S(2)}) collective-permute-start(bf16[64,640]{1,0:T(8,128)(2,1)S(1)} %constant_dynamic-update-slice_fusion.5), channel_id=1, source_target_pairs={{2,0},{3,1},{0,2},{1,3},{6,4},{7,5},{4,6},{5,7},{10,8},{11,9},{8,1... | collective-permute-start | bytes 245768 | tf_op jit(solution)/shard_map/ppermute | solution.py:29
  86.7 8.3 %collective-permute-start = (bf16[64,640]{1,0:T(8,128)(2,1)S(1)}, bf16[64,640]{1,0:T(8,128)(2,1)S(1)}, u32[]{:S(2)}, u32[]{:S(2)}) collective-permute-start(bf16[64,640]{1,0:T(8,128)(2,1)S(1)} %constant_dynamic-update-slice_fusion.5), channel_id=1, source_target_pairs={{1,0},{2,1},{3,2},{0,3},{5,4},{6,5},{7,6},{4,7},{9,8},{10,9},{11,1... | collective-permute-start | bytes 245768 | tf_op jit(solution)/shard_map/ppermute | solution.py:29
  89.5 104.8 %collective-permute-start.8 = (bf16[2560,384]{1,0:T(8,128)(2,1)}, bf16[2560,384]{1,0:T(8,128)(2,1)}, u32[]{:S(2)}, u32[]{:S(2)}) collective-permute-start(bf16[2560,384]{1,0:T(8,128)(2,1)} %bitcast.178), channel_id=1, source_target_pairs={{0,4},{4,0},{1,5},{5,1},{2,6},{6,2},{3,7},{7,3},{8,12},{12,8},{9,1... | collective-permute-start | bytes 5898248 | tf_op jit(solution)/shard_map/ppermute | solution.py:33
  99.6 45.6 %copy-start.28 = (f32[2560]{0:T(1024)S(1)}, f32[2560]{0:T(1024)}, u32[]{:S(2)}) copy-start(f32[2560]{0:T(1024)} %param.17) | copy-start | bytes 30724
  100.7 36.6 %collective-permute-start.16 = (bf16[64,640]{1,0:T(8,128)(2,1)S(1)}, bf16[64,640]{1,0:T(8,128)(2,1)S(1)}, u32[]{:S(2)}, u32[]{:S(2)}) collective-permute-start(bf16[64,640]{1,0:T(8,128)(2,1)S(1)} %add_convert_fusion.1), channel_id=1, source_target_pairs={{128,0},{256,128},{384,256},{0,384},{129,1},{257,129},{385,257},{1... | collective-permute-start | bytes 245768 | tf_op jit(solution)/shard_map/ppermute | solution.py:29
  104.4 33.0 %collective-permute-start.17 = (bf16[64,640]{1,0:T(8,128)(2,1)S(1)}, bf16[64,640]{1,0:T(8,128)(2,1)S(1)}, u32[]{:S(2)}, u32[]{:S(2)}) collective-permute-start(bf16[64,640]{1,0:T(8,128)(2,1)S(1)} %add_convert_fusion.1), channel_id=1, source_target_pairs={{256,0},{384,128},{0,256},{128,384},{257,1},{385,129},{1,257},{129... | collective-permute-start | bytes 245768 | tf_op jit(solution)/shard_map/ppermute | solution.py:29
  112.8 24.6 %collective-permute-start.18 = (bf16[64,640]{1,0:T(8,128)(2,1)S(1)}, bf16[64,640]{1,0:T(8,128)(2,1)S(1)}, u32[]{:S(2)}, u32[]{:S(2)}) collective-permute-start(bf16[64,640]{1,0:T(8,128)(2,1)S(1)} %add_convert_fusion.1), channel_id=1, source_target_pairs={{384,0},{0,128},{128,256},{256,384},{385,1},{1,129},{129,257},{257... | collective-permute-start | bytes 245768 | tf_op jit(solution)/shard_map/ppermute | solution.py:29
  137.4 16.3 %collective-permute-start.21 = (bf16[192,640]{1,0:T(8,128)(2,1)S(1)}, bf16[192,640]{1,0:T(8,128)(2,1)S(1)}, u32[]{:S(2)}, u32[]{:S(2)}) collective-permute-start(bf16[192,640]{1,0:T(8,128)(2,1)S(1)} %constant_dynamic-update-slice_fusion.10), channel_id=1, source_target_pairs={{3,0},{0,1},{1,2},{2,3},{7,4},{4,5},{5,6},{6,7},{11,8},{8,9},{9,10... | collective-permute-start | bytes 737288 | tf_op jit(solution)/shard_map/ppermute | solution.py:29
  140.3 21.3 %collective-permute-start.20 = (bf16[192,640]{1,0:T(8,128)(2,1)S(1)}, bf16[192,640]{1,0:T(8,128)(2,1)S(1)}, u32[]{:S(2)}, u32[]{:S(2)}) collective-permute-start(bf16[192,640]{1,0:T(8,128)(2,1)S(1)} %constant_dynamic-update-slice_fusion.10), channel_id=1, source_target_pairs={{2,0},{3,1},{0,2},{1,3},{6,4},{7,5},{4,6},{5,7},{10,8},{11,9},{8,1... | collective-permute-start | bytes 737288 | tf_op jit(solution)/shard_map/ppermute | solution.py:29
  142.3 19.4 %collective-permute-start.19 = (bf16[192,640]{1,0:T(8,128)(2,1)S(1)}, bf16[192,640]{1,0:T(8,128)(2,1)S(1)}, u32[]{:S(2)}, u32[]{:S(2)}) collective-permute-start(bf16[192,640]{1,0:T(8,128)(2,1)S(1)} %constant_dynamic-update-slice_fusion.10), channel_id=1, source_target_pairs={{1,0},{2,1},{3,2},{0,3},{5,4},{6,5},{7,6},{4,7},{9,8},{10,9},{11,1... | collective-permute-start | bytes 737288 | tf_op jit(solution)/shard_map/ppermute | solution.py:29
  146.4 18.0 %all-to-all-start.1 = ((bf16[16,8,2560]{2,1,0:T(8,128)(2,1)}), bf16[16,8,2560]{2,1,0:T(8,128)(2,1)S(1)}, u32[]{:S(2)}, u32[]{:S(2)}) async-start(bf16[16,8,2560]{2,1,0:T(8,128)(2,1)} %fusion.3), calls=%async_computation.1 | async-start | bytes 1310720 | tf_op jit(solution)/shard_map/all_to_all | solution.py:217
  164.3 22.7 %copy-start = (bf16[1,192,2560]{2,1,0:T(8,128)(2,1)S(1)}, bf16[1,192,2560]{2,1,0:T(8,128)(2,1)}, u32[]{:S(2)}) copy-start(bf16[1,192,2560]{2,1,0:T(8,128)(2,1)} %param.21) | copy-start | bytes 2949124
  164.3 27.3 %copy-start.29 = (s32[1,4]{1,0:T(1,128)S(1)}, s32[1,4]{1,0:T(1,128)}, u32[]{:S(2)}) copy-start(s32[1,4]{1,0:T(1,128)} %param.14) | copy-start | bytes 52
  164.4 27.3 %copy-start.31 = (s32[4,1]{0,1:T(1,128)S(1)}, s32[4,1]{0,1:T(1,128)}, u32[]{:S(2)}) copy-start(s32[4,1]{0,1:T(1,128)} %copy-done.30) | copy-start | bytes 52
  164.4 27.3 %copy-start.25 = (s32[1,4,2]{1,2,0:T(2,128)S(1)}, s32[1,4,2]{1,2,0:T(2,128)}, u32[]{:S(2)}) copy-start(s32[1,4,2]{1,2,0:T(2,128)} %param.15) | copy-start | bytes 100
  164.4 35.2 %all-to-all-start.4 = ((bf16[16,24,2560]{2,1,0:T(8,128)(2,1)}), bf16[16,24,2560]{2,1,0:T(8,128)(2,1)}, u32[]{:S(2)}, u32[]{:S(2)}) async-start(bf16[16,24,2560]{2,1,0:T(8,128)(2,1)} %bitcast.179), calls=%async_computation.4 | async-start | bytes 3932160 | tf_op jit(solution)/shard_map/all_to_all | solution.py:226
  172.6 49.9 %collective-permute-start.15 = (f32[6,64]{1,0:T(8,128)S(1)}, f32[6,64]{1,0:T(8,128)S(1)}, u32[]{:S(2)}, u32[]{:S(2)}) collective-permute-start(f32[6,64]{1,0:T(8,128)S(1)} %bitcast.232), channel_id=1, source_target_pairs={{384,0},{0,128},{128,256},{256,384},{385,1},{1,129},{129,257},{257... | collective-permute-start | bytes 4616 | tf_op jit(solution)/shard_map/ppermute | solution.py:29
  177.1 45.4 %collective-permute-start.14 = (f32[6,64]{1,0:T(8,128)S(1)}, f32[6,64]{1,0:T(8,128)S(1)}, u32[]{:S(2)}, u32[]{:S(2)}) collective-permute-start(f32[6,64]{1,0:T(8,128)S(1)} %bitcast.233), channel_id=1, source_target_pairs={{256,0},{384,128},{0,256},{128,384},{257,1},{385,129},{1,257},{129... | collective-permute-start | bytes 4616 | tf_op jit(solution)/shard_map/ppermute | solution.py:29
  183.8 38.8 %collective-permute-start.13 = (f32[6,64]{1,0:T(8,128)S(1)}, f32[6,64]{1,0:T(8,128)S(1)}, u32[]{:S(2)}, u32[]{:S(2)}) collective-permute-start(f32[6,64]{1,0:T(8,128)S(1)} %bitcast.234), channel_id=1, source_target_pairs={{128,0},{256,128},{384,256},{0,384},{129,1},{257,129},{385,257},{1... | collective-permute-start | bytes 4616 | tf_op jit(solution)/shard_map/ppermute | solution.py:29
  187.1 9.3 %collective-permute-start.9 = (bf16[192,2560]{1,0:T(8,128)(2,1)S(1)}, bf16[192,2560]{1,0:T(8,128)(2,1)S(1)}, u32[]{:S(2)}, u32[]{:S(2)}) collective-permute-start(bf16[192,2560]{1,0:T(8,128)(2,1)S(1)} %bitcast.177), channel_id=1, source_target_pairs={{0,4},{4,0},{1,5},{5,1},{2,6},{6,2},{3,7},{7,3},{8,12},{12,8},{9,1... | collective-permute-start | bytes 2949128 | tf_op jit(solution)/shard_map/ppermute | solution.py:33
  199.6 15.5 %all-to-all-start.2 = ((bf16[16,8,2560]{2,1,0:T(8,128)(2,1)}), bf16[16,8,2560]{2,1,0:T(8,128)(2,1)S(1)}, u32[]{:S(2)}, u32[]{:S(2)}) async-start(bf16[16,8,2560]{2,1,0:T(8,128)(2,1)} %fusion.4), calls=%async_computation.2 | async-start | bytes 1310720 | tf_op jit(solution)/shard_map/all_to_all | solution.py:231
  215.1 33.1 %all-to-all-start.5 = ((bf16[16,24,2560]{2,1,0:T(8,128)(2,1)}), bf16[16,24,2560]{2,1,0:T(8,128)(2,1)S(1)}, u32[]{:S(2)}, u32[]{:S(2)}) async-start(bf16[16,24,2560]{2,1,0:T(8,128)(2,1)} %bitcast.176), calls=%async_computation.5 | async-start | bytes 3932160 | tf_op jit(solution)/shard_map/all_to_all | solution.py:229
  223.9 31.5 %copy-start.19 = (pred[384]{0:T(512)(128)(4,1)S(1)}, pred[384]{0:T(512)(128)(4,1)}, u32[]{:S(2)}) copy-start(pred[384]{0:T(512)(128)(4,1)} %get-tuple-element.57) | copy-start | bytes 1156
  248.2 51.7 %all-to-all-start.3 = ((bf16[4,64,640]{2,1,0:T(8,128)(2,1)}), bf16[4,64,640]{2,1,0:T(8,128)(2,1)S(1)}, u32[]{:S(2)}, u32[]{:S(2)}) async-start(bf16[4,64,640]{2,1,0:T(8,128)(2,1)} %pad_maximum_fusion.7), calls=%async_computation.3 | async-start | bytes 655360 | tf_op jit(solution)/shard_map/all_to_all | solution.py:242
  260.8 9.1 %collective-permute-start.24 = (bf16[192,640]{1,0:T(8,128)(2,1)S(1)}, bf16[192,640]{1,0:T(8,128)(2,1)S(1)}, u32[]{:S(2)}, u32[]{:S(2)}) collective-permute-start(bf16[192,640]{1,0:T(8,128)(2,1)S(1)} %get-tuple-element.6), channel_id=1, source_target_pairs={{3,0},{0,1},{1,2},{2,3},{7,4},{4,5},{5,6},{6,7},{11,8},{8,9},{9,10... | collective-permute-start | bytes 737288 | tf_op jit(solution)/shard_map/ppermute | solution.py:29
  262.8 22.2 %collective-permute-start.23 = (bf16[192,640]{1,0:T(8,128)(2,1)S(1)}, bf16[192,640]{1,0:T(8,128)(2,1)S(1)}, u32[]{:S(2)}, u32[]{:S(2)}) collective-permute-start(bf16[192,640]{1,0:T(8,128)(2,1)S(1)} %get-tuple-element.7), channel_id=1, source_target_pairs={{2,0},{3,1},{0,2},{1,3},{6,4},{7,5},{4,6},{5,7},{10,8},{11,9},{8,1... | collective-permute-start | bytes 737288 | tf_op jit(solution)/shard_map/ppermute | solution.py:29
  266.1 18.9 %collective-permute-start.22 = (bf16[192,640]{1,0:T(8,128)(2,1)S(1)}, bf16[192,640]{1,0:T(8,128)(2,1)S(1)}, u32[]{:S(2)}, u32[]{:S(2)}) collective-permute-start(bf16[192,640]{1,0:T(8,128)(2,1)S(1)} %get-tuple-element.5), channel_id=1, source_target_pairs={{1,0},{2,1},{3,2},{0,3},{5,4},{6,5},{7,6},{4,7},{9,8},{10,9},{11,1... | collective-permute-start | bytes 737288 | tf_op jit(solution)/shard_map/ppermute | solution.py:29
  285.1 14.9 %collective-permute-start.27 = (bf16[64,640]{1,0:T(8,128)(2,1)S(1)}, bf16[64,640]{1,0:T(8,128)(2,1)S(1)}, u32[]{:S(2)}, u32[]{:S(2)}) collective-permute-start(bf16[64,640]{1,0:T(8,128)(2,1)S(1)} %get-tuple-element.29), channel_id=1, source_target_pairs={{128,0},{256,128},{384,256},{0,384},{129,1},{257,129},{385,257},{1... | collective-permute-start | bytes 245768 | tf_op jit(solution)/shard_map/ppermute | solution.py:29
  289.4 14.2 %collective-permute-start.26 = (bf16[64,640]{1,0:T(8,128)(2,1)S(1)}, bf16[64,640]{1,0:T(8,128)(2,1)S(1)}, u32[]{:S(2)}, u32[]{:S(2)}) collective-permute-start(bf16[64,640]{1,0:T(8,128)(2,1)S(1)} %get-tuple-element.30), channel_id=1, source_target_pairs={{256,0},{384,128},{0,256},{128,384},{257,1},{385,129},{1,257},{129... | collective-permute-start | bytes 245768 | tf_op jit(solution)/shard_map/ppermute | solution.py:29
  296.7 16.7 %collective-permute-start.25 = (bf16[64,640]{1,0:T(8,128)(2,1)S(1)}, bf16[64,640]{1,0:T(8,128)(2,1)S(1)}, u32[]{:S(2)}, u32[]{:S(2)}) collective-permute-start(bf16[64,640]{1,0:T(8,128)(2,1)S(1)} %get-tuple-element.28), channel_id=1, source_target_pairs={{384,0},{0,128},{128,256},{256,384},{385,1},{1,129},{129,257},{257... | collective-permute-start | bytes 245768 | tf_op jit(solution)/shard_map/ppermute | solution.py:29
  (23 other events, 229.6 us)

commit v2 on v1

v2 whole, which is shorter than its diff:
```python
import jax
import jax.numpy as jnp
from jax import lax
from jax.sharding import Mesh, PartitionSpec as P

HEAD_DIM = 128
PAGE = 16
SLOTS = 8
epsilon = 1e-05

AXES = ("zh", "y", "x", "c", "tp")
REQ = ("zh", "y", "x", "c")
PLANE = ("y", "x")
LINE = ("zh", "tp")
F32 = jnp.float32
BF16 = jnp.bfloat16
I32 = jnp.int32


def dot(a, b, dims):
    return lax.dot_general(a, b, (dims, ((), ())), preferred_element_type=F32)


def iota(shape, dim):
    return lax.broadcasted_iota(I32, shape, dim)


def swapped(value, axis, size, mate):
    return lax.ppermute(value, axis, [(i, mate(i)) for i in range(size)])


def swap_cores(value):
    return swapped(value, "c", 2, lambda i: 1 - i)


def swap_units(value):
    return swapped(value, "tp", 4, lambda i: i ^ 1)


def swap_groups(value):
    return swapped(value, "tp", 4, lambda i: 3 - i)


def turned(value):
    return swapped(value, LINE, 16, lambda i: i % 4 * 4 + i // 4)


def spread_to_all(value, axis, size):
    copies = jnp.broadcast_to(value[None], (size,) + value.shape)
    return lax.all_to_all(copies, axis, 0, 0, tiled=True)


def attend(queries, key_values, segment_row, segment_col):
    count = queries.shape[0]
    heads = queries.shape[1] // HEAD_DIM
    keys, values = key_values[:, :HEAD_DIM], key_values[:, HEAD_DIM:]
    stacked = jnp.concatenate(
        [queries[:, h * HEAD_DIM : (h + 1) * HEAD_DIM] for h in range(heads)], axis=0
    )
    scores = dot(stacked, keys, ((1,), (1,))) * HEAD_DIM ** (-0.5)
    scores = scores.reshape(heads, count, count)
    allowed = (segment_col == segment_row) & (iota((count, count), 1) <= iota((count, count), 0))
    scores = jnp.where(allowed[None], scores, -1e30)
    highest = jnp.max(scores, axis=-1, keepdims=True)
    weights = jnp.exp(scores - highest)
    probs = (weights / jnp.sum(weights, axis=-1, keepdims=True)).astype(BF16)
    context = dot(probs.reshape(heads * count, count), values, ((1,), (0,))).astype(BF16)
    return jnp.concatenate(
        [context[h * count : (h + 1) * count] for h in range(heads)], axis=1
    )


def packed_routing(choice, weight):
    high = lax.reduce_precision(weight, 8, 7)
    packed = jnp.concatenate([choice.astype(F32), high, weight - high], axis=1)
    return jnp.pad(packed, ((0, 0), (0, 128 - packed.shape[1]))).astype(BF16)


def routing(packed, top, first, own_experts):
    tokens = packed.shape[0]
    local = packed[:, :top].astype(F32) - first.astype(F32)
    high, low = (packed[:, top * i : top * (i + 1)].astype(F32) for i in (1, 2))
    rows = own_experts * SLOTS
    expert = (iota((tokens, rows), 1) // SLOTS).astype(F32)
    slot = (iota((tokens, rows), 1) % SLOTS).astype(F32)
    named = jnp.zeros((tokens, rows), F32)
    highs = jnp.zeros((tokens, rows), F32)
    lows = jnp.zeros((tokens, rows), F32)
    for k in range(top):
        hit = local[:, k : k + 1] == expert
        named = jnp.where(hit, 1.0, named)
        highs = jnp.where(hit, high[:, k : k + 1], highs)
        lows = jnp.where(hit, low[:, k : k + 1], lows)
    earlier = (iota((tokens, tokens), 1) < iota((tokens, tokens), 0)).astype(BF16)
    ranks = dot(earlier, named.astype(BF16), ((1,), (0,)))
    taken = (named > 0.5) & (ranks == slot)
    parts = [jnp.where(taken, part, 0.0).astype(BF16) for part in (highs, lows)]
    return taken.astype(BF16), parts


def normalize(mid, gain):
    wide = mid.astype(F32)
    square = jnp.mean(wide * wide, axis=1, keepdims=True)
    return (wide * lax.rsqrt(square + epsilon) * gain).astype(BF16)


def experts_of(rows, weights):
    total = None
    for gate_up, down in weights:
        units = down.shape[0]
        projected = dot(rows, gate_up, ((1,), (0,)))
        activated = (jax.nn.silu(projected[:, :units]) * projected[:, units:]).astype(BF16)
        part = dot(activated, down, ((1,), (0,)))
        total = part if total is None else total + part
    return total.astype(BF16)


def combined(returned, parts):
    high, low = parts
    return dot(high, returned, ((1,), (0,))) + dot(low, returned, ((1,), (0,)))


def on_device(
    queries,
    key_values,
    hidden,
    lengths,
    page_table,
    out_weight,
    norm_gain,
    expert_choice,
    route_weight,
    gate_up,
    down,
):
    count = queries.shape[0]
    width = hidden.shape[1]
    n_zh, n_tp = lax.axis_size("zh"), lax.axis_size("tp")
    planes = lax.axis_size("y") * lax.axis_size("x")
    zh, tp = lax.axis_index("zh"), lax.axis_index("tp")
    share = width // n_tp
    top = expert_choice.shape[1]
    gate_up_own, down_own = gate_up[0], down[0]

    projection = spread_to_all(out_weight.T, ("y", "x", "c"), 2 * planes)
    projection = projection.reshape(share, out_weight.shape[0])

    row = lengths[0]
    places = jnp.arange(count, dtype=I32)
    ends = jnp.cumsum(row)
    starts = ends - row
    segment = jnp.sum((ends[None, :] <= places[:, None]).astype(I32), axis=1)
    picked = segment[:, None] == jnp.arange(row.shape[0], dtype=I32)[None, :]
    offset = places - jnp.sum(jnp.where(picked, starts[None, :], 0), axis=1)

    context = attend(queries, key_values, segment[None, :], segment[:, None])
    contexts = spread_to_all(context, "zh", n_zh)

    hidden_own = turned(lax.dynamic_slice_in_dim(hidden, tp * share, share, 1))
    near_packed = turned(packed_routing(expert_choice, route_weight))
    far_packed = swap_groups(near_packed)

    weights = [(gate_up_own, down_own)]
    weights.append((swap_units(gate_up_own), swap_units(down_own)))
    weights.append((swap_cores(gate_up_own), swap_cores(down_own)))
    weights.append((swap_cores(weights[1][0]), swap_cores(weights[1][1])))

    partial = dot(contexts.reshape(n_zh * count, -1), projection, ((1,), (1,))).astype(BF16)
    partial = lax.all_to_all(
        partial.reshape(n_zh, count, share), "tp", 0, 0, tiled=True
    )
    attn = jnp.sum(partial.astype(F32), axis=0)
    mid_own = (hidden_own.astype(F32) + attn).astype(BF16)
    mid_own = lax.optimization_barrier(mid_own)

    blocks = spread_to_all(mid_own, "zh", n_zh)
    near = jnp.concatenate([blocks[i] for i in range(n_zh)], axis=1)
    far = swap_groups(near)
    first = zh * planes

    def sent(mid, packed):
        selector, parts = routing(packed, top, first, planes)
        rows = dot(selector, normalize(mid, norm_gain), ((0,), (0,))).astype(BF16)
        rows = rows.reshape(planes, SLOTS, width)
        return lax.all_to_all(rows, PLANE, 0, 0, tiled=True), parts

    near_in, near_parts = sent(near, near_packed)
    far_in, far_parts = sent(far, far_packed)
    near_out = experts_of(near_in.reshape(-1, width), weights).reshape(near_in.shape)
    far_out = experts_of(far_in.reshape(-1, width), weights).reshape(far_in.shape)
    far_back = lax.all_to_all(far_out, PLANE, 0, 0, tiled=True)
    far_back, near_out = lax.optimization_barrier((far_back, near_out))
    near_back = lax.all_to_all(near_out, PLANE, 0, 0, tiled=True)

    far_moe = combined(far_back.reshape(-1, width), far_parts).astype(BF16)
    near_moe = combined(near_back.reshape(-1, width), near_parts)
    near_moe = (near_moe + swap_groups(far_moe).astype(F32)).astype(BF16)
    columns = jnp.stack([near_moe[:, i * share : (i + 1) * share] for i in range(n_zh)])
    gathered = lax.all_to_all(columns, "zh", 0, 0, tiled=True)
    moe = jnp.sum(gathered.astype(F32), axis=0)
    layer_out = turned((mid_own.astype(F32) + moe).astype(BF16))

    pages = page_table[0]
    flat_pages = pages.reshape(-1)
    pool = flat_pages.shape[0]
    page_of = segment * pages.shape[1] + offset // PAGE
    slot_page = jnp.sum(
        jnp.where(
            page_of[:, None] == jnp.arange(pool, dtype=I32)[None, :], flat_pages[None, :], 0
        ),
        axis=1,
    )
    cache_rows = slot_page * PAGE + offset % PAGE
    put = (iota((pool * PAGE, count), 0) == cache_rows[None, :]).astype(BF16)
    cache = dot(put, key_values, ((1,), (0,))).astype(BF16)
    return (layer_out, cache.reshape(pool, PAGE, key_values.shape[1]))


def solution(mesh):
    grid = Mesh(mesh.devices.reshape(4, 4, 4, 2, 4), AXES)
    placed = (
        P(REQ, "tp"),
        P(REQ, "tp"),
        P(REQ, None),
        P(REQ, None),
        P(REQ, None, None),
        P("tp", REQ),
        P(),
        P(REQ, None),
        P(REQ, None),
        P(REQ, None, "tp"),
        P(REQ, "tp", None),
    )
    return jax.shard_map(
        on_device,
        mesh=grid,
        in_specs=placed,
        out_specs=(P(REQ, "tp"), P(REQ, None, "tp")),
        check_vma=False,
    )
```

time: 316 us -> 298 us (0.943)
  the two profiles are of different devices: /device:TPU:109 before, /device:TPU:84 now
where the time goes in v2:
time: 298 us; the launch traced here: 296 us
  starting transfers between devices  126 us (42%)
  waiting for transfers between devices  125 us (42%)
  matrix products  37.7 us (13%)
  local copies, waits for them, and re-layouts  4.7 us (2%)
    ppermute x12, waiting for transfers between devices, swapped(): return lax.ppermute(value, axis, [(i, mate(i)) for i in range(size)])  73 us
    ppermute x12, starting transfers between devices, swapped(): return lax.ppermute(value, axis, [(i, mate(i)) for i in range(size)])  48.3 us
    dot_general x28, matrix products, dot(): return lax.dot_general(a, b, (dims, ((), ())), preferred_element_type=F32)  37.7 us
    all_to_all x3, waiting for transfers between devices, spread_to_all(): return lax.all_to_all(copies, axis, 0, 0, tiled=True)  30.4 us
    all_to_all x3, starting transfers between devices, spread_to_all(): return lax.all_to_all(copies, axis, 0, 0, tiled=True)  28.5 us
    all_to_all x1, waiting for transfers between devices, on_device(): gathered = lax.all_to_all(columns, 'zh', 0, 0, tiled=True)  17.5 us
    all_to_all x2, starting transfers between devices, sent(): return (lax.all_to_all(rows, PLANE, 0, 0, tiled=True), parts)  16.4 us
    all_to_all x1, starting transfers between devices, on_device(): gathered = lax.all_to_all(columns, 'zh', 0, 0, tiled=True)  13.7 us
  transfers between devices with their start and end apart: 21, of which 12 were waited for; matrix products, arithmetic and copies ran while one was open for 13% of the time, Pallas kernels for 0%

profile of v2, /device:TPU:84, one launch (start us, length us, event | category | flops | bytes accessed | tf_op | source)
XLA Modules:
  0.0 296.3 jit_solution(4557177195064752805)
XLA Ops:
  0.7 1.8 broadcast_in_dim.272
  2.5 7.5 %all-to-all-start.1 = ((bf16[32,20,640]{2,1,0:T(8,128)(2,1)}), bf16[32,20,640]{2,1,0:T(8,128)(2,1)S(1)}, u32[]{:S(2)}, u32[]{:S(2)}) async-start(bf16[32,20,640]{2,1,0:T(8,128)(2,1)} %broadcast_in_dim.272), calls=%async_computation.1 | async-start | bytes 1966080 | tf_op jit(solution)/shard_map/all_to_all | solution.py:50
  11.1 11.3 %all-to-all-done.1 = bf16[32,20,640]{2,1,0:T(8,128)(2,1)S(1)} async-done(((bf16[32,20,640]{2,1,0:T(8,128)(2,1)}), bf16[32,20,640]{2,1,0:T(8,128)(2,1)S(1)}, u32[]{:S(2)}, u32[]{:S(2)}) %all-to-all-start.1) | async-done | bytes 819232 | tf_op jit(solution)/shard_map/all_to_all | solution.py:50
  23.2 13.3 %all-to-all-start = ((bf16[4,64,640]{2,1,0:T(8,128)(2,1)}), bf16[4,64,640]{2,1,0:T(8,128)(2,1)S(1)}, u32[]{:S(2)}, u32[]{:S(2)}) async-start(bf16[4,64,640]{2,1,0:T(8,128)(2,1)} %broadcast_in_dim.271), calls=%async_computation | async-start | bytes 655360 | tf_op jit(solution)/shard_map/all_to_all | solution.py:50
  36.5 2.9 collective-permute-start.5
  39.4 1.9 collective-permute-start.7
  41.4 2.9 collective-permute-start.4
  44.3 2.1 collective-permute-start.6
  46.5 11.7 %collective-permute-start.1 = (bf16[64,128]{0,1:T(8,128)(2,1)S(1)}, bf16[64,128]{0,1:T(8,128)(2,1)S(1)}, u32[]{:S(2)}, u32[]{:S(2)}) collective-permute-start(bf16[64,128]{0,1:T(8,128)(2,1)S(1)} %fusion.77), channel_id=1, source_target_pairs={{0,0},{1,128},{2,256},{3,384},{128,1},{129,129},{130,257},{131,385... | collective-permute-start | bytes 49160 | tf_op jit(solution)/shard_map/ppermute | solution.py:29
  58.5 3.2 %all-to-all-done = bf16[4,64,640]{2,1,0:T(8,128)(2,1)S(1)} async-done(((bf16[4,64,640]{2,1,0:T(8,128)(2,1)}), bf16[4,64,640]{2,1,0:T(8,128)(2,1)S(1)}, u32[]{:S(2)}, u32[]{:S(2)}) %all-to-all-start) | async-done | bytes 327712 | tf_op jit(solution)/shard_map/all_to_all | solution.py:50
  62.9 4.6 %all-to-all-start.2 = ((bf16[4,64,640]{2,1,0:T(8,128)(2,1)}), bf16[4,64,640]{2,1,0:T(8,128)(2,1)S(1)}, u32[]{:S(2)}, u32[]{:S(2)}) async-start(bf16[4,64,640]{2,1,0:T(8,128)(2,1)} %bitcast.5), calls=%async_computation.2 | async-start | bytes 655360 | tf_op jit(solution)/shard_map/all_to_all | solution.py:169
  67.4 54.1 %collective-permute-done.1 = bf16[64,128]{0,1:T(8,128)(2,1)S(1)} collective-permute-done((bf16[64,128]{0,1:T(8,128)(2,1)S(1)}, bf16[64,128]{0,1:T(8,128)(2,1)S(1)}, u32[]{:S(2)}, u32[]{:S(2)}) %collective-permute-start.1) | collective-permute-done | bytes 16416 | tf_op jit(solution)/shard_map/ppermute | solution.py:29
  121.5 11.3 %collective-permute-start = (bf16[64,640]{1,0:T(8,128)(2,1)S(1)}, bf16[64,640]{1,0:T(8,128)(2,1)S(1)}, u32[]{:S(2)}, u32[]{:S(2)}) collective-permute-start(bf16[64,640]{1,0:T(8,128)(2,1)S(1)} %constant_dynamic-slice_fusion), channel_id=1, source_target_pairs={{0,0},{1,128},{2,256},{3,384},{128,1},{129,129},{130,257},{131,385... | collective-permute-start | bytes 245768 | tf_op jit(solution)/shard_map/ppermute | solution.py:29
  133.2 2.5 collective-permute-done
  135.7 1.9 collective-permute-start.2
  138.3 7.7 %all-to-all-start.3 = ((bf16[4,64,640]{2,1,0:T(8,128)(2,1)}), bf16[4,64,640]{2,1,0:T(8,128)(2,1)S(1)}, u32[]{:S(2)}, u32[]{:S(2)}) async-start(bf16[4,64,640]{2,1,0:T(8,128)(2,1)} %broadcast_in_dim.286), calls=%async_computation.3 | async-start | bytes 655360 | tf_op jit(solution)/shard_map/all_to_all | solution.py:50
  146.4 15.9 %all-to-all-done.3 = bf16[4,64,640]{2,1,0:T(8,128)(2,1)S(1)} async-done(((bf16[4,64,640]{2,1,0:T(8,128)(2,1)}), bf16[4,64,640]{2,1,0:T(8,128)(2,1)S(1)}, u32[]{:S(2)}, u32[]{:S(2)}) %all-to-all-start.3) | async-done | bytes 327712 | tf_op jit(solution)/shard_map/all_to_all | solution.py:50
  162.5 2.7 collective-permute-start.3
  165.1 1.3 fusion.3
  166.4 8.4 %all-to-all-start.6 = ((bf16[16,8,2560]{2,1,0:T(8,128)(2,1)}), bf16[16,8,2560]{2,1,0:T(8,128)(2,1)S(1)}, u32[]{:S(2)}, u32[]{:S(2)}) async-start(bf16[16,8,2560]{2,1,0:T(8,128)(2,1)} %fusion.3), calls=%async_computation.6 | async-start | bytes 1310720 | tf_op jit(solution)/shard_map/all_to_all | solution.py:185
  174.8 1.9 collective-permute-start.9
  176.7 2.4 collective-permute-start.8
  181.6 8.0 %all-to-all-start.4 = ((bf16[16,8,2560]{2,1,0:T(8,128)(2,1)}), bf16[16,8,2560]{2,1,0:T(8,128)(2,1)S(1)}, u32[]{:S(2)}, u32[]{:S(2)}) async-start(bf16[16,8,2560]{2,1,0:T(8,128)(2,1)} %fusion.2), calls=%async_computation.4 | async-start | bytes 1310720 | tf_op jit(solution)/shard_map/all_to_all | solution.py:185
  189.6 2.1 fusion.28
  191.7 2.1 fusion.26
  193.8 1.6 fusion.58
  195.3 1.6 convolution_add_fusion.2
  196.9 2.1 fusion.24
  199.0 2.1 fusion.36
  201.1 2.1 fusion.34
  203.1 2.1 fusion.32
  205.2 1.6 fusion.53
  206.8 1.6 convolution_add_fusion.5
  208.4 1.6 convolution_add_fusion.4
  210.0 2.1 fusion.30
  212.1 2.4 fusion.5
  214.5 7.2 %all-to-all-start.5 = ((bf16[16,8,2560]{2,1,0:T(8,128)(2,1)}), bf16[16,8,2560]{2,1,0:T(8,128)(2,1)S(1)}, u32[]{:S(2)}, u32[]{:S(2)}) async-start(bf16[16,8,2560]{2,1,0:T(8,128)(2,1)} %fusion.5), calls=%async_computation.5 | async-start | bytes 1310720 | tf_op jit(solution)/shard_map/all_to_all | solution.py:191
  221.7 1.6 convolution_add_fusion.1
  223.3 2.1 fusion.22
  225.4 2.4 fusion.4
  228.6 7.5 %all-to-all-start.7 = ((bf16[16,8,2560]{2,1,0:T(8,128)(2,1)}), bf16[16,8,2560]{2,1,0:T(8,128)(2,1)S(1)}, u32[]{:S(2)}, u32[]{:S(2)}) async-start(bf16[16,8,2560]{2,1,0:T(8,128)(2,1)} %fusion.4), calls=%async_computation.7 | async-start | bytes 1310720 | tf_op jit(solution)/shard_map/all_to_all | solution.py:193
  236.8 3.8 %collective-permute-start.10 = (bf16[64,2560]{1,0:T(8,128)(2,1)S(1)}, bf16[64,2560]{1,0:T(8,128)(2,1)S(1)}, u32[]{:S(2)}, u32[]{:S(2)}) collective-permute-start(bf16[64,2560]{1,0:T(8,128)(2,1)S(1)} %fusion.6), channel_id=1, source_target_pairs={{0,3},{1,2},{2,1},{3,0},{4,7},{5,6},{6,5},{7,4},{8,11},{9,10},{10,... | collective-permute-start | bytes 983048 | tf_op jit(solution)/shard_map/ppermute | solution.py:29
  240.6 2.3 all-to-all-done.7
  243.3 5.4 %collective-permute-done.10 = bf16[64,2560]{1,0:T(8,128)(2,1)S(1)} collective-permute-done((bf16[64,2560]{1,0:T(8,128)(2,1)S(1)}, bf16[64,2560]{1,0:T(8,128)(2,1)S(1)}, u32[]{:S(2)}, u32[]{:S(2)}) %collective-permute-start.10) | collective-permute-done | bytes 327712 | tf_op jit(solution)/shard_map/ppermute | solution.py:29
  249.9 13.7 %all-to-all-start.8 = ((bf16[4,64,640]{2,1,0:T(8,128)(2,1)}), bf16[4,64,640]{2,1,0:T(8,128)(2,1)S(1)}, u32[]{:S(2)}, u32[]{:S(2)}) async-start(bf16[4,64,640]{2,1,0:T(8,128)(2,1)} %pad_maximum_fusion.1), calls=%async_computation.8 | async-start | bytes 655360 | tf_op jit(solution)/shard_map/all_to_all | solution.py:199
  264.0 17.5 %all-to-all-done.8 = bf16[4,64,640]{2,1,0:T(8,128)(2,1)S(1)} async-done(((bf16[4,64,640]{2,1,0:T(8,128)(2,1)}), bf16[4,64,640]{2,1,0:T(8,128)(2,1)S(1)}, u32[]{:S(2)}, u32[]{:S(2)}) %all-to-all-start.8) | async-done | bytes 327712 | tf_op jit(solution)/shard_map/all_to_all | solution.py:199
  281.6 2.7 collective-permute-start.11
  285.0 10.7 %collective-permute-done.11 = bf16[64,640]{1,0:T(8,128)(2,1)S(1)} collective-permute-done((bf16[64,640]{1,0:T(8,128)(2,1)S(1)}, bf16[64,640]{1,0:T(8,128)(2,1)S(1)}, u32[]{:S(2)}, u32[]{:S(2)}) %collective-permute-start.11) | collective-permute-done | bytes 81952 | tf_op jit(solution)/shard_map/ppermute | solution.py:29
  (93 shorter events, 12.2 us)
Async XLA Ops:
  0.6 57.6 %copy-start = (bf16[64,2560]{1,0:T(8,128)(2,1)S(1)}, bf16[64,2560]{1,0:T(8,128)(2,1)}, u32[]{:S(2)}) copy-start(bf16[64,2560]{1,0:T(8,128)(2,1)} %param.13) | copy-start | bytes 983044
  0.6 9.4 %copy-start.7 = (s32[1,4]{1,0:T(1,128)S(1)}, s32[1,4]{1,0:T(1,128)}, u32[]{:S(2)}) copy-start(s32[1,4]{1,0:T(1,128)} %param.14) | copy-start | bytes 52
  0.7 9.9 %copy-start.1 = (bf16[64,640]{1,0:T(8,128)(2,1)S(1)}, bf16[64,640]{1,0:T(8,128)(2,1)}, u32[]{:S(2)}) copy-start(bf16[64,640]{1,0:T(8,128)(2,1)} %param.11) | copy-start | bytes 245764
  0.7 9.9 %copy-start.2 = (bf16[64,256]{1,0:T(8,128)(2,1)S(1)}, bf16[64,256]{1,0:T(8,128)(2,1)}, u32[]{:S(2)}) copy-start(bf16[64,256]{1,0:T(8,128)(2,1)} %param.12) | copy-start | bytes 98308
  2.5 43.9 %copy-start.4 = (s32[64,6]{0,1:T(8,128)S(1)}, s32[64,6]{0,1:T(8,128)}, u32[]{:S(2)}) copy-start(s32[64,6]{0,1:T(8,128)} %param.18) | copy-start | bytes 4612
  2.5 43.9 %copy-start.5 = (f32[64,6]{0,1:T(8,128)S(1)}, f32[64,6]{0,1:T(8,128)}, u32[]{:S(2)}) copy-start(f32[64,6]{0,1:T(8,128)} %param.19) | copy-start | bytes 4612
  2.5 20.0 %all-to-all-start.1 = ((bf16[32,20,640]{2,1,0:T(8,128)(2,1)}), bf16[32,20,640]{2,1,0:T(8,128)(2,1)S(1)}, u32[]{:S(2)}, u32[]{:S(2)}) async-start(bf16[32,20,640]{2,1,0:T(8,128)(2,1)} %broadcast_in_dim.272), calls=%async_computation.1 | async-start | bytes 1966080 | tf_op jit(solution)/shard_map/all_to_all | solution.py:50
  23.2 38.5 %all-to-all-start = ((bf16[4,64,640]{2,1,0:T(8,128)(2,1)}), bf16[4,64,640]{2,1,0:T(8,128)(2,1)S(1)}, u32[]{:S(2)}, u32[]{:S(2)}) async-start(bf16[4,64,640]{2,1,0:T(8,128)(2,1)} %broadcast_in_dim.271), calls=%async_computation | async-start | bytes 655360 | tf_op jit(solution)/shard_map/all_to_all | solution.py:50
  36.5 138.3 %collective-permute-start.5 = (bf16[192,2560]{1,0:T(8,128)(2,1)}, bf16[192,2560]{1,0:T(8,128)(2,1)}, u32[]{:S(2)}, u32[]{:S(2)}) collective-permute-start(bf16[192,2560]{1,0:T(8,128)(2,1)} %bitcast.31), channel_id=1, source_target_pairs={{0,1},{1,0},{2,3},{3,2},{4,5},{5,4},{6,7},{7,6},{8,9},{9,8},{10,11... | collective-permute-start | bytes 2949128 | tf_op jit(solution)/shard_map/ppermute | solution.py:29
  39.4 169.0 %collective-permute-start.7 = (bf16[192,2560]{1,0:T(8,128)(2,1)}, bf16[192,2560]{1,0:T(8,128)(2,1)}, u32[]{:S(2)}, u32[]{:S(2)}) collective-permute-start(bf16[192,2560]{1,0:T(8,128)(2,1)} %bitcast.31), channel_id=1, source_target_pairs={{0,4},{4,0},{1,5},{5,1},{2,6},{6,2},{3,7},{7,3},{8,12},{12,8},{9,1... | collective-permute-start | bytes 2949128 | tf_op jit(solution)/shard_map/ppermute | solution.py:29
  41.4 135.3 %collective-permute-start.4 = (bf16[2560,384]{1,0:T(8,128)(2,1)}, bf16[2560,384]{1,0:T(8,128)(2,1)}, u32[]{:S(2)}, u32[]{:S(2)}) collective-permute-start(bf16[2560,384]{1,0:T(8,128)(2,1)} %bitcast.30), channel_id=1, source_target_pairs={{0,1},{1,0},{2,3},{3,2},{4,5},{5,4},{6,7},{7,6},{8,9},{9,8},{10,11... | collective-permute-start | bytes 5898248 | tf_op jit(solution)/shard_map/ppermute | solution.py:29
  44.3 152.7 %collective-permute-start.6 = (bf16[2560,384]{1,0:T(8,128)(2,1)}, bf16[2560,384]{1,0:T(8,128)(2,1)}, u32[]{:S(2)}, u32[]{:S(2)}) collective-permute-start(bf16[2560,384]{1,0:T(8,128)(2,1)} %bitcast.30), channel_id=1, source_target_pairs={{0,4},{4,0},{1,5},{5,1},{2,6},{6,2},{3,7},{7,3},{8,12},{12,8},{9,1... | collective-permute-start | bytes 5898248 | tf_op jit(solution)/shard_map/ppermute | solution.py:29
  46.5 75.0 %collective-permute-start.1 = (bf16[64,128]{0,1:T(8,128)(2,1)S(1)}, bf16[64,128]{0,1:T(8,128)(2,1)S(1)}, u32[]{:S(2)}, u32[]{:S(2)}) collective-permute-start(bf16[64,128]{0,1:T(8,128)(2,1)S(1)} %fusion.77), channel_id=1, source_target_pairs={{0,0},{1,128},{2,256},{3,384},{128,1},{129,129},{130,257},{131,385... | collective-permute-start | bytes 49160 | tf_op jit(solution)/shard_map/ppermute | solution.py:29
  62.9 70.2 %all-to-all-start.2 = ((bf16[4,64,640]{2,1,0:T(8,128)(2,1)}), bf16[4,64,640]{2,1,0:T(8,128)(2,1)S(1)}, u32[]{:S(2)}, u32[]{:S(2)}) async-start(bf16[4,64,640]{2,1,0:T(8,128)(2,1)} %bitcast.5), calls=%async_computation.2 | async-start | bytes 655360 | tf_op jit(solution)/shard_map/all_to_all | solution.py:169
  121.5 14.1 %collective-permute-start = (bf16[64,640]{1,0:T(8,128)(2,1)S(1)}, bf16[64,640]{1,0:T(8,128)(2,1)S(1)}, u32[]{:S(2)}, u32[]{:S(2)}) collective-permute-start(bf16[64,640]{1,0:T(8,128)(2,1)S(1)} %constant_dynamic-slice_fusion), channel_id=1, source_target_pairs={{0,0},{1,128},{2,256},{3,384},{128,1},{129,129},{130,257},{131,385... | collective-permute-start | bytes 245768 | tf_op jit(solution)/shard_map/ppermute | solution.py:29
  133.1 32.0 %copy-start.3 = (f32[2560]{0:T(1024)S(1)}, f32[2560]{0:T(1024)}, u32[]{:S(2)}) copy-start(f32[2560]{0:T(1024)} %param.17) | copy-start | bytes 30724
  135.7 10.4 %collective-permute-start.2 = (bf16[64,128]{0,1:T(8,128)(2,1)S(1)}, bf16[64,128]{0,1:T(8,128)(2,1)S(1)}, u32[]{:S(2)}, u32[]{:S(2)}) collective-permute-start(bf16[64,128]{0,1:T(8,128)(2,1)S(1)} %collective-permute-done.1), channel_id=1, source_target_pairs={{0,3},{1,2},{2,1},{3,0},{4,7},{5,6},{6,5},{7,4},{8,11},{9,10},{10,... | collective-permute-start | bytes 49160 | tf_op jit(solution)/shard_map/ppermute | solution.py:29
  138.3 23.9 %all-to-all-start.3 = ((bf16[4,64,640]{2,1,0:T(8,128)(2,1)}), bf16[4,64,640]{2,1,0:T(8,128)(2,1)S(1)}, u32[]{:S(2)}, u32[]{:S(2)}) async-start(bf16[4,64,640]{2,1,0:T(8,128)(2,1)} %broadcast_in_dim.286), calls=%async_computation.3 | async-start | bytes 655360 | tf_op jit(solution)/shard_map/all_to_all | solution.py:50
  162.5 17.0 %collective-permute-start.3 = (bf16[64,2560]{1,0:T(8,128)(2,1)S(1)}, bf16[64,2560]{1,0:T(8,128)(2,1)S(1)}, u32[]{:S(2)}, u32[]{:S(2)}) collective-permute-start(bf16[64,2560]{1,0:T(8,128)(2,1)S(1)} %get-tuple-element.7), channel_id=1, source_target_pairs={{0,3},{1,2},{2,1},{3,0},{4,7},{5,6},{6,5},{7,4},{8,11},{9,10},{10,... | collective-permute-start | bytes 983048 | tf_op jit(solution)/shard_map/ppermute | solution.py:29
  166.4 15.2 %all-to-all-start.6 = ((bf16[16,8,2560]{2,1,0:T(8,128)(2,1)}), bf16[16,8,2560]{2,1,0:T(8,128)(2,1)S(1)}, u32[]{:S(2)}, u32[]{:S(2)}) async-start(bf16[16,8,2560]{2,1,0:T(8,128)(2,1)} %fusion.3), calls=%async_computation.6 | async-start | bytes 1310720 | tf_op jit(solution)/shard_map/all_to_all | solution.py:185
  174.8 37.3 %collective-permute-start.9 = (bf16[192,2560]{1,0:T(8,128)(2,1)}, bf16[192,2560]{1,0:T(8,128)(2,1)}, u32[]{:S(2)}, u32[]{:S(2)}) collective-permute-start(bf16[192,2560]{1,0:T(8,128)(2,1)} %collective-permute-done.5), channel_id=1, source_target_pairs={{0,4},{4,0},{1,5},{5,1},{2,6},{6,2},{3,7},{7,3},{8,12},{12,8},{9,1... | collective-permute-start | bytes 2949128 | tf_op jit(solution)/shard_map/ppermute | solution.py:29
  176.7 33.3 %collective-permute-start.8 = (bf16[2560,384]{1,0:T(8,128)(2,1)}, bf16[2560,384]{1,0:T(8,128)(2,1)}, u32[]{:S(2)}, u32[]{:S(2)}) collective-permute-start(bf16[2560,384]{1,0:T(8,128)(2,1)} %collective-permute-done.4), channel_id=1, source_target_pairs={{0,4},{4,0},{1,5},{5,1},{2,6},{6,2},{3,7},{7,3},{8,12},{12,8},{9,1... | collective-permute-start | bytes 5898248 | tf_op jit(solution)/shard_map/ppermute | solution.py:29
  181.6 17.4 %all-to-all-start.4 = ((bf16[16,8,2560]{2,1,0:T(8,128)(2,1)}), bf16[16,8,2560]{2,1,0:T(8,128)(2,1)S(1)}, u32[]{:S(2)}, u32[]{:S(2)}) async-start(bf16[16,8,2560]{2,1,0:T(8,128)(2,1)} %fusion.2), calls=%async_computation.4 | async-start | bytes 1310720 | tf_op jit(solution)/shard_map/all_to_all | solution.py:185
  214.5 14.1 %all-to-all-start.5 = ((bf16[16,8,2560]{2,1,0:T(8,128)(2,1)}), bf16[16,8,2560]{2,1,0:T(8,128)(2,1)S(1)}, u32[]{:S(2)}, u32[]{:S(2)}) async-start(bf16[16,8,2560]{2,1,0:T(8,128)(2,1)} %fusion.5), calls=%async_computation.5 | async-start | bytes 1310720 | tf_op jit(solution)/shard_map/all_to_all | solution.py:191
  228.6 14.3 %all-to-all-start.7 = ((bf16[16,8,2560]{2,1,0:T(8,128)(2,1)}), bf16[16,8,2560]{2,1,0:T(8,128)(2,1)S(1)}, u32[]{:S(2)}, u32[]{:S(2)}) async-start(bf16[16,8,2560]{2,1,0:T(8,128)(2,1)} %fusion.4), calls=%async_computation.7 | async-start | bytes 1310720 | tf_op jit(solution)/shard_map/all_to_all | solution.py:193
  236.8 11.9 %collective-permute-start.10 = (bf16[64,2560]{1,0:T(8,128)(2,1)S(1)}, bf16[64,2560]{1,0:T(8,128)(2,1)S(1)}, u32[]{:S(2)}, u32[]{:S(2)}) collective-permute-start(bf16[64,2560]{1,0:T(8,128)(2,1)S(1)} %fusion.6), channel_id=1, source_target_pairs={{0,3},{1,2},{2,1},{3,0},{4,7},{5,6},{6,5},{7,4},{8,11},{9,10},{10,... | collective-permute-start | bytes 983048 | tf_op jit(solution)/shard_map/ppermute | solution.py:29
  248.7 14.9 %copy-start.6 = (s32[1,4,2]{1,2,0:T(2,128)S(1)}, s32[1,4,2]{1,2,0:T(2,128)}, u32[]{:S(2)}) copy-start(s32[1,4,2]{1,2,0:T(2,128)} %param.15) | copy-start | bytes 100
  249.9 31.6 %all-to-all-start.8 = ((bf16[4,64,640]{2,1,0:T(8,128)(2,1)}), bf16[4,64,640]{2,1,0:T(8,128)(2,1)S(1)}, u32[]{:S(2)}, u32[]{:S(2)}) async-start(bf16[4,64,640]{2,1,0:T(8,128)(2,1)} %pad_maximum_fusion.1), calls=%async_computation.8 | async-start | bytes 655360 | tf_op jit(solution)/shard_map/all_to_all | solution.py:199
  281.6 14.1 %collective-permute-start.11 = (bf16[64,640]{1,0:T(8,128)(2,1)S(1)}, bf16[64,640]{1,0:T(8,128)(2,1)S(1)}, u32[]{:S(2)}, u32[]{:S(2)}) collective-permute-start(bf16[64,640]{1,0:T(8,128)(2,1)S(1)} %add_convert_fusion.1), channel_id=1, source_target_pairs={{0,0},{1,128},{2,256},{3,384},{128,1},{129,129},{130,257},{131,385... | collective-permute-start | bytes 245768 | tf_op jit(solution)/shard_map/ppermute | solution.py:29

commit v3 on v2

--- a/solution.py
+++ b/solution.py
@@ -1,7 +1,12 @@
+import functools
+
 import jax
 import jax.numpy as jnp
 from jax import lax
+from jax.experimental import pallas as pl
+from jax.experimental.pallas import tpu as pltpu
 from jax.sharding import Mesh, PartitionSpec as P
+
 
 HEAD_DIM = 128
 PAGE = 16
@@ -23,6 +28,10 @@
 
 def iota(shape, dim):
     return lax.broadcasted_iota(I32, shape, dim)
+
+
+def from_ahead(value, axis, step, size):
+    return lax.ppermute(value, axis, [((i + step) % size, i) for i in range(size)])
 
 
 def swapped(value, axis, size, mate):
@@ -104,15 +113,50 @@
     return (wide * lax.rsqrt(square + epsilon) * gain).astype(BF16)
 
 
-def experts_of(rows, weights):
-    total = None
-    for gate_up, down in weights:
-        units = down.shape[0]
-        projected = dot(rows, gate_up, ((1,), (0,)))
-        activated = (jax.nn.silu(projected[:, :units]) * projected[:, units:]).astype(BF16)
-        part = dot(activated, down, ((1,), (0,)))
-        total = part if total is None else total + part
-    return total.astype(BF16)
+def experts_kernel(groups, rows_ref, *refs):
+    sources, (out_ref, gate_up, down, total, arrived) = refs[: 2 * groups], refs[2 * groups :]
+    copies = []
+    for group in range(groups):
+        for i, target in enumerate((gate_up, down)):
+            number = 2 * group + i
+            copies.append(
+                pltpu.make_async_copy(sources[number], target.at[group], arrived.at[number])
+            )
+    for copy in copies:
+        copy.start()
+    units = down.shape[1]
+    for group in range(groups):
+        copies[2 * group].wait()
+        projected = jnp.dot(rows_ref[...], gate_up[group], preferred_element_type=F32)
+        gate, upper = projected[:, :units], projected[:, units:]
+        activated = (gate / (1.0 + jnp.exp(-gate)) * upper).astype(BF16)
+        copies[2 * group + 1].wait()
+        part = jnp.dot(activated, down[group], preferred_element_type=F32)
+        if group == 0:
+            total[...] = part
+        else:
+            total[...] += part
+    out_ref[...] = total[...].astype(BF16)
+
+
+def experts_of(rows, gate_ups, downs):
+    groups = len(gate_ups)
+    operands = [a for both in zip(gate_ups, downs) for a in both]
+    vmem = pl.BlockSpec(memory_space=pltpu.VMEM)
+    anywhere = pl.BlockSpec(memory_space=pl.ANY)
+    return pl.pallas_call(
+        functools.partial(experts_kernel, groups),
+        out_shape=jax.ShapeDtypeStruct(rows.shape, BF16),
+        in_specs=[vmem] + [anywhere] * len(operands),
+        out_specs=vmem,
+        scratch_shapes=[
+            pltpu.VMEM((groups,) + gate_ups[0].shape, BF16),
+            pltpu.VMEM((groups,) + downs[0].shape, BF16),
+            pltpu.VMEM(rows.shape, F32),
+            pltpu.SemaphoreType.DMA((len(operands),)),
+        ],
+        name="experts",
+    )(rows, *operands)
 
 
 def combined(returned, parts):
@@ -120,7 +164,7 @@
     return dot(high, returned, ((1,), (0,))) + dot(low, returned, ((1,), (0,)))
 
 
-def on_device(
+def layer(
     queries,
     key_values,
     hidden,
@@ -142,6 +186,9 @@
     top = expert_choice.shape[1]
     gate_up_own, down_own = gate_up[0], down[0]
 
+    pair_gate_up = swap_units(gate_up_own)
+    pair_down = swap_units(down_own)
+
     projection = spread_to_all(out_weight.T, ("y", "x", "c"), 2 * planes)
     projection = projection.reshape(share, out_weight.shape[0])
 
@@ -154,18 +201,27 @@
     offset = places - jnp.sum(jnp.where(picked, starts[None, :], 0), axis=1)
 
     context = attend(queries, key_values, segment[None, :], segment[:, None])
-    contexts = spread_to_all(context, "zh", n_zh)
+    contexts = [context]
+    for j in range(1, n_zh):
+        contexts.append(from_ahead(context, "zh", j, n_zh))
+    contexts = jnp.stack(contexts)
+    contexts = jnp.concatenate(
+        [
+            lax.dynamic_index_in_dim(contexts, (i - zh) % n_zh, 0, keepdims=False)
+            for i in range(n_zh)
+        ],
+        axis=0,
+    )
 
     hidden_own = turned(lax.dynamic_slice_in_dim(hidden, tp * share, share, 1))
-    near_packed = turned(packed_routing(expert_choice, route_weight))
+    near_packed = packed_routing(expert_choice, route_weight)
+    near_packed = turned(near_packed)
     far_packed = swap_groups(near_packed)
 
-    weights = [(gate_up_own, down_own)]
-    weights.append((swap_units(gate_up_own), swap_units(down_own)))
-    weights.append((swap_cores(gate_up_own), swap_cores(down_own)))
-    weights.append((swap_cores(weights[1][0]), swap_cores(weights[1][1])))
-
-    partial = dot(contexts.reshape(n_zh * count, -1), projection, ((1,), (1,))).astype(BF16)
+    gate_ups = [gate_up_own, swap_cores(gate_up_own), pair_gate_up, swap_cores(pair_gate_up)]
+    downs = [down_own, swap_cores(down_own), pair_down, swap_cores(pair_down)]
+
+    partial = dot(contexts, projection, ((1,), (1,))).astype(BF16)
     partial = lax.all_to_all(
         partial.reshape(n_zh, count, share), "tp", 0, 0, tiled=True
     )
@@ -186,8 +242,8 @@
 
     near_in, near_parts = sent(near, near_packed)
     far_in, far_parts = sent(far, far_packed)
-    near_out = experts_of(near_in.reshape(-1, width), weights).reshape(near_in.shape)
-    far_out = experts_of(far_in.reshape(-1, width), weights).reshape(far_in.shape)
+    near_out = experts_of(near_in.reshape(-1, width), gate_ups, downs).reshape(near_in.shape)
+    far_out = experts_of(far_in.reshape(-1, width), gate_ups, downs).reshape(far_in.shape)
     far_back = lax.all_to_all(far_out, PLANE, 0, 0, tiled=True)
     far_back, near_out = lax.optimization_barrier((far_back, near_out))
     near_back = lax.all_to_all(near_out, PLANE, 0, 0, tiled=True)
@@ -232,7 +288,7 @@
         P(REQ, "tp", None),
     )
     return jax.shard_map(
-        on_device,
+        layer,
         mesh=grid,
         in_specs=placed,
         out_specs=(P(REQ, "tp"), P(REQ, None, "tp")),

time: 298 us -> 294 us (0.987)
  the two profiles are of different devices: /device:TPU:84 before, /device:TPU:82 now
where the time goes in v3:
time: 294 us; the launch traced here: 292 us
  waiting for transfers between devices  134 us (46%)
  starting transfers between devices  122 us (41%)
  Pallas kernels  14.3 us (5%)
  matrix products  9.08 us (3%)
  local copies, waits for them, and re-layouts  7.91 us (3%)
  other arithmetic  3.62 us (1%)
    ppermute x12, waiting for transfers between devices, swapped(): return lax.ppermute(value, axis, [(i, mate(i)) for i in range(size)])  103 us
    ppermute x12, starting transfers between devices, swapped(): return lax.ppermute(value, axis, [(i, mate(i)) for i in range(size)])  45.1 us
    ppermute x3, starting transfers between devices, from_ahead(): lax.ppermute(value, axis, [((i + step) % size, i) for i in range(size)])  23.7 us
    all_to_all x2, starting transfers between devices, sent(): return (lax.all_to_all(rows, PLANE, 0, 0, tiled=True), parts)  14.8 us
    pallas_call x2, Pallas kernels, experts_of(): pl.pallas_call(functools.partial(experts_kernel, groups), out_shape=jax.S...  14.3 us
    all_to_all x2, starting transfers between devices, spread_to_all(): return lax.all_to_all(copies, axis, 0, 0, tiled=True)  14.1 us
    all_to_all x1, waiting for transfers between devices, layer(): gathered = lax.all_to_all(columns, 'zh', 0, 0, tiled=True)  13.9 us
    ppermute x3, waiting for transfers between devices, from_ahead(): lax.ppermute(value, axis, [((i + step) % size, i) for i in range(size)])  9.88 us
  transfers between devices with their start and end apart: 23, of which 11 were waited for; matrix products, arithmetic and copies ran while one was open for 4% of the time, Pallas kernels for 5%

profile of v3, /device:TPU:82, one launch (start us, length us, event | category | flops | bytes accessed | tf_op | source)
XLA Modules:
  0.0 292.2 jit_solution(1445614332938524407)
XLA Ops:
  0.7 1.8 broadcast_in_dim.265
  2.5 7.4 %all-to-all-start = ((bf16[32,20,640]{2,1,0:T(8,128)(2,1)}), bf16[32,20,640]{2,1,0:T(8,128)(2,1)S(1)}, u32[]{:S(2)}, u32[]{:S(2)}) async-start(bf16[32,20,640]{2,1,0:T(8,128)(2,1)} %broadcast_in_dim.265), calls=%async_computation | async-start | bytes 1966080 | tf_op jit(solution)/shard_map/all_to_all | solution.py:59
  11.6 10.9 %collective-permute-start.1 = (bf16[64,640]{1,0:T(8,128)(2,1)S(1)}, bf16[64,640]{1,0:T(8,128)(2,1)S(1)}, u32[]{:S(2)}, u32[]{:S(2)}) collective-permute-start(bf16[64,640]{1,0:T(8,128)(2,1)S(1)} %constant_dynamic-update-slice_fusion.5), channel_id=1, source_target_pairs={{128,0},{256,128},{384,256},{0,384},{129,1},{257,129},{385,257},{1... | collective-permute-start | bytes 245768 | tf_op jit(solution)/shard_map/ppermute | solution.py:34
  22.5 5.4 %collective-permute-start.2 = (bf16[64,640]{1,0:T(8,128)(2,1)S(1)}, bf16[64,640]{1,0:T(8,128)(2,1)S(1)}, u32[]{:S(2)}, u32[]{:S(2)}) collective-permute-start(bf16[64,640]{1,0:T(8,128)(2,1)S(1)} %constant_dynamic-update-slice_fusion.5), channel_id=1, source_target_pairs={{256,0},{384,128},{0,256},{128,384},{257,1},{385,129},{1,257},{129... | collective-permute-start | bytes 245768 | tf_op jit(solution)/shard_map/ppermute | solution.py:34
  28.0 7.3 %collective-permute-start.3 = (bf16[64,640]{1,0:T(8,128)(2,1)S(1)}, bf16[64,640]{1,0:T(8,128)(2,1)S(1)}, u32[]{:S(2)}, u32[]{:S(2)}) collective-permute-start(bf16[64,640]{1,0:T(8,128)(2,1)S(1)} %constant_dynamic-update-slice_fusion.5), channel_id=1, source_target_pairs={{384,0},{0,128},{128,256},{256,384},{385,1},{1,129},{129,257},{257... | collective-permute-start | bytes 245768 | tf_op jit(solution)/shard_map/ppermute | solution.py:34
  35.4 9.9 %collective-permute-done.2 = bf16[64,640]{1,0:T(8,128)(2,1)S(1)} collective-permute-done((bf16[64,640]{1,0:T(8,128)(2,1)S(1)}, bf16[64,640]{1,0:T(8,128)(2,1)S(1)}, u32[]{:S(2)}, u32[]{:S(2)}) %collective-permute-start.2) | collective-permute-done | bytes 81952 | tf_op jit(solution)/shard_map/ppermute | solution.py:34
  45.3 0.7 dynamic-slice_bitcast_fusion.3
  46.0 1.1 reshape.166
  47.1 2.5 convolution_convert_fusion.2
  49.5 6.1 %all-to-all-start.1 = ((bf16[4,64,640]{2,1,0:T(8,128)(2,1)}), bf16[4,64,640]{2,1,0:T(8,128)(2,1)}, u32[]{:S(2)}, u32[]{:S(2)}) async-start(bf16[4,64,640]{2,1,0:T(8,128)(2,1)} %bitcast.149), calls=%async_computation.1 | async-start | bytes 655360 | tf_op jit(solution)/shard_map/all_to_all | solution.py:225
  55.6 3.4 %collective-permute-start.9 = (bf16[2560,384]{1,0:T(8,128)(2,1)S(1)}, bf16[2560,384]{1,0:T(8,128)(2,1)}, u32[]{:S(2)}, u32[]{:S(2)}) collective-permute-start(bf16[2560,384]{1,0:T(8,128)(2,1)S(1)} %bitcast.141), channel_id=1, source_target_pairs={{0,1},{1,0},{2,3},{3,2},{4,5},{5,4},{6,7},{7,6},{8,9},{9,8},{10,11... | collective-permute-start | bytes 5898248 | tf_op jit(solution)/shard_map/ppermute | solution.py:38
  59.0 1.9 collective-permute-start.7
  60.9 2.5 collective-permute-start.10
  63.4 2.1 collective-permute-start.8
  65.6 6.6 %collective-permute-start = (bf16[64,640]{1,0:T(8,128)(2,1)S(1)}, bf16[64,640]{1,0:T(8,128)(2,1)S(1)}, u32[]{:S(2)}, u32[]{:S(2)}) collective-permute-start(bf16[64,640]{1,0:T(8,128)(2,1)S(1)} %constant_dynamic-slice_fusion), channel_id=1, source_target_pairs={{0,0},{1,128},{2,256},{3,384},{128,1},{129,129},{130,257},{131,385... | collective-permute-start | bytes 245768 | tf_op jit(solution)/shard_map/ppermute | solution.py:38
  72.2 0.7 reduce-precision_convert_fusion
  72.9 1.0 convert_reduce_fusion.1
  73.9 53.7 %collective-permute-done = bf16[64,640]{1,0:T(8,128)(2,1)S(1)} collective-permute-done((bf16[64,640]{1,0:T(8,128)(2,1)S(1)}, bf16[64,640]{1,0:T(8,128)(2,1)S(1)}, u32[]{:S(2)}, u32[]{:S(2)}) %collective-permute-start) | collective-permute-done | bytes 81952 | tf_op jit(solution)/shard_map/ppermute | solution.py:38
  127.7 0.8 broadcast_in_dim.279
  128.4 6.7 %all-to-all-start.2 = ((bf16[4,64,640]{2,1,0:T(8,128)(2,1)}), bf16[4,64,640]{2,1,0:T(8,128)(2,1)}, u32[]{:S(2)}, u32[]{:S(2)}) async-start(bf16[4,64,640]{2,1,0:T(8,128)(2,1)} %broadcast_in_dim.279), calls=%async_computation.2 | async-start | bytes 655360 | tf_op jit(solution)/shard_map/all_to_all | solution.py:59
  135.2 16.6 %collective-permute-start.4 = (bf16[64,128]{0,1:T(8,128)(2,1)S(1)}, bf16[64,128]{0,1:T(8,128)(2,1)S(1)}, u32[]{:S(2)}, u32[]{:S(2)}) collective-permute-start(bf16[64,128]{0,1:T(8,128)(2,1)S(1)} %fusion.38), channel_id=1, source_target_pairs={{0,0},{1,128},{2,256},{3,384},{128,1},{129,129},{130,257},{131,385... | collective-permute-start | bytes 49160 | tf_op jit(solution)/shard_map/ppermute | solution.py:38
  151.8 9.9 %collective-permute-done.4 = bf16[64,128]{0,1:T(8,128)(2,1)S(1)} collective-permute-done((bf16[64,128]{0,1:T(8,128)(2,1)S(1)}, bf16[64,128]{0,1:T(8,128)(2,1)S(1)}, u32[]{:S(2)}, u32[]{:S(2)}) %collective-permute-start.4) | collective-permute-done | bytes 16416 | tf_op jit(solution)/shard_map/ppermute | solution.py:38
  161.7 1.9 collective-permute-start.5
  163.6 3.9 %collective-permute-done.5 = bf16[64,128]{0,1:T(8,128)(2,1)S(1)} collective-permute-done((bf16[64,128]{0,1:T(8,128)(2,1)S(1)}, bf16[64,128]{0,1:T(8,128)(2,1)S(1)}, u32[]{:S(2)}, u32[]{:S(2)}) %collective-permute-start.5) | collective-permute-done | bytes 16416 | tf_op jit(solution)/shard_map/ppermute | solution.py:38
  167.5 1.0 slice_bitcast_fusion.7
  168.7 1.9 collective-permute-start.6
  170.7 1.9 collective-permute-start.11
  172.9 13.3 %collective-permute-done.6 = bf16[64,2560]{1,0:T(8,128)(2,1)S(1)} collective-permute-done((bf16[64,2560]{1,0:T(8,128)(2,1)S(1)}, bf16[64,2560]{1,0:T(8,128)(2,1)S(1)}, u32[]{:S(2)}, u32[]{:S(2)}) %collective-permute-start.6) | collective-permute-done | bytes 327712 | tf_op jit(solution)/shard_map/ppermute | solution.py:38
  186.3 1.2 fusion
  187.6 7.2 %all-to-all-start.3 = ((bf16[16,8,2560]{2,1,0:T(8,128)(2,1)}), bf16[16,8,2560]{2,1,0:T(8,128)(2,1)}, u32[]{:S(2)}, u32[]{:S(2)}) async-start(bf16[16,8,2560]{2,1,0:T(8,128)(2,1)} %fusion), calls=%async_computation.3 | async-start | bytes 1310720 | tf_op jit(solution)/shard_map/all_to_all | solution.py:241
  194.8 1.9 collective-permute-start.12
  197.0 2.2 fusion.1
  199.2 3.4 %all-to-all-done.3 = bf16[16,8,2560]{2,1,0:T(8,128)(2,1)} async-done(((bf16[16,8,2560]{2,1,0:T(8,128)(2,1)}), bf16[16,8,2560]{2,1,0:T(8,128)(2,1)}, u32[]{:S(2)}, u32[]{:S(2)}) %all-to-all-start.3) | async-done | bytes 655392 | tf_op jit(solution)/shard_map/all_to_all | solution.py:241
  202.6 7.6 %all-to-all-start.5 = ((bf16[16,8,2560]{2,1,0:T(8,128)(2,1)}), bf16[16,8,2560]{2,1,0:T(8,128)(2,1)}, u32[]{:S(2)}, u32[]{:S(2)}) async-start(bf16[16,8,2560]{2,1,0:T(8,128)(2,1)} %fusion.1), calls=%async_computation.5 | async-start | bytes 1310720 | tf_op jit(solution)/shard_map/all_to_all | solution.py:241
  210.2 0.8 fusion.145
  211.0 7.2 %experts.2 = bf16[128,2560]{1,0:T(8,128)(2,1)} custom-call(bf16[128,2560]{1,0:T(8,128)(2,1)} %bitcast.36.rows_ref, bf16[2560,384]{1,0:T(8,128)(2,1)} %bitcast.139, bf16[192,2560]{1,0:T(8,128)(2,1)} %bitcast.143, bf16[2560,384]{1,0:T(8,128)(2,1)} %collective-permute-done.7.refs_2_, bf16[192,2560]{1,0:T(8,128)(2,1)} %collective-permute-done.8.refs_3_, ...), custom_call_target="tpu_custom_call" | custom-call | tf_op jit(solution)/shard_map/experts/pallas_call | solution.py:147
  218.1 7.2 %all-to-all-start.4 = ((bf16[16,8,2560]{2,1,0:T(8,128)(2,1)}), bf16[16,8,2560]{2,1,0:T(8,128)(2,1)S(1)}, u32[]{:S(2)}, u32[]{:S(2)}) async-start(bf16[16,8,2560]{2,1,0:T(8,128)(2,1)} %bitcast.148), calls=%async_computation.4 | async-start | bytes 1310720 | tf_op jit(solution)/shard_map/all_to_all | solution.py:247
  225.4 7.2 %experts.3 = bf16[128,2560]{1,0:T(8,128)(2,1)} custom-call(bf16[128,2560]{1,0:T(8,128)(2,1)} %bitcast.41.rows_ref, bf16[2560,384]{1,0:T(8,128)(2,1)} %bitcast.140, bf16[192,2560]{1,0:T(8,128)(2,1)} %bitcast.144, bf16[2560,384]{1,0:T(8,128)(2,1)} %collective-permute-done.7.refs_2_, bf16[192,2560]{1,0:T(8,128)(2,1)} %collective-permute-done.8.refs_3_, ...), custom_call_target="tpu_custom_call" | custom-call | tf_op jit(solution)/shard_map/experts/pallas_call | solution.py:147
  232.8 7.1 %all-to-all-start.6 = ((bf16[16,8,2560]{2,1,0:T(8,128)(2,1)}), bf16[16,8,2560]{2,1,0:T(8,128)(2,1)S(1)}, u32[]{:S(2)}, u32[]{:S(2)}) async-start(bf16[16,8,2560]{2,1,0:T(8,128)(2,1)} %bitcast.147), calls=%async_computation.6 | async-start | bytes 1310720 | tf_op jit(solution)/shard_map/all_to_all | solution.py:249
  240.6 2.5 collective-permute-start.13
  243.1 4.1 %all-to-all-done.6 = bf16[16,8,2560]{2,1,0:T(8,128)(2,1)S(1)} async-done(((bf16[16,8,2560]{2,1,0:T(8,128)(2,1)}), bf16[16,8,2560]{2,1,0:T(8,128)(2,1)S(1)}, u32[]{:S(2)}, u32[]{:S(2)}) %all-to-all-start.6) | async-done | bytes 655392 | tf_op jit(solution)/shard_map/all_to_all | solution.py:249
  247.6 11.7 %collective-permute-done.13 = bf16[64,2560]{1,0:T(8,128)(2,1)S(1)} collective-permute-done((bf16[64,2560]{1,0:T(8,128)(2,1)S(1)}, bf16[64,2560]{1,0:T(8,128)(2,1)S(1)}, u32[]{:S(2)}, u32[]{:S(2)}) %collective-permute-start.13) | collective-permute-done | bytes 327712 | tf_op jit(solution)/shard_map/ppermute | solution.py:38
  259.7 0.8 pad_maximum_fusion.2
  260.5 3.5 %all-to-all-start.7 = ((bf16[4,64,640]{2,1,0:T(8,128)(2,1)}), bf16[4,64,640]{2,1,0:T(8,128)(2,1)S(1)}, u32[]{:S(2)}, u32[]{:S(2)}) async-start(bf16[4,64,640]{2,1,0:T(8,128)(2,1)} %pad_maximum_fusion.2), calls=%async_computation.7 | async-start | bytes 655360 | tf_op jit(solution)/shard_map/all_to_all | solution.py:255
  264.4 13.9 %all-to-all-done.7 = bf16[4,64,640]{2,1,0:T(8,128)(2,1)S(1)} async-done(((bf16[4,64,640]{2,1,0:T(8,128)(2,1)}), bf16[4,64,640]{2,1,0:T(8,128)(2,1)S(1)}, u32[]{:S(2)}, u32[]{:S(2)}) %all-to-all-start.7) | async-done | bytes 327712 | tf_op jit(solution)/shard_map/all_to_all | solution.py:255
  278.3 1.9 collective-permute-start.14
  280.2 0.8 convolution_convert_fusion.4
  281.0 10.5 %collective-permute-done.14 = bf16[64,640]{1,0:T(8,128)(2,1)S(1)} collective-permute-done((bf16[64,640]{1,0:T(8,128)(2,1)S(1)}, bf16[64,640]{1,0:T(8,128)(2,1)S(1)}, u32[]{:S(2)}, u32[]{:S(2)}) %collective-permute-start.14) | collective-permute-done | bytes 81952 | tf_op jit(solution)/shard_map/ppermute | solution.py:38
  (100 shorter events, 5.5 us)
Async XLA Ops:
  0.6 64.9 %copy-start = (bf16[64,2560]{1,0:T(8,128)(2,1)S(1)}, bf16[64,2560]{1,0:T(8,128)(2,1)}, u32[]{:S(2)}) copy-start(bf16[64,2560]{1,0:T(8,128)(2,1)} %param.13) | copy-start | bytes 983044
  0.6 9.3 %copy-start.12 = (s32[1,4]{1,0:T(1,128)S(1)}, s32[1,4]{1,0:T(1,128)}, u32[]{:S(2)}) copy-start(s32[1,4]{1,0:T(1,128)} %param.14) | copy-start | bytes 52
  0.7 10.3 %copy-start.4 = (bf16[64,640]{1,0:T(8,128)(2,1)S(1)}, bf16[64,640]{1,0:T(8,128)(2,1)}, u32[]{:S(2)}) copy-start(bf16[64,640]{1,0:T(8,128)(2,1)} %param.11) | copy-start | bytes 245764
  0.7 10.4 %copy-start.5 = (bf16[64,256]{1,0:T(8,128)(2,1)S(1)}, bf16[64,256]{1,0:T(8,128)(2,1)}, u32[]{:S(2)}) copy-start(bf16[64,256]{1,0:T(8,128)(2,1)} %param.12) | copy-start | bytes 98308
  2.5 43.5 %all-to-all-start = ((bf16[32,20,640]{2,1,0:T(8,128)(2,1)}), bf16[32,20,640]{2,1,0:T(8,128)(2,1)S(1)}, u32[]{:S(2)}, u32[]{:S(2)}) async-start(bf16[32,20,640]{2,1,0:T(8,128)(2,1)} %broadcast_in_dim.265), calls=%async_computation | async-start | bytes 1966080 | tf_op jit(solution)/shard_map/all_to_all | solution.py:59
  10.1 0.6 copy-start.14
  10.8 34.5 %copy-start.8 = (s32[64]{0:T(128)}, s32[64]{0:T(128)S(1)}, u32[]{:S(2)}) copy-start(s32[64]{0:T(128)S(1)} %convert_reduce_fusion.2) | copy-start | bytes 772
  11.6 23.8 %collective-permute-start.1 = (bf16[64,640]{1,0:T(8,128)(2,1)S(1)}, bf16[64,640]{1,0:T(8,128)(2,1)S(1)}, u32[]{:S(2)}, u32[]{:S(2)}) collective-permute-start(bf16[64,640]{1,0:T(8,128)(2,1)S(1)} %constant_dynamic-update-slice_fusion.5), channel_id=1, source_target_pairs={{128,0},{256,128},{384,256},{0,384},{129,1},{257,129},{385,257},{1... | collective-permute-start | bytes 245768 | tf_op jit(solution)/shard_map/ppermute | solution.py:34
  22.5 22.7 %collective-permute-start.2 = (bf16[64,640]{1,0:T(8,128)(2,1)S(1)}, bf16[64,640]{1,0:T(8,128)(2,1)S(1)}, u32[]{:S(2)}, u32[]{:S(2)}) collective-permute-start(bf16[64,640]{1,0:T(8,128)(2,1)S(1)} %constant_dynamic-update-slice_fusion.5), channel_id=1, source_target_pairs={{256,0},{384,128},{0,256},{128,384},{257,1},{385,129},{1,257},{129... | collective-permute-start | bytes 245768 | tf_op jit(solution)/shard_map/ppermute | solution.py:34
  28.0 17.3 %collective-permute-start.3 = (bf16[64,640]{1,0:T(8,128)(2,1)S(1)}, bf16[64,640]{1,0:T(8,128)(2,1)S(1)}, u32[]{:S(2)}, u32[]{:S(2)}) collective-permute-start(bf16[64,640]{1,0:T(8,128)(2,1)S(1)} %constant_dynamic-update-slice_fusion.5), channel_id=1, source_target_pairs={{384,0},{0,128},{128,256},{256,384},{385,1},{1,129},{129,257},{257... | collective-permute-start | bytes 245768 | tf_op jit(solution)/shard_map/ppermute | solution.py:34
  46.0 9.6 %copy-start.1 = (bf16[1,2560,384]{2,1,0:T(8,128)(2,1)S(1)}, bf16[1,2560,384]{2,1,0:T(8,128)(2,1)}, u32[]{:S(2)}) copy-start(bf16[1,2560,384]{2,1,0:T(8,128)(2,1)} %param.20) | copy-start | bytes 5898244
  47.1 13.9 %copy-start.2 = (bf16[1,192,2560]{2,1,0:T(8,128)(2,1)S(1)}, bf16[1,192,2560]{2,1,0:T(8,128)(2,1)}, u32[]{:S(2)}) copy-start(bf16[1,192,2560]{2,1,0:T(8,128)(2,1)} %param.21) | copy-start | bytes 2949124
  49.5 85.6 %copy-start.7 = (s32[64,6]{0,1:T(8,128)S(1)}, s32[64,6]{0,1:T(8,128)}, u32[]{:S(2)}) copy-start(s32[64,6]{0,1:T(8,128)} %param.18) | copy-start | bytes 4612
  49.5 23.3 %all-to-all-start.1 = ((bf16[4,64,640]{2,1,0:T(8,128)(2,1)}), bf16[4,64,640]{2,1,0:T(8,128)(2,1)}, u32[]{:S(2)}, u32[]{:S(2)}) async-start(bf16[4,64,640]{2,1,0:T(8,128)(2,1)} %bitcast.149), calls=%async_computation.1 | async-start | bytes 655360 | tf_op jit(solution)/shard_map/all_to_all | solution.py:225
  55.6 115.1 %collective-permute-start.9 = (bf16[2560,384]{1,0:T(8,128)(2,1)S(1)}, bf16[2560,384]{1,0:T(8,128)(2,1)}, u32[]{:S(2)}, u32[]{:S(2)}) collective-permute-start(bf16[2560,384]{1,0:T(8,128)(2,1)S(1)} %bitcast.141), channel_id=1, source_target_pairs={{0,1},{1,0},{2,3},{3,2},{4,5},{5,4},{6,7},{7,6},{8,9},{9,8},{10,11... | collective-permute-start | bytes 5898248 | tf_op jit(solution)/shard_map/ppermute | solution.py:38
  59.0 152.0 %collective-permute-start.7 = (bf16[2560,384]{1,0:T(8,128)(2,1)S(1)}, bf16[2560,384]{1,0:T(8,128)(2,1)}, u32[]{:S(2)}, u32[]{:S(2)}) collective-permute-start(bf16[2560,384]{1,0:T(8,128)(2,1)S(1)} %bitcast.142), channel_id=1, source_target_pairs={{0,4},{4,0},{1,5},{5,1},{2,6},{6,2},{3,7},{7,3},{8,12},{12,8},{9,1... | collective-permute-start | bytes 5898248 | tf_op jit(solution)/shard_map/ppermute | solution.py:38
  60.9 133.9 %collective-permute-start.10 = (bf16[192,2560]{1,0:T(8,128)(2,1)S(1)}, bf16[192,2560]{1,0:T(8,128)(2,1)}, u32[]{:S(2)}, u32[]{:S(2)}) collective-permute-start(bf16[192,2560]{1,0:T(8,128)(2,1)S(1)} %bitcast.145), channel_id=1, source_target_pairs={{0,1},{1,0},{2,3},{3,2},{4,5},{5,4},{6,7},{7,6},{8,9},{9,8},{10,11... | collective-permute-start | bytes 2949128 | tf_op jit(solution)/shard_map/ppermute | solution.py:38
  63.4 147.5 %collective-permute-start.8 = (bf16[192,2560]{1,0:T(8,128)(2,1)S(1)}, bf16[192,2560]{1,0:T(8,128)(2,1)}, u32[]{:S(2)}, u32[]{:S(2)}) collective-permute-start(bf16[192,2560]{1,0:T(8,128)(2,1)S(1)} %bitcast.146), channel_id=1, source_target_pairs={{0,4},{4,0},{1,5},{5,1},{2,6},{6,2},{3,7},{7,3},{8,12},{12,8},{9,1... | collective-permute-start | bytes 2949128 | tf_op jit(solution)/shard_map/ppermute | solution.py:38
  65.6 62.1 %collective-permute-start = (bf16[64,640]{1,0:T(8,128)(2,1)S(1)}, bf16[64,640]{1,0:T(8,128)(2,1)S(1)}, u32[]{:S(2)}, u32[]{:S(2)}) collective-permute-start(bf16[64,640]{1,0:T(8,128)(2,1)S(1)} %constant_dynamic-slice_fusion), channel_id=1, source_target_pairs={{0,0},{1,128},{2,256},{3,384},{128,1},{129,129},{130,257},{131,385... | collective-permute-start | bytes 245768 | tf_op jit(solution)/shard_map/ppermute | solution.py:38
  72.9 113.5 %copy-start.6 = (f32[2560]{0:T(1024)S(1)}, f32[2560]{0:T(1024)}, u32[]{:S(2)}) copy-start(f32[2560]{0:T(1024)} %param.17) | copy-start | bytes 30724
  128.4 39.1 %all-to-all-start.2 = ((bf16[4,64,640]{2,1,0:T(8,128)(2,1)}), bf16[4,64,640]{2,1,0:T(8,128)(2,1)}, u32[]{:S(2)}, u32[]{:S(2)}) async-start(bf16[4,64,640]{2,1,0:T(8,128)(2,1)} %broadcast_in_dim.279), calls=%async_computation.2 | async-start | bytes 655360 | tf_op jit(solution)/shard_map/all_to_all | solution.py:59
  135.2 26.5 %collective-permute-start.4 = (bf16[64,128]{0,1:T(8,128)(2,1)S(1)}, bf16[64,128]{0,1:T(8,128)(2,1)S(1)}, u32[]{:S(2)}, u32[]{:S(2)}) collective-permute-start(bf16[64,128]{0,1:T(8,128)(2,1)S(1)} %fusion.38), channel_id=1, source_target_pairs={{0,0},{1,128},{2,256},{3,384},{128,1},{129,129},{130,257},{131,385... | collective-permute-start | bytes 49160 | tf_op jit(solution)/shard_map/ppermute | solution.py:38
  161.7 10.9 %copy-start.10 = (bf16[64,128]{0,1:T(8,128)(2,1)}, bf16[64,128]{0,1:T(8,128)(2,1)S(1)}, u32[]{:S(2)}) copy-start(bf16[64,128]{0,1:T(8,128)(2,1)S(1)} %collective-permute-done.4) | copy-start | bytes 49156
  161.7 5.8 %collective-permute-start.5 = (bf16[64,128]{0,1:T(8,128)(2,1)S(1)}, bf16[64,128]{0,1:T(8,128)(2,1)S(1)}, u32[]{:S(2)}, u32[]{:S(2)}) collective-permute-start(bf16[64,128]{0,1:T(8,128)(2,1)S(1)} %collective-permute-done.4), channel_id=1, source_target_pairs={{0,3},{1,2},{2,1},{3,0},{4,7},{5,6},{6,5},{7,4},{8,11},{9,10},{10,... | collective-permute-start | bytes 49160 | tf_op jit(solution)/shard_map/ppermute | solution.py:38
  168.7 17.4 %copy-start.3 = (bf16[64,2560]{1,0:T(8,128)(2,1)}, bf16[64,2560]{1,0:T(8,128)(2,1)S(1)}, u32[]{:S(2)}) copy-start(bf16[64,2560]{1,0:T(8,128)(2,1)S(1)} %get-tuple-element.7) | copy-start | bytes 983044
  168.7 17.4 %collective-permute-start.6 = (bf16[64,2560]{1,0:T(8,128)(2,1)S(1)}, bf16[64,2560]{1,0:T(8,128)(2,1)S(1)}, u32[]{:S(2)}, u32[]{:S(2)}) collective-permute-start(bf16[64,2560]{1,0:T(8,128)(2,1)S(1)} %get-tuple-element.7), channel_id=1, source_target_pairs={{0,3},{1,2},{2,1},{3,0},{4,7},{5,6},{6,5},{7,4},{8,11},{9,10},{10,... | collective-permute-start | bytes 983048 | tf_op jit(solution)/shard_map/ppermute | solution.py:38
  170.7 40.3 %collective-permute-start.11 = (bf16[2560,384]{1,0:T(8,128)(2,1)}, bf16[2560,384]{1,0:T(8,128)(2,1)}, u32[]{:S(2)}, u32[]{:S(2)}) collective-permute-start(bf16[2560,384]{1,0:T(8,128)(2,1)} %collective-permute-done.9.refs_4_), channel_id=1, source_target_pairs={{0,4},{4,0},{1,5},{5,1},{2,6},{6,2},{3,7},{7,3},{8,12},{12,8},{9,1... | collective-permute-start | bytes 5898248 | tf_op jit(solution)/shard_map/ppermute | solution.py:38
  187.6 15.0 %all-to-all-start.3 = ((bf16[16,8,2560]{2,1,0:T(8,128)(2,1)}), bf16[16,8,2560]{2,1,0:T(8,128)(2,1)}, u32[]{:S(2)}, u32[]{:S(2)}) async-start(bf16[16,8,2560]{2,1,0:T(8,128)(2,1)} %fusion), calls=%async_computation.3 | async-start | bytes 1310720 | tf_op jit(solution)/shard_map/all_to_all | solution.py:241
  194.8 16.2 %collective-permute-start.12 = (bf16[192,2560]{1,0:T(8,128)(2,1)}, bf16[192,2560]{1,0:T(8,128)(2,1)}, u32[]{:S(2)}, u32[]{:S(2)}) collective-permute-start(bf16[192,2560]{1,0:T(8,128)(2,1)} %collective-permute-done.10.refs_5_), channel_id=1, source_target_pairs={{0,4},{4,0},{1,5},{5,1},{2,6},{6,2},{3,7},{7,3},{8,12},{12,8},{9,1... | collective-permute-start | bytes 2949128 | tf_op jit(solution)/shard_map/ppermute | solution.py:38
  202.6 15.6 %all-to-all-start.5 = ((bf16[16,8,2560]{2,1,0:T(8,128)(2,1)}), bf16[16,8,2560]{2,1,0:T(8,128)(2,1)}, u32[]{:S(2)}, u32[]{:S(2)}) async-start(bf16[16,8,2560]{2,1,0:T(8,128)(2,1)} %fusion.1), calls=%async_computation.5 | async-start | bytes 1310720 | tf_op jit(solution)/shard_map/all_to_all | solution.py:241
  218.1 14.6 %all-to-all-start.4 = ((bf16[16,8,2560]{2,1,0:T(8,128)(2,1)}), bf16[16,8,2560]{2,1,0:T(8,128)(2,1)S(1)}, u32[]{:S(2)}, u32[]{:S(2)}) async-start(bf16[16,8,2560]{2,1,0:T(8,128)(2,1)} %bitcast.148), calls=%async_computation.4 | async-start | bytes 1310720 | tf_op jit(solution)/shard_map/all_to_all | solution.py:247
  232.8 14.5 %all-to-all-start.6 = ((bf16[16,8,2560]{2,1,0:T(8,128)(2,1)}), bf16[16,8,2560]{2,1,0:T(8,128)(2,1)S(1)}, u32[]{:S(2)}, u32[]{:S(2)}) async-start(bf16[16,8,2560]{2,1,0:T(8,128)(2,1)} %bitcast.147), calls=%async_computation.6 | async-start | bytes 1310720 | tf_op jit(solution)/shard_map/all_to_all | solution.py:249
  240.6 18.7 %collective-permute-start.13 = (bf16[64,2560]{1,0:T(8,128)(2,1)S(1)}, bf16[64,2560]{1,0:T(8,128)(2,1)S(1)}, u32[]{:S(2)}, u32[]{:S(2)}) collective-permute-start(bf16[64,2560]{1,0:T(8,128)(2,1)S(1)} %fusion.2), channel_id=1, source_target_pairs={{0,3},{1,2},{2,1},{3,0},{4,7},{5,6},{6,5},{7,4},{8,11},{9,10},{10,... | collective-permute-start | bytes 983048 | tf_op jit(solution)/shard_map/ppermute | solution.py:38
  259.3 4.7 %copy-start.11 = (s32[1,4,2]{1,2,0:T(2,128)S(1)}, s32[1,4,2]{1,2,0:T(2,128)}, u32[]{:S(2)}) copy-start(s32[1,4,2]{1,2,0:T(2,128)} %param.15) | copy-start | bytes 100
  259.3 4.9 %copy-start.13 = (s32[1,4]{1,0:T(1,128)S(1)}, s32[1,4]{1,0:T(1,128)}, u32[]{:S(2)}) copy-start(s32[1,4]{1,0:T(1,128)} %param.14) | copy-start | bytes 52
  259.3 4.9 %copy-start.15 = (s32[4,1]{0,1:T(1,128)S(1)}, s32[4,1]{0,1:T(1,128)}, u32[]{:S(2)}) copy-start(s32[4,1]{0,1:T(1,128)} %copy-done.14) | copy-start | bytes 52
  259.3 4.9 %copy-start.9 = (s32[64]{0:T(128)S(1)}, s32[64]{0:T(128)}, u32[]{:S(2)}) copy-start(s32[64]{0:T(128)} %copy-done.8) | copy-start | bytes 772
  260.5 17.7 %all-to-all-start.7 = ((bf16[4,64,640]{2,1,0:T(8,128)(2,1)}), bf16[4,64,640]{2,1,0:T(8,128)(2,1)S(1)}, u32[]{:S(2)}, u32[]{:S(2)}) async-start(bf16[4,64,640]{2,1,0:T(8,128)(2,1)} %pad_maximum_fusion.2), calls=%async_computation.7 | async-start | bytes 655360 | tf_op jit(solution)/shard_map/all_to_all | solution.py:255
  278.3 13.3 %collective-permute-start.14 = (bf16[64,640]{1,0:T(8,128)(2,1)S(1)}, bf16[64,640]{1,0:T(8,128)(2,1)S(1)}, u32[]{:S(2)}, u32[]{:S(2)}) collective-permute-start(bf16[64,640]{1,0:T(8,128)(2,1)S(1)} %add_convert_fusion.1), channel_id=1, source_target_pairs={{0,0},{1,128},{2,256},{3,384},{128,1},{129,129},{130,257},{131,385... | collective-permute-start | bytes 245768 | tf_op jit(solution)/shard_map/ppermute | solution.py:38

commit v4 on v3

--- a/solution.py
+++ b/solution.py
@@ -113,24 +113,37 @@
     return (wide * lax.rsqrt(square + epsilon) * gain).astype(BF16)
 
 
-def experts_kernel(groups, rows_ref, *refs):
-    sources, (out_ref, gate_up, down, total, arrived) = refs[: 2 * groups], refs[2 * groups :]
+def experts_kernel(layout, rows_ref, *refs):
+    count = sum(len(part) for parts in layout for part in parts)
+    sources, (out_ref, gate_up, down, total, arrived) = refs[:count], refs[count:]
     copies = []
-    for group in range(groups):
-        for i, target in enumerate((gate_up, down)):
-            number = 2 * group + i
-            copies.append(
-                pltpu.make_async_copy(sources[number], target.at[group], arrived.at[number])
-            )
+    for group, (up_parts, down_parts) in enumerate(layout):
+        own = []
+        for target, parts in ((gate_up, up_parts), (down, down_parts)):
+            start = 0
+            for size in parts:
+                i = len(copies) + len(own)
+                own.append(
+                    pltpu.make_async_copy(
+                        sources[i], target.at[group, pl.ds(start, size)], arrived.at[i]
+                    )
+                )
+                start += size
+        copies += own
     for copy in copies:
         copy.start()
     units = down.shape[1]
-    for group in range(groups):
-        copies[2 * group].wait()
+    position = 0
+    for group, (up_parts, down_parts) in enumerate(layout):
+        for _ in up_parts:
+            copies[position].wait()
+            position += 1
         projected = jnp.dot(rows_ref[...], gate_up[group], preferred_element_type=F32)
         gate, upper = projected[:, :units], projected[:, units:]
         activated = (gate / (1.0 + jnp.exp(-gate)) * upper).astype(BF16)
-        copies[2 * group + 1].wait()
+        for _ in down_parts:
+            copies[position].wait()
+            position += 1
         part = jnp.dot(activated, down[group], preferred_element_type=F32)
         if group == 0:
             total[...] = part
@@ -140,18 +153,22 @@
 
 
 def experts_of(rows, gate_ups, downs):
-    groups = len(gate_ups)
-    operands = [a for both in zip(gate_ups, downs) for a in both]
+    layout = tuple(
+        (tuple(a.shape[0] for a in ups), tuple(a.shape[0] for a in lows))
+        for ups, lows in zip(gate_ups, downs)
+    )
+    operands = [a for ups, lows in zip(gate_ups, downs) for a in (*ups, *lows)]
+    groups, (depth, columns), units = len(gate_ups), gate_ups[0][0].shape, downs[0][0].shape[0]
     vmem = pl.BlockSpec(memory_space=pltpu.VMEM)
     anywhere = pl.BlockSpec(memory_space=pl.ANY)
     return pl.pallas_call(
-        functools.partial(experts_kernel, groups),
+        functools.partial(experts_kernel, layout),
         out_shape=jax.ShapeDtypeStruct(rows.shape, BF16),
         in_specs=[vmem] + [anywhere] * len(operands),
         out_specs=vmem,
         scratch_shapes=[
-            pltpu.VMEM((groups,) + gate_ups[0].shape, BF16),
-            pltpu.VMEM((groups,) + downs[0].shape, BF16),
+            pltpu.VMEM((groups, depth, columns), BF16),
+            pltpu.VMEM((groups, units, depth), BF16),
             pltpu.VMEM(rows.shape, F32),
             pltpu.SemaphoreType.DMA((len(operands),)),
         ],
@@ -186,8 +203,9 @@
     top = expert_choice.shape[1]
     gate_up_own, down_own = gate_up[0], down[0]
 
-    pair_gate_up = swap_units(gate_up_own)
-    pair_down = swap_units(down_own)
+    cuts = (0, 2 * share, 3 * share, 4 * share)
+    slices = [gate_up_own[a:b] for a, b in zip(cuts, cuts[1:])] + [down_own]
+    pair = [swap_units(value) for value in slices]
 
     projection = spread_to_all(out_weight.T, ("y", "x", "c"), 2 * planes)
     projection = projection.reshape(share, out_weight.shape[0])
@@ -218,8 +236,11 @@
     near_packed = turned(near_packed)
     far_packed = swap_groups(near_packed)
 
-    gate_ups = [gate_up_own, swap_cores(gate_up_own), pair_gate_up, swap_cores(pair_gate_up)]
-    downs = [down_own, swap_cores(down_own), pair_down, swap_cores(pair_down)]
+    cross = [swap_cores(value) for value in pair]
+    core_gate_up = swap_cores(gate_up_own)
+    core_down = swap_cores(down_own)
+    gate_ups = [[gate_up_own], [core_gate_up], pair[:3], cross[:3]]
+    downs = [[down_own], [core_down], pair[3:], cross[3:]]
 
     partial = dot(contexts, projection, ((1,), (1,))).astype(BF16)
     partial = lax.all_to_all(

time: 294 us -> 280 us (0.952)
  the two profiles are of different devices: /device:TPU:82 before, /device:TPU:66 now
where the time goes in v4:
time: 280 us; the launch traced here: 278 us
  starting transfers between devices  149 us (53%)
  waiting for transfers between devices  89.2 us (32%)
  Pallas kernels  14.6 us (5%)
  local copies, waits for them, and re-layouts  10.8 us (4%)
  matrix products  9.18 us (3%)
  other arithmetic  4.31 us (2%)
    ppermute x16, starting transfers between devices, swapped(): return lax.ppermute(value, axis, [(i, mate(i)) for i in range(size)])  72.9 us
    all_to_all x2, waiting for transfers between devices, spread_to_all(): return lax.all_to_all(copies, axis, 0, 0, tiled=True)  26.6 us
    ppermute x16, waiting for transfers between devices, swapped(): return lax.ppermute(value, axis, [(i, mate(i)) for i in range(size)])  25.5 us
    ppermute x3, starting transfers between devices, from_ahead(): lax.ppermute(value, axis, [((i + step) % size, i) for i in range(size)])  23.7 us
    all_to_all x1, waiting for transfers between devices, layer(): gathered = lax.all_to_all(columns, 'zh', 0, 0, tiled=True)  17.1 us
    pallas_call x2, Pallas kernels, experts_of(): pl.pallas_call(functools.partial(experts_kernel, layout), out_shape=jax.S...  14.6 us
    all_to_all x2, starting transfers between devices, sent(): return (lax.all_to_all(rows, PLANE, 0, 0, tiled=True), parts)  14.5 us
    all_to_all x2, starting transfers between devices, spread_to_all(): return lax.all_to_all(copies, axis, 0, 0, tiled=True)  11.7 us
  transfers between devices with their start and end apart: 27, of which 10 were waited for; matrix products, arithmetic and copies ran while one was open for 6% of the time, Pallas kernels for 5%

profile of v4, /device:TPU:66, one launch (start us, length us, event | category | flops | bytes accessed | tf_op | source)
XLA Modules:
  0.0 278.2 jit_solution(6921504977544652539)
XLA Ops:
  0.7 1.8 broadcast_in_dim.265
  2.5 7.6 %all-to-all-start = ((bf16[32,20,640]{2,1,0:T(8,128)(2,1)}), bf16[32,20,640]{2,1,0:T(8,128)(2,1)S(1)}, u32[]{:S(2)}, u32[]{:S(2)}) async-start(bf16[32,20,640]{2,1,0:T(8,128)(2,1)} %broadcast_in_dim.265), calls=%async_computation | async-start | bytes 1966080 | tf_op jit(solution)/shard_map/all_to_all | solution.py:59
  11.8 10.9 %collective-permute-start.1 = (bf16[64,640]{1,0:T(8,128)(2,1)S(1)}, bf16[64,640]{1,0:T(8,128)(2,1)S(1)}, u32[]{:S(2)}, u32[]{:S(2)}) collective-permute-start(bf16[64,640]{1,0:T(8,128)(2,1)S(1)} %constant_dynamic-update-slice_fusion.5), channel_id=1, source_target_pairs={{128,0},{256,128},{384,256},{0,384},{129,1},{257,129},{385,257},{1... | collective-permute-start | bytes 245768 | tf_op jit(solution)/shard_map/ppermute | solution.py:34
  22.7 5.4 %collective-permute-start.2 = (bf16[64,640]{1,0:T(8,128)(2,1)S(1)}, bf16[64,640]{1,0:T(8,128)(2,1)S(1)}, u32[]{:S(2)}, u32[]{:S(2)}) collective-permute-start(bf16[64,640]{1,0:T(8,128)(2,1)S(1)} %constant_dynamic-update-slice_fusion.5), channel_id=1, source_target_pairs={{256,0},{384,128},{0,256},{128,384},{257,1},{385,129},{1,257},{129... | collective-permute-start | bytes 245768 | tf_op jit(solution)/shard_map/ppermute | solution.py:34
  28.2 7.3 %collective-permute-start.3 = (bf16[64,640]{1,0:T(8,128)(2,1)S(1)}, bf16[64,640]{1,0:T(8,128)(2,1)S(1)}, u32[]{:S(2)}, u32[]{:S(2)}) collective-permute-start(bf16[64,640]{1,0:T(8,128)(2,1)S(1)} %constant_dynamic-update-slice_fusion.5), channel_id=1, source_target_pairs={{384,0},{0,128},{128,256},{256,384},{385,1},{1,129},{129,257},{257... | collective-permute-start | bytes 245768 | tf_op jit(solution)/shard_map/ppermute | solution.py:34
  35.5 9.9 %collective-permute-done.2 = bf16[64,640]{1,0:T(8,128)(2,1)S(1)} collective-permute-done((bf16[64,640]{1,0:T(8,128)(2,1)S(1)}, bf16[64,640]{1,0:T(8,128)(2,1)S(1)}, u32[]{:S(2)}, u32[]{:S(2)}) %collective-permute-start.2) | collective-permute-done | bytes 81952 | tf_op jit(solution)/shard_map/ppermute | solution.py:34
  46.2 1.1 reshape.169
  47.2 2.5 convolution_convert_fusion.2
  49.8 6.0 %all-to-all-start.1 = ((bf16[4,64,640]{2,1,0:T(8,128)(2,1)}), bf16[4,64,640]{2,1,0:T(8,128)(2,1)}, u32[]{:S(2)}, u32[]{:S(2)}) async-start(bf16[4,64,640]{2,1,0:T(8,128)(2,1)} %bitcast.154), calls=%async_computation.1 | async-start | bytes 655360 | tf_op jit(solution)/shard_map/all_to_all | solution.py:246
  55.7 6.3 %collective-permute-start = (bf16[64,640]{1,0:T(8,128)(2,1)S(1)}, bf16[64,640]{1,0:T(8,128)(2,1)S(1)}, u32[]{:S(2)}, u32[]{:S(2)}) collective-permute-start(bf16[64,640]{1,0:T(8,128)(2,1)S(1)} %constant_dynamic-slice_fusion), channel_id=1, source_target_pairs={{0,0},{1,128},{2,256},{3,384},{128,1},{129,129},{130,257},{131,385... | collective-permute-start | bytes 245768 | tf_op jit(solution)/shard_map/ppermute | solution.py:38
  63.4 6.5 %collective-permute-start.4 = (bf16[64,128]{0,1:T(8,128)(2,1)S(1)}, bf16[64,128]{0,1:T(8,128)(2,1)S(1)}, u32[]{:S(2)}, u32[]{:S(2)}) collective-permute-start(bf16[64,128]{0,1:T(8,128)(2,1)S(1)} %fusion.38), channel_id=1, source_target_pairs={{0,0},{1,128},{2,256},{3,384},{128,1},{129,129},{130,257},{131,385... | collective-permute-start | bytes 49160 | tf_op jit(solution)/shard_map/ppermute | solution.py:38
  69.9 3.1 %collective-permute-start.12 = (bf16[192,2560]{1,0:T(8,128)(2,1)S(1)}, bf16[192,2560]{1,0:T(8,128)(2,1)}, u32[]{:S(2)}, u32[]{:S(2)}) collective-permute-start(bf16[192,2560]{1,0:T(8,128)(2,1)S(1)} %bitcast.150), channel_id=1, source_target_pairs={{0,1},{1,0},{2,3},{3,2},{4,5},{5,4},{6,7},{7,6},{8,9},{9,8},{10,11... | collective-permute-start | bytes 2949128 | tf_op jit(solution)/shard_map/ppermute | solution.py:38
  73.0 1.1 slice_bitcast_fusion.1
  74.1 2.8 collective-permute-start.10
  76.9 1.0 convert_reduce_fusion.1
  78.7 4.1 %all-to-all-start.2 = ((bf16[4,64,640]{2,1,0:T(8,128)(2,1)}), bf16[4,64,640]{2,1,0:T(8,128)(2,1)}, u32[]{:S(2)}, u32[]{:S(2)}) async-start(bf16[4,64,640]{2,1,0:T(8,128)(2,1)} %broadcast_in_dim.279), calls=%async_computation.2 | async-start | bytes 655360 | tf_op jit(solution)/shard_map/all_to_all | solution.py:59
  82.8 1.1 slice_bitcast_fusion
  83.9 3.3 %collective-permute-start.9 = (bf16[1280,384]{1,0:T(8,128)(2,1)}, bf16[1280,384]{1,0:T(8,128)(2,1)}, u32[]{:S(2)}, u32[]{:S(2)}) collective-permute-start(bf16[1280,384]{1,0:T(8,128)(2,1)} %slice_bitcast_fusion), channel_id=1, source_target_pairs={{0,1},{1,0},{2,3},{3,2},{4,5},{5,4},{6,7},{7,6},{8,9},{9,8},{10,11... | collective-permute-start | bytes 2949128 | tf_op jit(solution)/shard_map/ppermute | solution.py:38
  87.3 1.9 collective-permute-start.7
  89.2 4.9 %collective-permute-start.5 = (bf16[64,128]{0,1:T(8,128)(2,1)S(1)}, bf16[64,128]{0,1:T(8,128)(2,1)S(1)}, u32[]{:S(2)}, u32[]{:S(2)}) collective-permute-start(bf16[64,128]{0,1:T(8,128)(2,1)S(1)} %collective-permute-done.4), channel_id=1, source_target_pairs={{0,3},{1,2},{2,1},{3,0},{4,7},{5,6},{6,5},{7,4},{8,11},{9,10},{10,... | collective-permute-start | bytes 49160 | tf_op jit(solution)/shard_map/ppermute | solution.py:38
  94.2 2.0 collective-permute-done.5
  96.2 26.6 %all-to-all-done.2 = bf16[4,64,640]{2,1,0:T(8,128)(2,1)} async-done(((bf16[4,64,640]{2,1,0:T(8,128)(2,1)}), bf16[4,64,640]{2,1,0:T(8,128)(2,1)}, u32[]{:S(2)}, u32[]{:S(2)}) %all-to-all-start.2) | async-done | bytes 327712 | tf_op jit(solution)/shard_map/all_to_all | solution.py:59
  122.9 1.0 slice_bitcast_fusion.10
  124.1 4.7 %collective-permute-start.6 = (bf16[64,2560]{1,0:T(8,128)(2,1)S(1)}, bf16[64,2560]{1,0:T(8,128)(2,1)S(1)}, u32[]{:S(2)}, u32[]{:S(2)}) collective-permute-start(bf16[64,2560]{1,0:T(8,128)(2,1)S(1)} %get-tuple-element.7), channel_id=1, source_target_pairs={{0,3},{1,2},{2,1},{3,0},{4,7},{5,6},{6,5},{7,4},{8,11},{9,10},{10,... | collective-permute-start | bytes 983048 | tf_op jit(solution)/shard_map/ppermute | solution.py:38
  129.0 4.8 %collective-permute-done.6 = bf16[64,2560]{1,0:T(8,128)(2,1)S(1)} collective-permute-done((bf16[64,2560]{1,0:T(8,128)(2,1)S(1)}, bf16[64,2560]{1,0:T(8,128)(2,1)S(1)}, u32[]{:S(2)}, u32[]{:S(2)}) %collective-permute-start.6) | collective-permute-done | bytes 327712 | tf_op jit(solution)/shard_map/ppermute | solution.py:38
  133.8 22.4 %collective-permute-start.11 = (bf16[640,384]{1,0:T(8,128)(2,1)}, bf16[640,384]{1,0:T(8,128)(2,1)}, u32[]{:S(2)}, u32[]{:S(2)}) collective-permute-start(bf16[640,384]{1,0:T(8,128)(2,1)} %get-tuple-element.8), channel_id=1, source_target_pairs={{0,1},{1,0},{2,3},{3,2},{4,5},{5,4},{6,7},{7,6},{8,9},{9,8},{10,11... | collective-permute-start | bytes 1474568 | tf_op jit(solution)/shard_map/ppermute | solution.py:38
  156.4 1.2 fusion
  157.7 7.3 %all-to-all-start.3 = ((bf16[16,8,2560]{2,1,0:T(8,128)(2,1)}), bf16[16,8,2560]{2,1,0:T(8,128)(2,1)}, u32[]{:S(2)}, u32[]{:S(2)}) async-start(bf16[16,8,2560]{2,1,0:T(8,128)(2,1)} %fusion), calls=%async_computation.3 | async-start | bytes 1310720 | tf_op jit(solution)/shard_map/all_to_all | solution.py:262
  164.9 1.9 collective-permute-start.8
  166.9 2.4 collective-permute-start.14
  169.3 1.9 collective-permute-start.16
  171.2 2.4 collective-permute-start.13
  173.9 2.2 fusion.1
  176.1 7.2 %all-to-all-start.5 = ((bf16[16,8,2560]{2,1,0:T(8,128)(2,1)}), bf16[16,8,2560]{2,1,0:T(8,128)(2,1)}, u32[]{:S(2)}, u32[]{:S(2)}) async-start(bf16[16,8,2560]{2,1,0:T(8,128)(2,1)} %fusion.1), calls=%async_computation.5 | async-start | bytes 1310720 | tf_op jit(solution)/shard_map/all_to_all | solution.py:262
  183.4 1.9 collective-permute-start.15
  186.1 1.3 collective-permute-done.15.refs_10_
  188.1 7.3 %experts.2 = bf16[128,2560]{1,0:T(8,128)(2,1)} custom-call(bf16[128,2560]{1,0:T(8,128)(2,1)} %bitcast.36.rows_ref, bf16[2560,384]{1,0:T(8,128)(2,1)} %bitcast.145, bf16[192,2560]{1,0:T(8,128)(2,1)} %bitcast.148, bf16[2560,384]{1,0:T(8,128)(2,1)} %collective-permute-done.7.refs_2_, bf16[192,2560]{1,0:T(8,128)(2,1)} %collective-permute-done.8.refs_3_, ...), custom_call_target="tpu_custom_call" | custom-call | tf_op jit(solution)/shard_map/experts/pallas_call | solution.py:164
  195.4 7.2 %all-to-all-start.4 = ((bf16[16,8,2560]{2,1,0:T(8,128)(2,1)}), bf16[16,8,2560]{2,1,0:T(8,128)(2,1)S(1)}, u32[]{:S(2)}, u32[]{:S(2)}) async-start(bf16[16,8,2560]{2,1,0:T(8,128)(2,1)} %bitcast.153), calls=%async_computation.4 | async-start | bytes 1310720 | tf_op jit(solution)/shard_map/all_to_all | solution.py:268
  202.7 7.3 %experts.3 = bf16[128,2560]{1,0:T(8,128)(2,1)} custom-call(bf16[128,2560]{1,0:T(8,128)(2,1)} %bitcast.44.rows_ref, bf16[2560,384]{1,0:T(8,128)(2,1)} %bitcast.146, bf16[192,2560]{1,0:T(8,128)(2,1)} %bitcast.149, bf16[2560,384]{1,0:T(8,128)(2,1)} %collective-permute-done.7.refs_2_, bf16[192,2560]{1,0:T(8,128)(2,1)} %collective-permute-done.8.refs_3_, ...), custom_call_target="tpu_custom_call" | custom-call | tf_op jit(solution)/shard_map/experts/pallas_call | solution.py:164
  210.0 4.5 %all-to-all-done.4 = bf16[16,8,2560]{2,1,0:T(8,128)(2,1)S(1)} async-done(((bf16[16,8,2560]{2,1,0:T(8,128)(2,1)}), bf16[16,8,2560]{2,1,0:T(8,128)(2,1)S(1)}, u32[]{:S(2)}, u32[]{:S(2)}) %all-to-all-start.4) | async-done | bytes 655392 | tf_op jit(solution)/shard_map/all_to_all | solution.py:268
  214.5 4.8 %all-to-all-start.6 = ((bf16[16,8,2560]{2,1,0:T(8,128)(2,1)}), bf16[16,8,2560]{2,1,0:T(8,128)(2,1)S(1)}, u32[]{:S(2)}, u32[]{:S(2)}) async-start(bf16[16,8,2560]{2,1,0:T(8,128)(2,1)} %bitcast.152), calls=%async_computation.6 | async-start | bytes 1310720 | tf_op jit(solution)/shard_map/all_to_all | solution.py:270
  220.1 4.5 %collective-permute-start.17 = (bf16[64,2560]{1,0:T(8,128)(2,1)S(1)}, bf16[64,2560]{1,0:T(8,128)(2,1)S(1)}, u32[]{:S(2)}, u32[]{:S(2)}) collective-permute-start(bf16[64,2560]{1,0:T(8,128)(2,1)S(1)} %fusion.2), channel_id=1, source_target_pairs={{0,3},{1,2},{2,1},{3,0},{4,7},{5,6},{6,5},{7,4},{8,11},{9,10},{10,... | collective-permute-start | bytes 983048 | tf_op jit(solution)/shard_map/ppermute | solution.py:38
  224.7 5.5 %all-to-all-done.6 = bf16[16,8,2560]{2,1,0:T(8,128)(2,1)S(1)} async-done(((bf16[16,8,2560]{2,1,0:T(8,128)(2,1)}), bf16[16,8,2560]{2,1,0:T(8,128)(2,1)S(1)}, u32[]{:S(2)}, u32[]{:S(2)}) %all-to-all-start.6) | async-done | bytes 655392 | tf_op jit(solution)/shard_map/all_to_all | solution.py:270
  230.6 6.9 %collective-permute-done.17 = bf16[64,2560]{1,0:T(8,128)(2,1)S(1)} collective-permute-done((bf16[64,2560]{1,0:T(8,128)(2,1)S(1)}, bf16[64,2560]{1,0:T(8,128)(2,1)S(1)}, u32[]{:S(2)}, u32[]{:S(2)}) %collective-permute-start.17) | collective-permute-done | bytes 327712 | tf_op jit(solution)/shard_map/ppermute | solution.py:38
  238.7 8.1 %all-to-all-start.7 = ((bf16[4,64,640]{2,1,0:T(8,128)(2,1)}), bf16[4,64,640]{2,1,0:T(8,128)(2,1)S(1)}, u32[]{:S(2)}, u32[]{:S(2)}) async-start(bf16[4,64,640]{2,1,0:T(8,128)(2,1)} %pad_maximum_fusion.2), calls=%async_computation.7 | async-start | bytes 655360 | tf_op jit(solution)/shard_map/all_to_all | solution.py:276
  247.2 17.1 %all-to-all-done.7 = bf16[4,64,640]{2,1,0:T(8,128)(2,1)S(1)} async-done(((bf16[4,64,640]{2,1,0:T(8,128)(2,1)}), bf16[4,64,640]{2,1,0:T(8,128)(2,1)S(1)}, u32[]{:S(2)}, u32[]{:S(2)}) %all-to-all-start.7) | async-done | bytes 327712 | tf_op jit(solution)/shard_map/all_to_all | solution.py:276
  264.4 1.9 collective-permute-start.18
  267.1 10.5 %collective-permute-done.18 = bf16[64,640]{1,0:T(8,128)(2,1)S(1)} collective-permute-done((bf16[64,640]{1,0:T(8,128)(2,1)S(1)}, bf16[64,640]{1,0:T(8,128)(2,1)S(1)}, u32[]{:S(2)}, u32[]{:S(2)}) %collective-permute-start.18) | collective-permute-done | bytes 81952 | tf_op jit(solution)/shard_map/ppermute | solution.py:38
  (110 shorter events, 11.2 us)
Async XLA Ops:
  0.6 55.1 %copy-start = (bf16[64,2560]{1,0:T(8,128)(2,1)S(1)}, bf16[64,2560]{1,0:T(8,128)(2,1)}, u32[]{:S(2)}) copy-start(bf16[64,2560]{1,0:T(8,128)(2,1)} %param.13) | copy-start | bytes 983044
  0.6 9.5 %copy-start.12 = (s32[1,4]{1,0:T(1,128)S(1)}, s32[1,4]{1,0:T(1,128)}, u32[]{:S(2)}) copy-start(s32[1,4]{1,0:T(1,128)} %param.14) | copy-start | bytes 52
  0.7 10.5 %copy-start.5 = (bf16[64,640]{1,0:T(8,128)(2,1)S(1)}, bf16[64,640]{1,0:T(8,128)(2,1)}, u32[]{:S(2)}) copy-start(bf16[64,640]{1,0:T(8,128)(2,1)} %param.11) | copy-start | bytes 245764
  0.7 10.6 %copy-start.6 = (bf16[64,256]{1,0:T(8,128)(2,1)S(1)}, bf16[64,256]{1,0:T(8,128)(2,1)}, u32[]{:S(2)}) copy-start(bf16[64,256]{1,0:T(8,128)(2,1)} %param.12) | copy-start | bytes 98308
  2.5 43.6 %all-to-all-start = ((bf16[32,20,640]{2,1,0:T(8,128)(2,1)}), bf16[32,20,640]{2,1,0:T(8,128)(2,1)S(1)}, u32[]{:S(2)}, u32[]{:S(2)}) async-start(bf16[32,20,640]{2,1,0:T(8,128)(2,1)} %broadcast_in_dim.265), calls=%async_computation | async-start | bytes 1966080 | tf_op jit(solution)/shard_map/all_to_all | solution.py:59
  10.3 0.5 copy-start.14
  10.9 0.8 copy-start.8
  11.8 23.8 %collective-permute-start.1 = (bf16[64,640]{1,0:T(8,128)(2,1)S(1)}, bf16[64,640]{1,0:T(8,128)(2,1)S(1)}, u32[]{:S(2)}, u32[]{:S(2)}) collective-permute-start(bf16[64,640]{1,0:T(8,128)(2,1)S(1)} %constant_dynamic-update-slice_fusion.5), channel_id=1, source_target_pairs={{128,0},{256,128},{384,256},{0,384},{129,1},{257,129},{385,257},{1... | collective-permute-start | bytes 245768 | tf_op jit(solution)/shard_map/ppermute | solution.py:34
  22.7 22.7 %collective-permute-start.2 = (bf16[64,640]{1,0:T(8,128)(2,1)S(1)}, bf16[64,640]{1,0:T(8,128)(2,1)S(1)}, u32[]{:S(2)}, u32[]{:S(2)}) collective-permute-start(bf16[64,640]{1,0:T(8,128)(2,1)S(1)} %constant_dynamic-update-slice_fusion.5), channel_id=1, source_target_pairs={{256,0},{384,128},{0,256},{128,384},{257,1},{385,129},{1,257},{129... | collective-permute-start | bytes 245768 | tf_op jit(solution)/shard_map/ppermute | solution.py:34
  28.2 17.3 %collective-permute-start.3 = (bf16[64,640]{1,0:T(8,128)(2,1)S(1)}, bf16[64,640]{1,0:T(8,128)(2,1)S(1)}, u32[]{:S(2)}, u32[]{:S(2)}) collective-permute-start(bf16[64,640]{1,0:T(8,128)(2,1)S(1)} %constant_dynamic-update-slice_fusion.5), channel_id=1, source_target_pairs={{384,0},{0,128},{128,256},{256,384},{385,1},{1,129},{129,257},{257... | collective-permute-start | bytes 245768 | tf_op jit(solution)/shard_map/ppermute | solution.py:34
  47.2 22.7 %copy-start.2 = (bf16[1,192,2560]{2,1,0:T(8,128)(2,1)S(1)}, bf16[1,192,2560]{2,1,0:T(8,128)(2,1)}, u32[]{:S(2)}) copy-start(bf16[1,192,2560]{2,1,0:T(8,128)(2,1)} %param.21) | copy-start | bytes 2949124
  47.2 25.8 %copy-start.1 = (bf16[1,2560,384]{2,1,0:T(8,128)(2,1)S(1)}, bf16[1,2560,384]{2,1,0:T(8,128)(2,1)}, u32[]{:S(2)}) copy-start(bf16[1,2560,384]{2,1,0:T(8,128)(2,1)} %param.20) | copy-start | bytes 5898244
  49.8 27.1 %all-to-all-start.1 = ((bf16[4,64,640]{2,1,0:T(8,128)(2,1)}), bf16[4,64,640]{2,1,0:T(8,128)(2,1)}, u32[]{:S(2)}, u32[]{:S(2)}) async-start(bf16[4,64,640]{2,1,0:T(8,128)(2,1)} %bitcast.154), calls=%async_computation.1 | async-start | bytes 655360 | tf_op jit(solution)/shard_map/all_to_all | solution.py:246
  55.7 22.2 %collective-permute-start = (bf16[64,640]{1,0:T(8,128)(2,1)S(1)}, bf16[64,640]{1,0:T(8,128)(2,1)S(1)}, u32[]{:S(2)}, u32[]{:S(2)}) collective-permute-start(bf16[64,640]{1,0:T(8,128)(2,1)S(1)} %constant_dynamic-slice_fusion), channel_id=1, source_target_pairs={{0,0},{1,128},{2,256},{3,384},{128,1},{129,129},{130,257},{131,385... | collective-permute-start | bytes 245768 | tf_op jit(solution)/shard_map/ppermute | solution.py:38
  63.4 25.8 %collective-permute-start.4 = (bf16[64,128]{0,1:T(8,128)(2,1)S(1)}, bf16[64,128]{0,1:T(8,128)(2,1)S(1)}, u32[]{:S(2)}, u32[]{:S(2)}) collective-permute-start(bf16[64,128]{0,1:T(8,128)(2,1)S(1)} %fusion.38), channel_id=1, source_target_pairs={{0,0},{1,128},{2,256},{3,384},{128,1},{129,129},{130,257},{131,385... | collective-permute-start | bytes 49160 | tf_op jit(solution)/shard_map/ppermute | solution.py:38
  69.9 99.4 %collective-permute-start.12 = (bf16[192,2560]{1,0:T(8,128)(2,1)S(1)}, bf16[192,2560]{1,0:T(8,128)(2,1)}, u32[]{:S(2)}, u32[]{:S(2)}) collective-permute-start(bf16[192,2560]{1,0:T(8,128)(2,1)S(1)} %bitcast.150), channel_id=1, source_target_pairs={{0,1},{1,0},{2,3},{3,2},{4,5},{5,4},{6,7},{7,6},{8,9},{9,8},{10,11... | collective-permute-start | bytes 2949128 | tf_op jit(solution)/shard_map/ppermute | solution.py:38
  74.1 90.8 %collective-permute-start.10 = (bf16[640,384]{1,0:T(8,128)(2,1)}, bf16[640,384]{1,0:T(8,128)(2,1)}, u32[]{:S(2)}, u32[]{:S(2)}) collective-permute-start(bf16[640,384]{1,0:T(8,128)(2,1)} %get-tuple-element.9), channel_id=1, source_target_pairs={{0,1},{1,0},{2,3},{3,2},{4,5},{5,4},{6,7},{7,6},{8,9},{9,8},{10,11... | collective-permute-start | bytes 1474568 | tf_op jit(solution)/shard_map/ppermute | solution.py:38
  78.7 44.1 %all-to-all-start.2 = ((bf16[4,64,640]{2,1,0:T(8,128)(2,1)}), bf16[4,64,640]{2,1,0:T(8,128)(2,1)}, u32[]{:S(2)}, u32[]{:S(2)}) async-start(bf16[4,64,640]{2,1,0:T(8,128)(2,1)} %broadcast_in_dim.279), calls=%async_computation.2 | async-start | bytes 655360 | tf_op jit(solution)/shard_map/all_to_all | solution.py:59
  82.8 73.6 %copy-start.7 = (f32[2560]{0:T(1024)S(1)}, f32[2560]{0:T(1024)}, u32[]{:S(2)}) copy-start(f32[2560]{0:T(1024)} %param.17) | copy-start | bytes 30724
  83.9 87.3 %collective-permute-start.9 = (bf16[1280,384]{1,0:T(8,128)(2,1)}, bf16[1280,384]{1,0:T(8,128)(2,1)}, u32[]{:S(2)}, u32[]{:S(2)}) collective-permute-start(bf16[1280,384]{1,0:T(8,128)(2,1)} %slice_bitcast_fusion), channel_id=1, source_target_pairs={{0,1},{1,0},{2,3},{3,2},{4,5},{5,4},{6,7},{7,6},{8,9},{9,8},{10,11... | collective-permute-start | bytes 2949128 | tf_op jit(solution)/shard_map/ppermute | solution.py:38
  87.3 100.1 %collective-permute-start.7 = (bf16[2560,384]{1,0:T(8,128)(2,1)S(1)}, bf16[2560,384]{1,0:T(8,128)(2,1)}, u32[]{:S(2)}, u32[]{:S(2)}) collective-permute-start(bf16[2560,384]{1,0:T(8,128)(2,1)S(1)} %bitcast.147), channel_id=1, source_target_pairs={{0,4},{4,0},{1,5},{5,1},{2,6},{6,2},{3,7},{7,3},{8,12},{12,8},{9,1... | collective-permute-start | bytes 5898248 | tf_op jit(solution)/shard_map/ppermute | solution.py:38
  89.2 34.8 %copy-start.10 = (bf16[64,128]{0,1:T(8,128)(2,1)}, bf16[64,128]{0,1:T(8,128)(2,1)S(1)}, u32[]{:S(2)}) copy-start(bf16[64,128]{0,1:T(8,128)(2,1)S(1)} %collective-permute-done.4) | copy-start | bytes 49156
  89.2 7.0 %collective-permute-start.5 = (bf16[64,128]{0,1:T(8,128)(2,1)S(1)}, bf16[64,128]{0,1:T(8,128)(2,1)S(1)}, u32[]{:S(2)}, u32[]{:S(2)}) collective-permute-start(bf16[64,128]{0,1:T(8,128)(2,1)S(1)} %collective-permute-done.4), channel_id=1, source_target_pairs={{0,3},{1,2},{2,1},{3,0},{4,7},{5,6},{6,5},{7,4},{8,11},{9,10},{10,... | collective-permute-start | bytes 49160 | tf_op jit(solution)/shard_map/ppermute | solution.py:38
  124.1 9.8 %copy-start.4 = (bf16[64,2560]{1,0:T(8,128)(2,1)}, bf16[64,2560]{1,0:T(8,128)(2,1)S(1)}, u32[]{:S(2)}) copy-start(bf16[64,2560]{1,0:T(8,128)(2,1)S(1)} %get-tuple-element.7) | copy-start | bytes 983044
  124.1 9.7 %collective-permute-start.6 = (bf16[64,2560]{1,0:T(8,128)(2,1)S(1)}, bf16[64,2560]{1,0:T(8,128)(2,1)S(1)}, u32[]{:S(2)}, u32[]{:S(2)}) collective-permute-start(bf16[64,2560]{1,0:T(8,128)(2,1)S(1)} %get-tuple-element.7), channel_id=1, source_target_pairs={{0,3},{1,2},{2,1},{3,0},{4,7},{5,6},{6,5},{7,4},{8,11},{9,10},{10,... | collective-permute-start | bytes 983048 | tf_op jit(solution)/shard_map/ppermute | solution.py:38
  133.8 33.0 %collective-permute-start.11 = (bf16[640,384]{1,0:T(8,128)(2,1)}, bf16[640,384]{1,0:T(8,128)(2,1)}, u32[]{:S(2)}, u32[]{:S(2)}) collective-permute-start(bf16[640,384]{1,0:T(8,128)(2,1)} %get-tuple-element.8), channel_id=1, source_target_pairs={{0,1},{1,0},{2,3},{3,2},{4,5},{5,4},{6,7},{7,6},{8,9},{9,8},{10,11... | collective-permute-start | bytes 1474568 | tf_op jit(solution)/shard_map/ppermute | solution.py:38
  157.7 18.5 %all-to-all-start.3 = ((bf16[16,8,2560]{2,1,0:T(8,128)(2,1)}), bf16[16,8,2560]{2,1,0:T(8,128)(2,1)}, u32[]{:S(2)}, u32[]{:S(2)}) async-start(bf16[16,8,2560]{2,1,0:T(8,128)(2,1)} %fusion), calls=%async_computation.3 | async-start | bytes 1310720 | tf_op jit(solution)/shard_map/all_to_all | solution.py:262
  164.9 22.4 %collective-permute-start.8 = (bf16[192,2560]{1,0:T(8,128)(2,1)S(1)}, bf16[192,2560]{1,0:T(8,128)(2,1)}, u32[]{:S(2)}, u32[]{:S(2)}) collective-permute-start(bf16[192,2560]{1,0:T(8,128)(2,1)S(1)} %bitcast.151), channel_id=1, source_target_pairs={{0,4},{4,0},{1,5},{5,1},{2,6},{6,2},{3,7},{7,3},{8,12},{12,8},{9,1... | collective-permute-start | bytes 2949128 | tf_op jit(solution)/shard_map/ppermute | solution.py:38
  166.9 16.5 %collective-permute-start.14 = (bf16[640,384]{1,0:T(8,128)(2,1)}, bf16[640,384]{1,0:T(8,128)(2,1)}, u32[]{:S(2)}, u32[]{:S(2)}) collective-permute-start(bf16[640,384]{1,0:T(8,128)(2,1)} %collective-permute-done.10.refs_5_), channel_id=1, source_target_pairs={{0,4},{4,0},{1,5},{5,1},{2,6},{6,2},{3,7},{7,3},{8,12},{12,8},{9,1... | collective-permute-start | bytes 1474568 | tf_op jit(solution)/shard_map/ppermute | solution.py:38
  169.3 18.0 %collective-permute-start.16 = (bf16[192,2560]{1,0:T(8,128)(2,1)}, bf16[192,2560]{1,0:T(8,128)(2,1)}, u32[]{:S(2)}, u32[]{:S(2)}) collective-permute-start(bf16[192,2560]{1,0:T(8,128)(2,1)} %collective-permute-done.12.refs_7_), channel_id=1, source_target_pairs={{0,4},{4,0},{1,5},{5,1},{2,6},{6,2},{3,7},{7,3},{8,12},{12,8},{9,1... | collective-permute-start | bytes 2949128 | tf_op jit(solution)/shard_map/ppermute | solution.py:38
  171.2 16.1 %collective-permute-start.13 = (bf16[1280,384]{1,0:T(8,128)(2,1)}, bf16[1280,384]{1,0:T(8,128)(2,1)}, u32[]{:S(2)}, u32[]{:S(2)}) collective-permute-start(bf16[1280,384]{1,0:T(8,128)(2,1)} %collective-permute-done.9.refs_4_), channel_id=1, source_target_pairs={{0,4},{4,0},{1,5},{5,1},{2,6},{6,2},{3,7},{7,3},{8,12},{12,8},{9,1... | collective-permute-start | bytes 2949128 | tf_op jit(solution)/shard_map/ppermute | solution.py:38
  176.1 19.3 %all-to-all-start.5 = ((bf16[16,8,2560]{2,1,0:T(8,128)(2,1)}), bf16[16,8,2560]{2,1,0:T(8,128)(2,1)}, u32[]{:S(2)}, u32[]{:S(2)}) async-start(bf16[16,8,2560]{2,1,0:T(8,128)(2,1)} %fusion.1), calls=%async_computation.5 | async-start | bytes 1310720 | tf_op jit(solution)/shard_map/all_to_all | solution.py:262
  183.4 4.0 %collective-permute-start.15 = (bf16[640,384]{1,0:T(8,128)(2,1)}, bf16[640,384]{1,0:T(8,128)(2,1)S(1)}, u32[]{:S(2)}, u32[]{:S(2)}) collective-permute-start(bf16[640,384]{1,0:T(8,128)(2,1)} %collective-permute-done.11.refs_6_), channel_id=1, source_target_pairs={{0,4},{4,0},{1,5},{5,1},{2,6},{6,2},{3,7},{7,3},{8,12},{12,8},{9,1... | collective-permute-start | bytes 1474568 | tf_op jit(solution)/shard_map/ppermute | solution.py:38
  187.3 0.8 copy-start.3
  195.4 19.1 %all-to-all-start.4 = ((bf16[16,8,2560]{2,1,0:T(8,128)(2,1)}), bf16[16,8,2560]{2,1,0:T(8,128)(2,1)S(1)}, u32[]{:S(2)}, u32[]{:S(2)}) async-start(bf16[16,8,2560]{2,1,0:T(8,128)(2,1)} %bitcast.153), calls=%async_computation.4 | async-start | bytes 1310720 | tf_op jit(solution)/shard_map/all_to_all | solution.py:268
  214.5 15.7 %all-to-all-start.6 = ((bf16[16,8,2560]{2,1,0:T(8,128)(2,1)}), bf16[16,8,2560]{2,1,0:T(8,128)(2,1)S(1)}, u32[]{:S(2)}, u32[]{:S(2)}) async-start(bf16[16,8,2560]{2,1,0:T(8,128)(2,1)} %bitcast.152), calls=%async_computation.6 | async-start | bytes 1310720 | tf_op jit(solution)/shard_map/all_to_all | solution.py:270
  220.1 17.3 %collective-permute-start.17 = (bf16[64,2560]{1,0:T(8,128)(2,1)S(1)}, bf16[64,2560]{1,0:T(8,128)(2,1)S(1)}, u32[]{:S(2)}, u32[]{:S(2)}) collective-permute-start(bf16[64,2560]{1,0:T(8,128)(2,1)S(1)} %fusion.2), channel_id=1, source_target_pairs={{0,3},{1,2},{2,1},{3,0},{4,7},{5,6},{6,5},{7,4},{8,11},{9,10},{10,... | collective-permute-start | bytes 983048 | tf_op jit(solution)/shard_map/ppermute | solution.py:38
  237.5 9.3 %copy-start.11 = (s32[1,4,2]{1,2,0:T(2,128)S(1)}, s32[1,4,2]{1,2,0:T(2,128)}, u32[]{:S(2)}) copy-start(s32[1,4,2]{1,2,0:T(2,128)} %param.15) | copy-start | bytes 100
  237.5 9.5 %copy-start.13 = (s32[1,4]{1,0:T(1,128)S(1)}, s32[1,4]{1,0:T(1,128)}, u32[]{:S(2)}) copy-start(s32[1,4]{1,0:T(1,128)} %param.14) | copy-start | bytes 52
  237.5 9.5 %copy-start.15 = (s32[4,1]{0,1:T(1,128)S(1)}, s32[4,1]{0,1:T(1,128)}, u32[]{:S(2)}) copy-start(s32[4,1]{0,1:T(1,128)} %copy-done.14) | copy-start | bytes 52
  237.5 9.5 %copy-start.9 = (s32[64]{0:T(128)S(1)}, s32[64]{0:T(128)}, u32[]{:S(2)}) copy-start(s32[64]{0:T(128)} %copy-done.8) | copy-start | bytes 772
  238.7 25.6 %all-to-all-start.7 = ((bf16[4,64,640]{2,1,0:T(8,128)(2,1)}), bf16[4,64,640]{2,1,0:T(8,128)(2,1)S(1)}, u32[]{:S(2)}, u32[]{:S(2)}) async-start(bf16[4,64,640]{2,1,0:T(8,128)(2,1)} %pad_maximum_fusion.2), calls=%async_computation.7 | async-start | bytes 655360 | tf_op jit(solution)/shard_map/all_to_all | solution.py:276
  264.4 13.3 %collective-permute-start.18 = (bf16[64,640]{1,0:T(8,128)(2,1)S(1)}, bf16[64,640]{1,0:T(8,128)(2,1)S(1)}, u32[]{:S(2)}, u32[]{:S(2)}) collective-permute-start(bf16[64,640]{1,0:T(8,128)(2,1)S(1)} %add_convert_fusion.1), channel_id=1, source_target_pairs={{0,0},{1,128},{2,256},{3,384},{128,1},{129,129},{130,257},{131,385... | collective-permute-start | bytes 245768 | tf_op jit(solution)/shard_map/ppermute | solution.py:38

commit v5 on v4

--- a/solution.py
+++ b/solution.py
@@ -203,8 +203,7 @@
     top = expert_choice.shape[1]
     gate_up_own, down_own = gate_up[0], down[0]
 
-    cuts = (0, 2 * share, 3 * share, 4 * share)
-    slices = [gate_up_own[a:b] for a, b in zip(cuts, cuts[1:])] + [down_own]
+    slices = [gate_up_own[i * share : (i + 1) * share] for i in range(4)] + [down_own]
     pair = [swap_units(value) for value in slices]
 
     projection = spread_to_all(out_weight.T, ("y", "x", "c"), 2 * planes)
@@ -239,8 +238,8 @@
     cross = [swap_cores(value) for value in pair]
     core_gate_up = swap_cores(gate_up_own)
     core_down = swap_cores(down_own)
-    gate_ups = [[gate_up_own], [core_gate_up], pair[:3], cross[:3]]
-    downs = [[down_own], [core_down], pair[3:], cross[3:]]
+    gate_ups = [[gate_up_own], [core_gate_up], pair[:4], cross[:4]]
+    downs = [[down_own], [core_down], pair[4:], cross[4:]]
 
     partial = dot(contexts, projection, ((1,), (1,))).astype(BF16)
     partial = lax.all_to_all(

time: 280 us -> 287 us (1.025)
  the two profiles are of different devices: /device:TPU:66 before, /device:TPU:64 now
where the time goes in v5:
time: 287 us; the launch traced here: 285 us
  starting transfers between devices  168 us (59%)
  waiting for transfers between devices  82.3 us (29%)
  Pallas kernels  14.4 us (5%)
  matrix products  9.23 us (3%)
  local copies, waits for them, and re-layouts  7.12 us (2%)
    ppermute x18, starting transfers between devices, swapped(): return lax.ppermute(value, axis, [(i, mate(i)) for i in range(size)])  96 us
    ppermute x18, waiting for transfers between devices, swapped(): return lax.ppermute(value, axis, [(i, mate(i)) for i in range(size)])  35 us
    ppermute x3, starting transfers between devices, from_ahead(): lax.ppermute(value, axis, [((i + step) % size, i) for i in range(size)])  23.7 us
    all_to_all x1, waiting for transfers between devices, layer(): gathered = lax.all_to_all(columns, 'zh', 0, 0, tiled=True)  17.4 us
    pallas_call x2, Pallas kernels, experts_of(): pl.pallas_call(functools.partial(experts_kernel, layout), out_shape=jax.S...  14.4 us
    all_to_all x2, starting transfers between devices, sent(): return (lax.all_to_all(rows, PLANE, 0, 0, tiled=True), parts)  13.9 us
    all_to_all x2, starting transfers between devices, spread_to_all(): return lax.all_to_all(copies, axis, 0, 0, tiled=True)  11.4 us
    ppermute x3, waiting for transfers between devices, from_ahead(): lax.ppermute(value, axis, [((i + step) % size, i) for i in range(size)])  10.3 us
  transfers between devices with their start and end apart: 29, of which 13 were waited for; matrix products, arithmetic and copies ran while one was open for 5% of the time, Pallas kernels for 5%

profile of v5, /device:TPU:64, one launch (start us, length us, event | category | flops | bytes accessed | tf_op | source)
XLA Modules:
  0.0 285.1 jit_solution(14261281081504469985)
XLA Ops:
  0.7 1.8 broadcast_in_dim.265
  2.5 7.3 %all-to-all-start = ((bf16[32,20,640]{2,1,0:T(8,128)(2,1)}), bf16[32,20,640]{2,1,0:T(8,128)(2,1)S(1)}, u32[]{:S(2)}, u32[]{:S(2)}) async-start(bf16[32,20,640]{2,1,0:T(8,128)(2,1)} %broadcast_in_dim.265), calls=%async_computation | async-start | bytes 1966080 | tf_op jit(solution)/shard_map/all_to_all | solution.py:59
  10.9 10.9 %collective-permute-start.1 = (bf16[64,640]{1,0:T(8,128)(2,1)S(1)}, bf16[64,640]{1,0:T(8,128)(2,1)S(1)}, u32[]{:S(2)}, u32[]{:S(2)}) collective-permute-start(bf16[64,640]{1,0:T(8,128)(2,1)S(1)} %constant_dynamic-update-slice_fusion.5), channel_id=1, source_target_pairs={{128,0},{256,128},{384,256},{0,384},{129,1},{257,129},{385,257},{1... | collective-permute-start | bytes 245768 | tf_op jit(solution)/shard_map/ppermute | solution.py:34
  21.9 5.4 %collective-permute-start.2 = (bf16[64,640]{1,0:T(8,128)(2,1)S(1)}, bf16[64,640]{1,0:T(8,128)(2,1)S(1)}, u32[]{:S(2)}, u32[]{:S(2)}) collective-permute-start(bf16[64,640]{1,0:T(8,128)(2,1)S(1)} %constant_dynamic-update-slice_fusion.5), channel_id=1, source_target_pairs={{256,0},{384,128},{0,256},{128,384},{257,1},{385,129},{1,257},{129... | collective-permute-start | bytes 245768 | tf_op jit(solution)/shard_map/ppermute | solution.py:34
  27.3 7.3 %collective-permute-start.3 = (bf16[64,640]{1,0:T(8,128)(2,1)S(1)}, bf16[64,640]{1,0:T(8,128)(2,1)S(1)}, u32[]{:S(2)}, u32[]{:S(2)}) collective-permute-start(bf16[64,640]{1,0:T(8,128)(2,1)S(1)} %constant_dynamic-update-slice_fusion.5), channel_id=1, source_target_pairs={{384,0},{0,128},{128,256},{256,384},{385,1},{1,129},{129,257},{257... | collective-permute-start | bytes 245768 | tf_op jit(solution)/shard_map/ppermute | solution.py:34
  34.7 10.3 %collective-permute-done.2 = bf16[64,640]{1,0:T(8,128)(2,1)S(1)} collective-permute-done((bf16[64,640]{1,0:T(8,128)(2,1)S(1)}, bf16[64,640]{1,0:T(8,128)(2,1)S(1)}, u32[]{:S(2)}, u32[]{:S(2)}) %collective-permute-start.2) | collective-permute-done | bytes 81952 | tf_op jit(solution)/shard_map/ppermute | solution.py:34
  45.3 1.2 convolution_convert_fusion.2
  46.5 5.7 %all-to-all-start.1 = ((bf16[4,64,640]{2,1,0:T(8,128)(2,1)}), bf16[4,64,640]{2,1,0:T(8,128)(2,1)S(1)}, u32[]{:S(2)}, u32[]{:S(2)}) async-start(bf16[4,64,640]{2,1,0:T(8,128)(2,1)} %bitcast.12), calls=%async_computation.1 | async-start | bytes 655360 | tf_op jit(solution)/shard_map/all_to_all | solution.py:245
  52.2 6.4 %collective-permute-start = (bf16[64,640]{1,0:T(8,128)(2,1)S(1)}, bf16[64,640]{1,0:T(8,128)(2,1)S(1)}, u32[]{:S(2)}, u32[]{:S(2)}) collective-permute-start(bf16[64,640]{1,0:T(8,128)(2,1)S(1)} %constant_dynamic-slice_fusion), channel_id=1, source_target_pairs={{0,0},{1,128},{2,256},{3,384},{128,1},{129,129},{130,257},{131,385... | collective-permute-start | bytes 245768 | tf_op jit(solution)/shard_map/ppermute | solution.py:38
  58.7 6.4 %collective-permute-start.4 = (bf16[64,128]{0,1:T(8,128)(2,1)S(1)}, bf16[64,128]{0,1:T(8,128)(2,1)S(1)}, u32[]{:S(2)}, u32[]{:S(2)}) collective-permute-start(bf16[64,128]{0,1:T(8,128)(2,1)S(1)} %fusion.38), channel_id=1, source_target_pairs={{0,0},{1,128},{2,256},{3,384},{128,1},{129,129},{130,257},{131,385... | collective-permute-start | bytes 49160 | tf_op jit(solution)/shard_map/ppermute | solution.py:38
  65.1 3.2 %collective-permute-done = bf16[64,640]{1,0:T(8,128)(2,1)S(1)} collective-permute-done((bf16[64,640]{1,0:T(8,128)(2,1)S(1)}, bf16[64,640]{1,0:T(8,128)(2,1)S(1)}, u32[]{:S(2)}, u32[]{:S(2)}) %collective-permute-start) | collective-permute-done | bytes 81952 | tf_op jit(solution)/shard_map/ppermute | solution.py:38
  69.1 4.1 %all-to-all-start.2 = ((bf16[4,64,640]{2,1,0:T(8,128)(2,1)}), bf16[4,64,640]{2,1,0:T(8,128)(2,1)}, u32[]{:S(2)}, u32[]{:S(2)}) async-start(bf16[4,64,640]{2,1,0:T(8,128)(2,1)} %broadcast_in_dim.279), calls=%async_computation.2 | async-start | bytes 655360 | tf_op jit(solution)/shard_map/all_to_all | solution.py:59
  73.2 1.3 slice_bitcast_fusion
  74.5 3.4 %collective-permute-start.9 = (bf16[640,384]{1,0:T(8,128)(2,1)}, bf16[640,384]{1,0:T(8,128)(2,1)}, u32[]{:S(2)}, u32[]{:S(2)}) collective-permute-start(bf16[640,384]{1,0:T(8,128)(2,1)} %get-tuple-element.10), channel_id=1, source_target_pairs={{0,1},{1,0},{2,3},{3,2},{4,5},{5,4},{6,7},{7,6},{8,9},{9,8},{10,11... | collective-permute-start | bytes 1474568 | tf_op jit(solution)/shard_map/ppermute | solution.py:38
  77.9 2.6 collective-permute-start.10
  80.5 3.2 %collective-permute-start.13 = (bf16[192,2560]{1,0:T(8,128)(2,1)S(1)}, bf16[192,2560]{1,0:T(8,128)(2,1)}, u32[]{:S(2)}, u32[]{:S(2)}) collective-permute-start(bf16[192,2560]{1,0:T(8,128)(2,1)S(1)} %bitcast.152), channel_id=1, source_target_pairs={{0,1},{1,0},{2,3},{3,2},{4,5},{5,4},{6,7},{7,6},{8,9},{9,8},{10,11... | collective-permute-start | bytes 2949128 | tf_op jit(solution)/shard_map/ppermute | solution.py:38
  83.8 1.9 collective-permute-start.7
  86.3 5.9 %collective-permute-start.5 = (bf16[64,128]{0,1:T(8,128)(2,1)S(1)}, bf16[64,128]{0,1:T(8,128)(2,1)S(1)}, u32[]{:S(2)}, u32[]{:S(2)}) collective-permute-start(bf16[64,128]{0,1:T(8,128)(2,1)S(1)} %collective-permute-done.4), channel_id=1, source_target_pairs={{0,3},{1,2},{2,1},{3,0},{4,7},{5,6},{6,5},{7,4},{8,11},{9,10},{10,... | collective-permute-start | bytes 49160 | tf_op jit(solution)/shard_map/ppermute | solution.py:38
  92.2 2.0 collective-permute-done.5
  94.3 3.8 %all-to-all-done.2 = bf16[4,64,640]{2,1,0:T(8,128)(2,1)} async-done(((bf16[4,64,640]{2,1,0:T(8,128)(2,1)}), bf16[4,64,640]{2,1,0:T(8,128)(2,1)}, u32[]{:S(2)}, u32[]{:S(2)}) %all-to-all-start.2) | async-done | bytes 327712 | tf_op jit(solution)/shard_map/all_to_all | solution.py:59
  99.3 1.9 collective-permute-start.6
  102.2 6.1 %collective-permute-done.6 = bf16[64,2560]{1,0:T(8,128)(2,1)S(1)} collective-permute-done((bf16[64,2560]{1,0:T(8,128)(2,1)S(1)}, bf16[64,2560]{1,0:T(8,128)(2,1)S(1)}, u32[]{:S(2)}, u32[]{:S(2)}) %collective-permute-start.6) | collective-permute-done | bytes 327712 | tf_op jit(solution)/shard_map/ppermute | solution.py:38
  108.3 44.2 %collective-permute-start.11 = (bf16[640,384]{1,0:T(8,128)(2,1)}, bf16[640,384]{1,0:T(8,128)(2,1)}, u32[]{:S(2)}, u32[]{:S(2)}) collective-permute-start(bf16[640,384]{1,0:T(8,128)(2,1)} %get-tuple-element.11), channel_id=1, source_target_pairs={{0,1},{1,0},{2,3},{3,2},{4,5},{5,4},{6,7},{7,6},{8,9},{9,8},{10,11... | collective-permute-start | bytes 1474568 | tf_op jit(solution)/shard_map/ppermute | solution.py:38
  152.7 1.9 collective-permute-start.12
  154.6 1.3 fusion
  155.9 7.0 %all-to-all-start.3 = ((bf16[16,8,2560]{2,1,0:T(8,128)(2,1)}), bf16[16,8,2560]{2,1,0:T(8,128)(2,1)}, u32[]{:S(2)}, u32[]{:S(2)}) async-start(bf16[16,8,2560]{2,1,0:T(8,128)(2,1)} %fusion), calls=%async_computation.3 | async-start | bytes 1310720 | tf_op jit(solution)/shard_map/all_to_all | solution.py:261
  162.9 1.9 collective-permute-start.8
  164.9 2.4 collective-permute-start.14
  167.2 6.7 %collective-permute-done.12.refs_7_ = bf16[640,384]{1,0:T(8,128)(2,1)} collective-permute-done((bf16[640,384]{1,0:T(8,128)(2,1)}, bf16[640,384]{1,0:T(8,128)(2,1)}, u32[]{:S(2)}, u32[]{:S(2)}) %collective-permute-start.12) | collective-permute-done | bytes 491552 | tf_op jit(solution)/shard_map/ppermute | solution.py:38
  173.9 1.9 collective-permute-start.15
  175.8 2.4 collective-permute-start.18
  179.2 2.2 fusion.1
  181.4 7.0 %all-to-all-start.5 = ((bf16[16,8,2560]{2,1,0:T(8,128)(2,1)}), bf16[16,8,2560]{2,1,0:T(8,128)(2,1)}, u32[]{:S(2)}, u32[]{:S(2)}) async-start(bf16[16,8,2560]{2,1,0:T(8,128)(2,1)} %fusion.1), calls=%async_computation.5 | async-start | bytes 1310720 | tf_op jit(solution)/shard_map/all_to_all | solution.py:261
  188.4 1.9 collective-permute-start.16
  190.3 2.4 collective-permute-start.17
  192.8 1.6 collective-permute-done.17.refs_12_
  195.2 7.2 %experts.2 = bf16[128,2560]{1,0:T(8,128)(2,1)} custom-call(bf16[128,2560]{1,0:T(8,128)(2,1)} %bitcast.36.rows_ref, bf16[2560,384]{1,0:T(8,128)(2,1)} %bitcast.147, bf16[192,2560]{1,0:T(8,128)(2,1)} %bitcast.150, bf16[2560,384]{1,0:T(8,128)(2,1)} %collective-permute-done.7.refs_2_, bf16[192,2560]{1,0:T(8,128)(2,1)} %collective-permute-done.8.refs_3_, ...), custom_call_target="tpu_custom_call" | custom-call | tf_op jit(solution)/shard_map/experts/pallas_call | solution.py:164
  202.4 7.2 %all-to-all-start.4 = ((bf16[16,8,2560]{2,1,0:T(8,128)(2,1)}), bf16[16,8,2560]{2,1,0:T(8,128)(2,1)S(1)}, u32[]{:S(2)}, u32[]{:S(2)}) async-start(bf16[16,8,2560]{2,1,0:T(8,128)(2,1)} %bitcast.155), calls=%async_computation.4 | async-start | bytes 1310720 | tf_op jit(solution)/shard_map/all_to_all | solution.py:267
  209.7 7.2 %experts.3 = bf16[128,2560]{1,0:T(8,128)(2,1)} custom-call(bf16[128,2560]{1,0:T(8,128)(2,1)} %bitcast.45.rows_ref, bf16[2560,384]{1,0:T(8,128)(2,1)} %bitcast.148, bf16[192,2560]{1,0:T(8,128)(2,1)} %bitcast.151, bf16[2560,384]{1,0:T(8,128)(2,1)} %collective-permute-done.7.refs_2_, bf16[192,2560]{1,0:T(8,128)(2,1)} %collective-permute-done.8.refs_3_, ...), custom_call_target="tpu_custom_call" | custom-call | tf_op jit(solution)/shard_map/experts/pallas_call | solution.py:164
  216.9 6.2 %all-to-all-done.4 = bf16[16,8,2560]{2,1,0:T(8,128)(2,1)S(1)} async-done(((bf16[16,8,2560]{2,1,0:T(8,128)(2,1)}), bf16[16,8,2560]{2,1,0:T(8,128)(2,1)S(1)}, u32[]{:S(2)}, u32[]{:S(2)}) %all-to-all-start.4) | async-done | bytes 655392 | tf_op jit(solution)/shard_map/all_to_all | solution.py:267
  223.1 3.6 %all-to-all-start.6 = ((bf16[16,8,2560]{2,1,0:T(8,128)(2,1)}), bf16[16,8,2560]{2,1,0:T(8,128)(2,1)S(1)}, u32[]{:S(2)}, u32[]{:S(2)}) async-start(bf16[16,8,2560]{2,1,0:T(8,128)(2,1)} %bitcast.154), calls=%async_computation.6 | async-start | bytes 1310720 | tf_op jit(solution)/shard_map/all_to_all | solution.py:269
  227.5 1.9 collective-permute-start.19
  229.4 9.6 %all-to-all-done.6 = bf16[16,8,2560]{2,1,0:T(8,128)(2,1)S(1)} async-done(((bf16[16,8,2560]{2,1,0:T(8,128)(2,1)}), bf16[16,8,2560]{2,1,0:T(8,128)(2,1)S(1)}, u32[]{:S(2)}, u32[]{:S(2)}) %all-to-all-start.6) | async-done | bytes 655392 | tf_op jit(solution)/shard_map/all_to_all | solution.py:269
  239.4 5.6 %collective-permute-done.19 = bf16[64,2560]{1,0:T(8,128)(2,1)S(1)} collective-permute-done((bf16[64,2560]{1,0:T(8,128)(2,1)S(1)}, bf16[64,2560]{1,0:T(8,128)(2,1)S(1)}, u32[]{:S(2)}, u32[]{:S(2)}) %collective-permute-start.19) | collective-permute-done | bytes 327712 | tf_op jit(solution)/shard_map/ppermute | solution.py:38
  246.2 6.6 %all-to-all-start.7 = ((bf16[4,64,640]{2,1,0:T(8,128)(2,1)}), bf16[4,64,640]{2,1,0:T(8,128)(2,1)S(1)}, u32[]{:S(2)}, u32[]{:S(2)}) async-start(bf16[4,64,640]{2,1,0:T(8,128)(2,1)} %pad_maximum_fusion.2), calls=%async_computation.7 | async-start | bytes 655360 | tf_op jit(solution)/shard_map/all_to_all | solution.py:275
  253.2 17.4 %all-to-all-done.7 = bf16[4,64,640]{2,1,0:T(8,128)(2,1)S(1)} async-done(((bf16[4,64,640]{2,1,0:T(8,128)(2,1)}), bf16[4,64,640]{2,1,0:T(8,128)(2,1)S(1)}, u32[]{:S(2)}, u32[]{:S(2)}) %all-to-all-start.7) | async-done | bytes 327712 | tf_op jit(solution)/shard_map/all_to_all | solution.py:275
  270.7 3.3 %collective-permute-start.20 = (bf16[64,640]{1,0:T(8,128)(2,1)S(1)}, bf16[64,640]{1,0:T(8,128)(2,1)S(1)}, u32[]{:S(2)}, u32[]{:S(2)}) collective-permute-start(bf16[64,640]{1,0:T(8,128)(2,1)S(1)} %add_convert_fusion.1), channel_id=1, source_target_pairs={{0,0},{1,128},{2,256},{3,384},{128,1},{129,129},{130,257},{131,385... | collective-permute-start | bytes 245768 | tf_op jit(solution)/shard_map/ppermute | solution.py:38
  274.8 9.7 %collective-permute-done.20 = bf16[64,640]{1,0:T(8,128)(2,1)S(1)} collective-permute-done((bf16[64,640]{1,0:T(8,128)(2,1)S(1)}, bf16[64,640]{1,0:T(8,128)(2,1)S(1)}, u32[]{:S(2)}, u32[]{:S(2)}) %collective-permute-start.20) | collective-permute-done | bytes 81952 | tf_op jit(solution)/shard_map/ppermute | solution.py:38
  (117 shorter events, 11.1 us)
Async XLA Ops:
  0.6 51.6 %copy-start = (bf16[64,2560]{1,0:T(8,128)(2,1)S(1)}, bf16[64,2560]{1,0:T(8,128)(2,1)}, u32[]{:S(2)}) copy-start(bf16[64,2560]{1,0:T(8,128)(2,1)} %param.13) | copy-start | bytes 983044
  0.6 9.2 %copy-start.12 = (s32[1,4]{1,0:T(1,128)S(1)}, s32[1,4]{1,0:T(1,128)}, u32[]{:S(2)}) copy-start(s32[1,4]{1,0:T(1,128)} %param.14) | copy-start | bytes 52
  0.7 9.7 %copy-start.6 = (bf16[64,640]{1,0:T(8,128)(2,1)S(1)}, bf16[64,640]{1,0:T(8,128)(2,1)}, u32[]{:S(2)}) copy-start(bf16[64,640]{1,0:T(8,128)(2,1)} %param.11) | copy-start | bytes 245764
  0.7 9.7 %copy-start.7 = (bf16[64,256]{1,0:T(8,128)(2,1)S(1)}, bf16[64,256]{1,0:T(8,128)(2,1)}, u32[]{:S(2)}) copy-start(bf16[64,256]{1,0:T(8,128)(2,1)} %param.12) | copy-start | bytes 98308
  2.5 42.6 %all-to-all-start = ((bf16[32,20,640]{2,1,0:T(8,128)(2,1)}), bf16[32,20,640]{2,1,0:T(8,128)(2,1)S(1)}, u32[]{:S(2)}, u32[]{:S(2)}) async-start(bf16[32,20,640]{2,1,0:T(8,128)(2,1)} %broadcast_in_dim.265), calls=%async_computation | async-start | bytes 1966080 | tf_op jit(solution)/shard_map/all_to_all | solution.py:59
  10.0 35.1 %copy-start.14 = (s32[4,1]{0,1:T(1,128)}, s32[4,1]{0,1:T(1,128)S(1)}, u32[]{:S(2)}) copy-start(s32[4,1]{0,1:T(1,128)S(1)} %reduce-window.4) | copy-start | bytes 52
  10.9 23.8 %collective-permute-start.1 = (bf16[64,640]{1,0:T(8,128)(2,1)S(1)}, bf16[64,640]{1,0:T(8,128)(2,1)S(1)}, u32[]{:S(2)}, u32[]{:S(2)}) collective-permute-start(bf16[64,640]{1,0:T(8,128)(2,1)S(1)} %constant_dynamic-update-slice_fusion.5), channel_id=1, source_target_pairs={{128,0},{256,128},{384,256},{0,384},{129,1},{257,129},{385,257},{1... | collective-permute-start | bytes 245768 | tf_op jit(solution)/shard_map/ppermute | solution.py:34
  21.9 23.1 %collective-permute-start.2 = (bf16[64,640]{1,0:T(8,128)(2,1)S(1)}, bf16[64,640]{1,0:T(8,128)(2,1)S(1)}, u32[]{:S(2)}, u32[]{:S(2)}) collective-permute-start(bf16[64,640]{1,0:T(8,128)(2,1)S(1)} %constant_dynamic-update-slice_fusion.5), channel_id=1, source_target_pairs={{256,0},{384,128},{0,256},{128,384},{257,1},{385,129},{1,257},{129... | collective-permute-start | bytes 245768 | tf_op jit(solution)/shard_map/ppermute | solution.py:34
  27.3 17.7 %collective-permute-start.3 = (bf16[64,640]{1,0:T(8,128)(2,1)S(1)}, bf16[64,640]{1,0:T(8,128)(2,1)S(1)}, u32[]{:S(2)}, u32[]{:S(2)}) collective-permute-start(bf16[64,640]{1,0:T(8,128)(2,1)S(1)} %constant_dynamic-update-slice_fusion.5), channel_id=1, source_target_pairs={{384,0},{0,128},{128,256},{256,384},{385,1},{1,129},{129,257},{257... | collective-permute-start | bytes 245768 | tf_op jit(solution)/shard_map/ppermute | solution.py:34
  45.3 13.3 %copy-start.9 = (s32[64,6]{0,1:T(8,128)S(1)}, s32[64,6]{0,1:T(8,128)}, u32[]{:S(2)}) copy-start(s32[64,6]{0,1:T(8,128)} %param.18) | copy-start | bytes 4612
  45.3 13.3 %copy-start.10 = (f32[64,6]{0,1:T(8,128)S(1)}, f32[64,6]{0,1:T(8,128)}, u32[]{:S(2)}) copy-start(f32[64,6]{0,1:T(8,128)} %param.19) | copy-start | bytes 4612
  45.3 27.9 %copy-start.1 = (bf16[1,2560,384]{2,1,0:T(8,128)(2,1)S(1)}, bf16[1,2560,384]{2,1,0:T(8,128)(2,1)}, u32[]{:S(2)}) copy-start(bf16[1,2560,384]{2,1,0:T(8,128)(2,1)} %param.20) | copy-start | bytes 5898244
  46.5 18.5 %all-to-all-start.1 = ((bf16[4,64,640]{2,1,0:T(8,128)(2,1)}), bf16[4,64,640]{2,1,0:T(8,128)(2,1)S(1)}, u32[]{:S(2)}, u32[]{:S(2)}) async-start(bf16[4,64,640]{2,1,0:T(8,128)(2,1)} %bitcast.12), calls=%async_computation.1 | async-start | bytes 655360 | tf_op jit(solution)/shard_map/all_to_all | solution.py:245
  52.2 16.1 %collective-permute-start = (bf16[64,640]{1,0:T(8,128)(2,1)S(1)}, bf16[64,640]{1,0:T(8,128)(2,1)S(1)}, u32[]{:S(2)}, u32[]{:S(2)}) collective-permute-start(bf16[64,640]{1,0:T(8,128)(2,1)S(1)} %constant_dynamic-slice_fusion), channel_id=1, source_target_pairs={{0,0},{1,128},{2,256},{3,384},{128,1},{129,129},{130,257},{131,385... | collective-permute-start | bytes 245768 | tf_op jit(solution)/shard_map/ppermute | solution.py:38
  58.7 27.6 %collective-permute-start.4 = (bf16[64,128]{0,1:T(8,128)(2,1)S(1)}, bf16[64,128]{0,1:T(8,128)(2,1)S(1)}, u32[]{:S(2)}, u32[]{:S(2)}) collective-permute-start(bf16[64,128]{0,1:T(8,128)(2,1)S(1)} %fusion.38), channel_id=1, source_target_pairs={{0,0},{1,128},{2,256},{3,384},{128,1},{129,129},{130,257},{131,385... | collective-permute-start | bytes 49160 | tf_op jit(solution)/shard_map/ppermute | solution.py:38
  69.1 29.0 %all-to-all-start.2 = ((bf16[4,64,640]{2,1,0:T(8,128)(2,1)}), bf16[4,64,640]{2,1,0:T(8,128)(2,1)}, u32[]{:S(2)}, u32[]{:S(2)}) async-start(bf16[4,64,640]{2,1,0:T(8,128)(2,1)} %broadcast_in_dim.279), calls=%async_computation.2 | async-start | bytes 655360 | tf_op jit(solution)/shard_map/all_to_all | solution.py:59
  73.2 7.3 %copy-start.2 = (bf16[1,192,2560]{2,1,0:T(8,128)(2,1)S(1)}, bf16[1,192,2560]{2,1,0:T(8,128)(2,1)}, u32[]{:S(2)}) copy-start(bf16[1,192,2560]{2,1,0:T(8,128)(2,1)} %param.21) | copy-start | bytes 2949124
  74.5 80.1 %copy-start.8 = (f32[2560]{0:T(1024)S(1)}, f32[2560]{0:T(1024)}, u32[]{:S(2)}) copy-start(f32[2560]{0:T(1024)} %param.17) | copy-start | bytes 30724
  74.5 78.1 %collective-permute-start.9 = (bf16[640,384]{1,0:T(8,128)(2,1)}, bf16[640,384]{1,0:T(8,128)(2,1)}, u32[]{:S(2)}, u32[]{:S(2)}) collective-permute-start(bf16[640,384]{1,0:T(8,128)(2,1)} %get-tuple-element.10), channel_id=1, source_target_pairs={{0,1},{1,0},{2,3},{3,2},{4,5},{5,4},{6,7},{7,6},{8,9},{9,8},{10,11... | collective-permute-start | bytes 1474568 | tf_op jit(solution)/shard_map/ppermute | solution.py:38
  77.9 84.9 %collective-permute-start.10 = (bf16[640,384]{1,0:T(8,128)(2,1)}, bf16[640,384]{1,0:T(8,128)(2,1)}, u32[]{:S(2)}, u32[]{:S(2)}) collective-permute-start(bf16[640,384]{1,0:T(8,128)(2,1)} %get-tuple-element.9), channel_id=1, source_target_pairs={{0,1},{1,0},{2,3},{3,2},{4,5},{5,4},{6,7},{7,6},{8,9},{9,8},{10,11... | collective-permute-start | bytes 1474568 | tf_op jit(solution)/shard_map/ppermute | solution.py:38
  80.5 95.3 %collective-permute-start.13 = (bf16[192,2560]{1,0:T(8,128)(2,1)S(1)}, bf16[192,2560]{1,0:T(8,128)(2,1)}, u32[]{:S(2)}, u32[]{:S(2)}) collective-permute-start(bf16[192,2560]{1,0:T(8,128)(2,1)S(1)} %bitcast.152), channel_id=1, source_target_pairs={{0,1},{1,0},{2,3},{3,2},{4,5},{5,4},{6,7},{7,6},{8,9},{9,8},{10,11... | collective-permute-start | bytes 2949128 | tf_op jit(solution)/shard_map/ppermute | solution.py:38
  83.8 110.7 %collective-permute-start.7 = (bf16[2560,384]{1,0:T(8,128)(2,1)S(1)}, bf16[2560,384]{1,0:T(8,128)(2,1)}, u32[]{:S(2)}, u32[]{:S(2)}) collective-permute-start(bf16[2560,384]{1,0:T(8,128)(2,1)S(1)} %bitcast.149), channel_id=1, source_target_pairs={{0,4},{4,0},{1,5},{5,1},{2,6},{6,2},{3,7},{7,3},{8,12},{12,8},{9,1... | collective-permute-start | bytes 5898248 | tf_op jit(solution)/shard_map/ppermute | solution.py:38
  85.7 22.6 %copy-start.16 = (pred[128]{0:T(512)(128)(4,1)}, pred[128]{0:T(512)(128)(4,1)S(1)}, u32[]{:S(2)}) copy-start(pred[128]{0:T(512)(128)(4,1)S(1)} %get-tuple-element.68) | copy-start | bytes 388
  85.7 70.1 %copy-start.17 = (s32[128]{0:T(128)}, s32[128]{0:T(128)S(1)}, u32[]{:S(2)}) copy-start(s32[128]{0:T(128)S(1)} %get-tuple-element.71) | copy-start | bytes 1540
  86.3 8.0 %collective-permute-start.5 = (bf16[64,128]{0,1:T(8,128)(2,1)S(1)}, bf16[64,128]{0,1:T(8,128)(2,1)S(1)}, u32[]{:S(2)}, u32[]{:S(2)}) collective-permute-start(bf16[64,128]{0,1:T(8,128)(2,1)S(1)} %collective-permute-done.4), channel_id=1, source_target_pairs={{0,3},{1,2},{2,1},{3,0},{4,7},{5,6},{6,5},{7,4},{8,11},{9,10},{10,... | collective-permute-start | bytes 49160 | tf_op jit(solution)/shard_map/ppermute | solution.py:38
  99.3 9.0 %copy-start.5 = (bf16[64,2560]{1,0:T(8,128)(2,1)}, bf16[64,2560]{1,0:T(8,128)(2,1)S(1)}, u32[]{:S(2)}) copy-start(bf16[64,2560]{1,0:T(8,128)(2,1)S(1)} %get-tuple-element.7) | copy-start | bytes 983044
  99.3 9.0 %collective-permute-start.6 = (bf16[64,2560]{1,0:T(8,128)(2,1)S(1)}, bf16[64,2560]{1,0:T(8,128)(2,1)S(1)}, u32[]{:S(2)}, u32[]{:S(2)}) collective-permute-start(bf16[64,2560]{1,0:T(8,128)(2,1)S(1)} %get-tuple-element.7), channel_id=1, source_target_pairs={{0,3},{1,2},{2,1},{3,0},{4,7},{5,6},{6,5},{7,4},{8,11},{9,10},{10,... | collective-permute-start | bytes 983048 | tf_op jit(solution)/shard_map/ppermute | solution.py:38
  108.3 56.6 %collective-permute-start.11 = (bf16[640,384]{1,0:T(8,128)(2,1)}, bf16[640,384]{1,0:T(8,128)(2,1)}, u32[]{:S(2)}, u32[]{:S(2)}) collective-permute-start(bf16[640,384]{1,0:T(8,128)(2,1)} %get-tuple-element.11), channel_id=1, source_target_pairs={{0,1},{1,0},{2,3},{3,2},{4,5},{5,4},{6,7},{7,6},{8,9},{9,8},{10,11... | collective-permute-start | bytes 1474568 | tf_op jit(solution)/shard_map/ppermute | solution.py:38
  152.7 21.2 %collective-permute-start.12 = (bf16[640,384]{1,0:T(8,128)(2,1)}, bf16[640,384]{1,0:T(8,128)(2,1)}, u32[]{:S(2)}, u32[]{:S(2)}) collective-permute-start(bf16[640,384]{1,0:T(8,128)(2,1)} %get-tuple-element.8), channel_id=1, source_target_pairs={{0,1},{1,0},{2,3},{3,2},{4,5},{5,4},{6,7},{7,6},{8,9},{9,8},{10,11... | collective-permute-start | bytes 1474568 | tf_op jit(solution)/shard_map/ppermute | solution.py:38
  155.9 25.6 %all-to-all-start.3 = ((bf16[16,8,2560]{2,1,0:T(8,128)(2,1)}), bf16[16,8,2560]{2,1,0:T(8,128)(2,1)}, u32[]{:S(2)}, u32[]{:S(2)}) async-start(bf16[16,8,2560]{2,1,0:T(8,128)(2,1)} %fusion), calls=%async_computation.3 | async-start | bytes 1310720 | tf_op jit(solution)/shard_map/all_to_all | solution.py:261
  162.9 31.6 %collective-permute-start.8 = (bf16[192,2560]{1,0:T(8,128)(2,1)S(1)}, bf16[192,2560]{1,0:T(8,128)(2,1)}, u32[]{:S(2)}, u32[]{:S(2)}) collective-permute-start(bf16[192,2560]{1,0:T(8,128)(2,1)S(1)} %bitcast.153), channel_id=1, source_target_pairs={{0,4},{4,0},{1,5},{5,1},{2,6},{6,2},{3,7},{7,3},{8,12},{12,8},{9,1... | collective-permute-start | bytes 2949128 | tf_op jit(solution)/shard_map/ppermute | solution.py:38
  164.9 23.5 %collective-permute-start.14 = (bf16[640,384]{1,0:T(8,128)(2,1)}, bf16[640,384]{1,0:T(8,128)(2,1)}, u32[]{:S(2)}, u32[]{:S(2)}) collective-permute-start(bf16[640,384]{1,0:T(8,128)(2,1)} %collective-permute-done.9.refs_4_), channel_id=1, source_target_pairs={{0,4},{4,0},{1,5},{5,1},{2,6},{6,2},{3,7},{7,3},{8,12},{12,8},{9,1... | collective-permute-start | bytes 1474568 | tf_op jit(solution)/shard_map/ppermute | solution.py:38
  173.9 16.5 %collective-permute-start.15 = (bf16[640,384]{1,0:T(8,128)(2,1)}, bf16[640,384]{1,0:T(8,128)(2,1)}, u32[]{:S(2)}, u32[]{:S(2)}) collective-permute-start(bf16[640,384]{1,0:T(8,128)(2,1)} %collective-permute-done.10.refs_5_), channel_id=1, source_target_pairs={{0,4},{4,0},{1,5},{5,1},{2,6},{6,2},{3,7},{7,3},{8,12},{12,8},{9,1... | collective-permute-start | bytes 1474568 | tf_op jit(solution)/shard_map/ppermute | solution.py:38
  175.8 18.6 %collective-permute-start.18 = (bf16[192,2560]{1,0:T(8,128)(2,1)}, bf16[192,2560]{1,0:T(8,128)(2,1)}, u32[]{:S(2)}, u32[]{:S(2)}) collective-permute-start(bf16[192,2560]{1,0:T(8,128)(2,1)} %collective-permute-done.13.refs_8_), channel_id=1, source_target_pairs={{0,4},{4,0},{1,5},{5,1},{2,6},{6,2},{3,7},{7,3},{8,12},{12,8},{9,1... | collective-permute-start | bytes 2949128 | tf_op jit(solution)/shard_map/ppermute | solution.py:38
  181.4 21.0 %all-to-all-start.5 = ((bf16[16,8,2560]{2,1,0:T(8,128)(2,1)}), bf16[16,8,2560]{2,1,0:T(8,128)(2,1)}, u32[]{:S(2)}, u32[]{:S(2)}) async-start(bf16[16,8,2560]{2,1,0:T(8,128)(2,1)} %fusion.1), calls=%async_computation.5 | async-start | bytes 1310720 | tf_op jit(solution)/shard_map/all_to_all | solution.py:261
  188.4 4.4 %collective-permute-start.16 = (bf16[640,384]{1,0:T(8,128)(2,1)}, bf16[640,384]{1,0:T(8,128)(2,1)S(1)}, u32[]{:S(2)}, u32[]{:S(2)}) collective-permute-start(bf16[640,384]{1,0:T(8,128)(2,1)} %collective-permute-done.11.refs_6_), channel_id=1, source_target_pairs={{0,4},{4,0},{1,5},{5,1},{2,6},{6,2},{3,7},{7,3},{8,12},{12,8},{9,1... | collective-permute-start | bytes 1474568 | tf_op jit(solution)/shard_map/ppermute | solution.py:38
  190.3 4.1 %collective-permute-start.17 = (bf16[640,384]{1,0:T(8,128)(2,1)}, bf16[640,384]{1,0:T(8,128)(2,1)S(1)}, u32[]{:S(2)}, u32[]{:S(2)}) collective-permute-start(bf16[640,384]{1,0:T(8,128)(2,1)} %collective-permute-done.12.refs_7_), channel_id=1, source_target_pairs={{0,4},{4,0},{1,5},{5,1},{2,6},{6,2},{3,7},{7,3},{8,12},{12,8},{9,1... | collective-permute-start | bytes 1474568 | tf_op jit(solution)/shard_map/ppermute | solution.py:38
  192.8 1.7 copy-start.3
  194.4 0.8 copy-start.4
  202.4 20.7 %all-to-all-start.4 = ((bf16[16,8,2560]{2,1,0:T(8,128)(2,1)}), bf16[16,8,2560]{2,1,0:T(8,128)(2,1)S(1)}, u32[]{:S(2)}, u32[]{:S(2)}) async-start(bf16[16,8,2560]{2,1,0:T(8,128)(2,1)} %bitcast.155), calls=%async_computation.4 | async-start | bytes 1310720 | tf_op jit(solution)/shard_map/all_to_all | solution.py:267
  223.1 15.9 %all-to-all-start.6 = ((bf16[16,8,2560]{2,1,0:T(8,128)(2,1)}), bf16[16,8,2560]{2,1,0:T(8,128)(2,1)S(1)}, u32[]{:S(2)}, u32[]{:S(2)}) async-start(bf16[16,8,2560]{2,1,0:T(8,128)(2,1)} %bitcast.154), calls=%async_computation.6 | async-start | bytes 1310720 | tf_op jit(solution)/shard_map/all_to_all | solution.py:269
  227.5 17.5 %collective-permute-start.19 = (bf16[64,2560]{1,0:T(8,128)(2,1)S(1)}, bf16[64,2560]{1,0:T(8,128)(2,1)S(1)}, u32[]{:S(2)}, u32[]{:S(2)}) collective-permute-start(bf16[64,2560]{1,0:T(8,128)(2,1)S(1)} %fusion.2), channel_id=1, source_target_pairs={{0,3},{1,2},{2,1},{3,0},{4,7},{5,6},{6,5},{7,4},{8,11},{9,10},{10,... | collective-permute-start | bytes 983048 | tf_op jit(solution)/shard_map/ppermute | solution.py:38
  245.0 7.9 %copy-start.11 = (s32[1,4,2]{1,2,0:T(2,128)S(1)}, s32[1,4,2]{1,2,0:T(2,128)}, u32[]{:S(2)}) copy-start(s32[1,4,2]{1,2,0:T(2,128)} %param.15) | copy-start | bytes 100
  245.0 8.0 %copy-start.13 = (s32[1,4]{1,0:T(1,128)S(1)}, s32[1,4]{1,0:T(1,128)}, u32[]{:S(2)}) copy-start(s32[1,4]{1,0:T(1,128)} %param.14) | copy-start | bytes 52
  245.0 8.0 %copy-start.15 = (s32[4,1]{0,1:T(1,128)S(1)}, s32[4,1]{0,1:T(1,128)}, u32[]{:S(2)}) copy-start(s32[4,1]{0,1:T(1,128)} %copy-done.14) | copy-start | bytes 52
  246.2 24.4 %all-to-all-start.7 = ((bf16[4,64,640]{2,1,0:T(8,128)(2,1)}), bf16[4,64,640]{2,1,0:T(8,128)(2,1)S(1)}, u32[]{:S(2)}, u32[]{:S(2)}) async-start(bf16[4,64,640]{2,1,0:T(8,128)(2,1)} %pad_maximum_fusion.2), calls=%async_computation.7 | async-start | bytes 655360 | tf_op jit(solution)/shard_map/all_to_all | solution.py:275
  270.7 13.8 %collective-permute-start.20 = (bf16[64,640]{1,0:T(8,128)(2,1)S(1)}, bf16[64,640]{1,0:T(8,128)(2,1)S(1)}, u32[]{:S(2)}, u32[]{:S(2)}) collective-permute-start(bf16[64,640]{1,0:T(8,128)(2,1)S(1)} %add_convert_fusion.1), channel_id=1, source_target_pairs={{0,0},{1,128},{2,256},{3,384},{128,1},{129,129},{130,257},{131,385... | collective-permute-start | bytes 245768 | tf_op jit(solution)/shard_map/ppermute | solution.py:38
